TPU v7x, 256 devices: a whole 4x4x8 slice. The times are simulated.
256 devices in a mesh: blk: 64 (over y, z_lo, x), lag: 4 (over z_hi, core).
Axes of the slice: x: 4, y: 4, z: 8 (z_hi: 2, z_lo: 4; z = z_hi * 4 + z_lo), core: 2. Of those that a mesh axis runs over, the one named last changes fastest.
Arguments:
- traces: float32 [8192, 8192], P('blk', 'lag'), may hold values from -13 to 13
- owner_map: int32 [5, 64], P(None, 'blk'), may hold values from 0 to 63
- pair_codes: int32 [5, 32768], P(None, 'blk'), may hold values from 0 to 16383, as said below
- pair_count: int32 [5, 64], P(None, 'blk'), may hold values from 128 to 512, as said below
Outputs:
- stacks: float32 [64, 8, 1024], P('blk', None, 'lag')
Inputs may be any that keep to these rules, and one draw needn't show every extreme that they name: `pair_codes`: each entry is i * 128 + j with i a channel of the earlier block and j one of the later block of the meeting; no entry repeats within one list, and in meeting 0 every entry has i < j. Only the first pair_count[o, b] slots of list (o, b) are live; in every meeting some block has exactly 512.
All inputs are finite; a program needn't handle non-finite values.
Results may differ from a plain program's by a relative error of at most 0.0077.
Values may be sent and summed in bfloat16 or wider, within the bound.
No kernel may reach another device: no remote copies, remote signals or barrier semaphores. Data moves between devices by JAX's collectives and lax.ppermute only.
A program may use at most 128 MiB of HBM per device.

v0:
```python
import math

import jax
import jax.numpy as jnp
from jax import lax
from jax.sharding import PartitionSpec as P

WIN = 1024
NF = 512
TAPS = 128
NBIN = 8
ROUNDS = 4
BINW = 80


band_low = 0.02
band_high = 0.48
water_level = 0.1


def from_behind(block, axis, distance):
    devices = range(lax.axis_size(axis))
    route = [(i - distance, i) for i in devices if i - distance in devices]
    return lax.ppermute(block, axis, route)


def tap_value(position, tap_count):
    middle = position - (tap_count - 1) / 2.0
    ideal_band = 2.0 * band_high * jnp.sinc(2.0 * band_high * middle) - 2.0 * band_low * jnp.sinc(
        2.0 * band_low * middle
    )
    taper_win = 0.5 - 0.5 * jnp.cos(2.0 * jnp.pi * (position + 0.5) / tap_count)
    return ideal_band * taper_win


def filter_matrix(tap_count, tile_len):
    row_ids = jnp.arange(tile_len + tap_count, dtype=jnp.int32)[:, None]
    col_ids = jnp.arange(tile_len, dtype=jnp.int32)[None, :]
    lagged = col_ids - row_ids + tap_count
    inside = (lagged >= 0) & (lagged < tap_count)
    values = tap_value(lagged.astype(jnp.float32), tap_count)
    return jnp.where(inside, values, 0.0).astype(jnp.float32)


def transform_table(window, freq_ids, is_imag):
    time_ids = jnp.arange(window, dtype=jnp.int32)[:, None]
    phase_ids = time_ids * freq_ids[None, :] % window
    angles = phase_ids.astype(jnp.float32) * (2.0 * math.pi / window)
    values = jnp.where(is_imag[None, :], -jnp.sin(angles), jnp.cos(angles))
    return (values / math.sqrt(window)).astype(jnp.bfloat16)


def inverse_table(window, freq_ids, windows):
    lag_steps = jnp.arange(window, dtype=jnp.int32)[None, :] - window // 2
    phase_ids = freq_ids[:, None] * lag_steps % window
    angles = phase_ids.astype(jnp.float32) * (2.0 * math.pi / window)
    weight = jnp.where(freq_ids == 0, 1.0, 2.0)[:, None] / (windows * math.sqrt(window))
    return jnp.concatenate([weight * jnp.cos(angles), -weight * jnp.sin(angles)], axis=0)


def whiten(received):
    values = received[:, :, 0, :]
    half_width = values.shape[2] // 2
    real_part = values[..., :half_width].astype(jnp.float32)
    imag_part = values[..., half_width:].astype(jnp.float32)
    band_power = jnp.mean(real_part * real_part + imag_part * imag_part, axis=1)
    gain_row = lax.rsqrt(band_power + water_level)
    gains_both = jnp.concatenate([gain_row, gain_row], axis=1)
    return (values.astype(jnp.float32) * gains_both[:, None, :]).astype(jnp.bfloat16)


def cross_mask(partner, own_block, pair_list, live_count, offset):
    channels, windows, full_width = own_block.shape
    half_width = full_width // 2
    slot_count = pair_list.shape[0]
    chan_ids = jnp.arange(channels, dtype=jnp.int32)
    is_valid = jnp.arange(slot_count, dtype=jnp.int32) < live_count
    first_ids = pair_list // channels
    second_ids = pair_list % channels
    pick_first = ((first_ids[:, None] == chan_ids[None, :]) & is_valid[:, None]).astype(
        jnp.bfloat16
    )
    pick_second = (second_ids[:, None] == chan_ids[None, :]).astype(jnp.bfloat16)
    chosen = jnp.einsum("pi,pj->ij", pick_first, pick_second, preferred_element_type=jnp.float32)
    distance = channels * offset + chan_ids[None, :] - chan_ids[:, None]
    bin_ids = distance // BINW
    own_flat = own_block.reshape(channels, windows * full_width)
    results = []
    for bin_level in range(NBIN):
        weights = jnp.where(bin_ids == bin_level, chosen, 0.0).astype(jnp.bfloat16)
        mixed_rows = jnp.dot(weights, own_flat, preferred_element_type=jnp.float32).reshape(
            channels, windows, full_width
        )
        mix_real = mixed_rows[..., :half_width]
        mix_imag = mixed_rows[..., half_width:]
        cross_real = jnp.sum(
            partner[..., :half_width] * mix_real + partner[..., half_width:] * mix_imag, axis=(0, 1)
        )
        cross_imag = jnp.sum(
            partner[..., :half_width] * mix_imag - partner[..., half_width:] * mix_real, axis=(0, 1)
        )
        results.append(jnp.concatenate([cross_real, cross_imag]))
    return jnp.stack(results)


def body(traces, owner_map, pair_codes, pair_count):
    channels, local_time = traces.shape
    lag_parts = lax.axis_size("lag")
    lag_index = lax.axis_index("lag")
    blk_parts = lax.axis_size("blk")
    tile_len = 2 * TAPS
    tile_count = local_time // tile_len
    history = from_behind(traces[:, local_time - TAPS :], "lag", 1)
    current = traces.reshape(channels, tile_count, tile_len)
    earlier = jnp.concatenate([history[:, None, :], current[:, :-1, tile_len - TAPS :]], axis=1)
    inputs = jnp.concatenate([earlier, current], axis=2)
    filtered = jnp.einsum(
        "cnu,uv->cnv", inputs, filter_matrix(TAPS, tile_len), precision=lax.Precision.HIGHEST
    ).astype(jnp.bfloat16)
    own_windows = local_time // WIN
    filtered = filtered.reshape(channels, own_windows, WIN)
    band_bins = NF // lag_parts
    columns = jnp.arange(2 * NF, dtype=jnp.int32)
    group_of = columns // (2 * band_bins)
    within = columns % (2 * band_bins)
    freq_ids = group_of * band_bins + within % band_bins
    spectra = jnp.einsum(
        "cwt,tf->cwf",
        filtered,
        transform_table(WIN, freq_ids, within >= band_bins),
        preferred_element_type=jnp.float32,
    ).astype(jnp.bfloat16)
    spectra = spectra.reshape(channels, own_windows, lag_parts, 2 * band_bins)
    whitened = whiten(lax.all_to_all(spectra, "lag", split_axis=2, concat_axis=1, tiled=True))
    meeting_sums = []
    partner = whitened
    for offset in range(ROUNDS + 1):
        if offset > 0:
            partner = from_behind(whitened, "blk", offset)
        meeting_sums.append(
            cross_mask(partner, whitened, pair_codes[offset], pair_count[offset, 0], offset)
        )
    binned = jnp.stack(meeting_sums)
    meet_count = binned.shape[0]
    targets = (owner_map[:, 0][:, None] == jnp.arange(blk_parts, dtype=jnp.int32)[None, :]).astype(
        jnp.float32
    )
    owner_term = jnp.einsum(
        "mn,mx->nx",
        targets,
        binned.reshape(meet_count, NBIN * 2 * band_bins),
        precision=lax.Precision.HIGHEST,
    )
    freq_here = lag_index * band_bins + jnp.arange(band_bins, dtype=jnp.int32)
    inverse = inverse_table(WIN, freq_here, whitened.shape[1])
    lagged = jnp.dot(
        owner_term.reshape(blk_parts * NBIN, 2 * band_bins),
        inverse,
        precision=lax.Precision.HIGHEST,
    ).reshape(blk_parts, NBIN, WIN)
    owned = lax.psum_scatter(lagged, "blk", scatter_dimension=0, tiled=True)
    stacks = lax.psum_scatter(owned, "lag", scatter_dimension=2, tiled=True)
    return stacks


def solution(mesh):
    return jax.shard_map(
        body,
        mesh=mesh,
        in_specs=(P("blk", "lag"), P(None, "blk"), P(None, "blk"), P(None, "blk")),
        out_specs=P("blk", None, "lag"),
        check_vma=False,
    )
```

profile of v0, /device:TPU:1, one launch (start us, length us, event | category | flops | bytes accessed | tf_op | source)
XLA Modules:
  0.0 562.4 jit_solution(5275050822535605853)
XLA Ops:
  6.5 0.8 slice.208
  7.4 10.3 %collective-permute-start = (f32[128,128]{1,0:T(8,128)S(1)}, f32[128,128]{1,0:T(8,128)S(1)}, u32[]{:S(2)}, u32[]{:S(2)}) collective-permute-start(f32[128,128]{1,0:T(8,128)S(1)} %slice.208), channel_id=1, source_target_pairs={{0,1},{1,2},{2,3},{4,5},{5,6},{6,7},{8,9},{9,10},{10,11},{12,13},{... | collective-permute-start | bytes 196616 | tf_op jit(solution)/shard_map/ppermute | solution.py:24
  17.7 1.6 copy.6
  19.8 0.7 fusion.763
  20.5 0.6 iota_compare_fusion.21
  21.2 0.6 iota_compare_fusion.20
  21.7 0.7 iota_compare_fusion.19
  22.5 0.5 fusion.239
  23.9 0.6 iota_compare_fusion.18
  24.6 3.4 fusion.25
  28.2 17.9 %fusion.22 = bf16[128,2,1024]{2,0,1:T(8,128)(2,1)S(1)} fusion(bf16[128,2,1024]{0,2,1:T(8,128)(2,1)S(1)} %bitcast.306, s32[1024]{0:T(1024)S(1)} %fusion.492, pred[1024]{0:T(1024)(128)(4,1)S(1)} %fusion.496), kind=kOutput, calls=%fused_computation.185 | convolution fusion | flops 556007424 | bytes 1053696 | tf_op jit(solution)/shard_map/cwt,tf->cwf/dot_general | solution.py:127
  46.5 1.1 copy.11
  47.6 3.5 all-to-all-start
  51.3 0.7 iota_compare_fusion.17
  52.5 0.5 fusion.247
  53.0 3.3 cosine_multiply_fusion
  56.2 7.0 %all-to-all-done = bf16[128,2,4,256]{0,3,1,2:T(8,128)(2,1)S(1)} async-done(((bf16[128,2,4,256]{0,3,1,2:T(8,128)(2,1)}), bf16[128,2,4,256]{0,3,1,2:T(8,128)(2,1)S(1)}, u32[]{:S(2)}, u32[]{:S(2)}) %all-to-all-start) | async-done | bytes 524320 | tf_op jit(solution)/shard_map/all_to_all | solution.py:134
  66.4 1.3 fusion.336
  67.7 1.3 fusion.333
  69.0 1.3 fusion.315
  70.3 1.3 fusion.318
  71.6 1.3 fusion.327
  72.9 1.3 fusion.330
  74.2 1.3 fusion.324
  75.5 1.3 fusion.321
  76.8 3.9 collective-permute-start.1
  80.7 4.4 collective-permute-start.2
  85.1 1.4 fusion.360
  86.5 1.3 fusion.357
  87.7 1.3 fusion.339
  89.0 1.3 fusion.342
  90.3 1.4 fusion.351
  91.6 1.3 fusion.354
  92.9 1.3 fusion.348
  94.2 1.3 fusion.345
  95.5 7.8 %collective-permute-start.3 = (bf16[128,8,256]{2,0,1:T(8,128)(2,1)S(1)}, bf16[128,8,256]{2,0,1:T(8,128)(2,1)}, u32[]{:S(2)}, u32[]{:S(2)}) collective-permute-start(bf16[128,8,256]{2,0,1:T(8,128)(2,1)S(1)} %multiply_convert_fusion.1), channel_id=1, source_target_pairs={{0,12},{4,16},{8,20},{12,24},{16,28},{20,32},{24,36},{28,40},{32,4... | collective-permute-start | bytes 1572872 | tf_op jit(solution)/shard_map/ppermute | solution.py:24
  103.6 1.3 fusion.381
  104.9 1.3 fusion.363
  106.2 1.3 fusion.366
  107.5 1.3 fusion.375
  108.8 1.3 fusion.378
  110.4 1.3 fusion.369
  111.7 2.7 collective-permute-start.4
  114.3 1.3 fusion.408
  115.6 1.3 fusion.405
  116.9 1.4 fusion.387
  118.3 1.3 fusion.390
  119.6 1.3 fusion.399
  120.8 1.3 fusion.402
  122.4 0.9 fusion.64
  123.5 1.3 fusion.396
  124.8 1.3 fusion.393
  126.1 3.0 fusion.96
  129.2 1.4 fusion.80
  130.7 3.9 fusion.128
  134.7 1.4 fusion.112
  136.1 3.6 fusion.160
  139.8 1.4 fusion.144
  141.3 3.6 fusion.192
  145.0 1.5 fusion.176
  146.7 0.5 fusion.499
  147.4 3.2 fusion.28
  150.6 321.7 %reduce-scatter.3.cloned.1.call-done = f32[1,8,1024]{2,1,0:T(8,128)} async-done(((f32[64,8,1024]{2,1,0:T(8,128)}), f32[1,8,1024]{2,1,0:T(8,128)}) %reduce-scatter.3.cloned.1.call-update) | async-done | bytes 32784 | tf_op jit(solution)/shard_map/reduce_scatter | solution.py:161
  472.4 83.2 %reduce-scatter.5.cloned.1.call-done = f32[1,8,256]{2,1,0:T(8,128)} async-done(((f32[1,8,1024]{2,1,0:T(8,128)}), f32[1,8,256]{2,1,0:T(8,128)}) %reduce-scatter.5.cloned.1.call-update) | async-done | bytes 8208 | tf_op jit(solution)/shard_map/reduce_scatter | solution.py:162
  (113 shorter events, 7.5 us)
Async XLA Ops:
  7.4 12.4 %copy-start.14 = (s32[5,512]{1,0:T(8,128)S(1)}, s32[5,512]{1,0:T(8,128)}, u32[]{:S(2)}) copy-start(s32[5,512]{1,0:T(8,128)} %param.7) | copy-start | bytes 30724
  7.4 12.4 %copy-start.13 = (s32[5,1]{0,1:T(1,128)S(1)}, s32[5,1]{0,1:T(1,128)}, u32[]{:S(2)}) copy-start(s32[5,1]{0,1:T(1,128)} %param.8) | copy-start | bytes 64
  7.4 17.2 %collective-permute-start = (f32[128,128]{1,0:T(8,128)S(1)}, f32[128,128]{1,0:T(8,128)S(1)}, u32[]{:S(2)}, u32[]{:S(2)}) collective-permute-start(f32[128,128]{1,0:T(8,128)S(1)} %slice.208), channel_id=1, source_target_pairs={{0,1},{1,2},{2,3},{4,5},{5,6},{6,7},{8,9},{9,10},{10,11},{12,13},{... | collective-permute-start | bytes 196616 | tf_op jit(solution)/shard_map/ppermute | solution.py:24
  47.6 15.6 %all-to-all-start = ((bf16[128,2,4,256]{0,3,1,2:T(8,128)(2,1)}), bf16[128,2,4,256]{0,3,1,2:T(8,128)(2,1)S(1)}, u32[]{:S(2)}, u32[]{:S(2)}) async-start(bf16[128,2,4,256]{0,3,1,2:T(8,128)(2,1)} %copy.11), calls=%async_computation | async-start | bytes 1048576 | tf_op jit(solution)/shard_map/all_to_all | solution.py:134
  51.1 421.2 %reduce-scatter.3.cloned.1.call-start = ((), (), s32[]{:S(2)}) async-start(), calls=%async_computation.3 | async-start | bytes 2129920 | tf_op jit(solution)/shard_map/reduce_scatter | solution.py:161
  76.8 49.3 %collective-permute-start.1 = (bf16[128,8,256]{2,0,1:T(8,128)(2,1)S(1)}, bf16[128,8,256]{2,0,1:T(8,128)(2,1)}, u32[]{:S(2)}, u32[]{:S(2)}) collective-permute-start(bf16[128,8,256]{2,0,1:T(8,128)(2,1)S(1)} %multiply_convert_fusion.1), channel_id=1, source_target_pairs={{0,4},{4,8},{8,12},{12,16},{16,20},{20,24},{24,28},{28,32},{32,36}... | collective-permute-start | bytes 1572872 | tf_op jit(solution)/shard_map/ppermute | solution.py:24
  80.7 49.9 %collective-permute-start.2 = (bf16[128,8,256]{2,0,1:T(8,128)(2,1)S(1)}, bf16[128,8,256]{2,0,1:T(8,128)(2,1)}, u32[]{:S(2)}, u32[]{:S(2)}) collective-permute-start(bf16[128,8,256]{2,0,1:T(8,128)(2,1)S(1)} %multiply_convert_fusion.1), channel_id=1, source_target_pairs={{0,8},{4,12},{8,16},{12,20},{16,24},{20,28},{24,32},{28,36},{32,40... | collective-permute-start | bytes 1572872 | tf_op jit(solution)/shard_map/ppermute | solution.py:24
  95.5 40.7 %collective-permute-start.3 = (bf16[128,8,256]{2,0,1:T(8,128)(2,1)S(1)}, bf16[128,8,256]{2,0,1:T(8,128)(2,1)}, u32[]{:S(2)}, u32[]{:S(2)}) collective-permute-start(bf16[128,8,256]{2,0,1:T(8,128)(2,1)S(1)} %multiply_convert_fusion.1), channel_id=1, source_target_pairs={{0,12},{4,16},{8,20},{12,24},{16,28},{20,32},{24,36},{28,40},{32,4... | collective-permute-start | bytes 1572872 | tf_op jit(solution)/shard_map/ppermute | solution.py:24
  111.7 29.6 %collective-permute-start.4 = (bf16[128,8,256]{2,0,1:T(8,128)(2,1)S(1)}, bf16[128,8,256]{2,0,1:T(8,128)(2,1)}, u32[]{:S(2)}, u32[]{:S(2)}) collective-permute-start(bf16[128,8,256]{2,0,1:T(8,128)(2,1)S(1)} %multiply_convert_fusion.1), channel_id=1, source_target_pairs={{0,16},{4,20},{8,24},{12,28},{16,32},{20,36},{24,40},{28,44},{32,4... | collective-permute-start | bytes 1572872 | tf_op jit(solution)/shard_map/ppermute | solution.py:24
  123.4 2.7 copy-start.8
  123.4 2.7 copy-start.9
  123.4 2.7 copy-start.10
  126.1 3.1 copy-start.5
  126.1 3.1 copy-start.6
  130.7 4.0 copy-start.3
  130.7 4.0 copy-start.4
  136.1 3.6 copy-start
  139.7 1.6 copy-start.7
  141.3 3.7 copy-start.1
  141.3 3.7 copy-start.2
  145.0 1.7 copy-start.15
  145.0 2.3 copy-start.11
  145.0 2.3 copy-start.12
  150.6 405.0 %reduce-scatter.5.cloned.1.call-start = ((), (), s32[]{:S(2)}) async-start(), calls=%async_computation.4 | async-start | bytes 40960 | tf_op jit(solution)/shard_map/reduce_scatter | solution.py:162
Sparse Core Ops, SparseCore 0:
  150.7 321.5 reduce-scatter.2
  475.2 80.3 reduce-scatter.4
where the time goes:
time: 563 us; the launch traced here: 562 us
  waiting for transfers between devices  412 us (73%)
  matrix products  69.3 us (12%)
  starting transfers between devices  32.8 us (6%)
  other arithmetic  28.2 us (5%)
  between operations  14.2 us (3%)
  local copies, waits for them, and re-layouts  6.02 us (1%)
    reduce_scatter x1, waiting for transfers between devices, body(): owned = lax.psum_scatter(lagged, 'blk', scatter_dimension=0, tiled=True)  322 us
    reduce_scatter x1, waiting for transfers between devices, body(): stacks = lax.psum_scatter(owned, 'lag', scatter_dimension=2, tiled=True)  83.2 us
    dot_general x40, matrix products, cross_mask(): jnp.dot(weights, own_flat, preferred_element_type=jnp.float32)  41.9 us
    ppermute x5, starting transfers between devices, from_behind(): return lax.ppermute(block, axis, route)  29.1 us
    reduce_sum x10, other arithmetic, cross_mask(): jnp.sum(partner[..., :half_width] * mix_real + partner[..., half_width:]...  21 us
    dot_general x1, matrix products, body(): jnp.einsum('cwt,tf->cwf', filtered, transform_table(WIN, freq_ids, within...  17.9 us
  transfers between devices with their start and end apart: 8, of which 3 were waited for; matrix products, arithmetic and copies ran while one was open for 10% of the time, Pallas kernels for 0%

commit v1 on v0

v1 whole, which is shorter than its diff:
```python
import math

import jax
import jax.numpy as jnp
import numpy as np
from jax import lax
from jax.experimental import pallas as pl
from jax.experimental.pallas import tpu as pltpu
from jax.sharding import PartitionSpec as P

CB = 128
WIN = 1024
HALF = 512
NF = 512
TAPS = 128
NBIN = 8
BINW = 80
MEETINGS = 5
PCAP = 512
WINDOWS = 8
LANES = 256

BAND_LOW = 0.02
BAND_HIGH = 0.48
WATER = 0.1

LEVELS = tuple(
    tuple(range((1 if o == 0 else CB * o - CB + 1) // BINW, (CB * o + CB - 1) // BINW + 1)) for o in range(MEETINGS)
)
STARTS = tuple(sum(len(v) for v in LEVELS[:o]) for o in range(MEETINGS))
LEVEL_COUNT = sum(len(v) for v in LEVELS)

F32 = jnp.float32
BF16 = jnp.bfloat16
HI = lax.Precision.HIGHEST
VMEM_LIMIT = 48 * 1024 * 1024


def filter_table():
    k = np.arange(TAPS, dtype=np.float64)
    m = k - (TAPS - 1) / 2.0
    ideal = 2 * BAND_HIGH * np.sinc(2 * BAND_HIGH * m) - 2 * BAND_LOW * np.sinc(2 * BAND_LOW * m)
    taps = ideal * (0.5 - 0.5 * np.cos(2 * np.pi * (k + 0.5) / TAPS))
    lagged = np.arange(TAPS)[None, :] - np.arange(2 * TAPS)[:, None] + TAPS
    inside = (lagged >= 0) & (lagged < TAPS)
    return np.where(inside, taps[np.clip(lagged, 0, TAPS - 1)], 0.0).astype(np.float32)


def transform_table():
    phase = np.arange(HALF)[:, None] * np.arange(NF)[None, :] % WIN
    angle = phase * (2 * np.pi / WIN)
    return (np.concatenate([np.cos(angle), -np.sin(angle)], axis=1) / math.sqrt(WIN)).astype(jnp.bfloat16)


def inverse_table():
    phase = np.arange(NF)[:, None] * np.arange(LANES)[None, :] % WIN
    angle = phase * (2 * np.pi / WIN)
    weight = np.where(np.arange(NF) == 0, 1.0, 2.0)[:, None] / (WINDOWS * math.sqrt(WIN))
    return np.concatenate([weight * np.cos(angle), -weight * np.sin(angle)], axis=0).astype(np.float32)


def call(kernel, out_shape, *args, smem=(), scratch=()):
    specs = [
        pl.BlockSpec(memory_space=pltpu.SMEM) if n in smem else pl.BlockSpec(memory_space=pltpu.VMEM)
        for n in range(len(args))
    ]
    many = isinstance(out_shape, (tuple, list))
    out_specs = [pl.BlockSpec(memory_space=pltpu.VMEM)] * len(out_shape) if many else pl.BlockSpec(memory_space=pltpu.VMEM)
    return pl.pallas_call(
        kernel,
        out_shape=out_shape,
        in_specs=specs,
        out_specs=out_specs,
        scratch_shapes=list(scratch),
        compiler_params=pltpu.CompilerParams(vmem_limit_bytes=VMEM_LIMIT),
    )(*args)


def shape(dims, dtype):
    return jax.ShapeDtypeStruct(dims, dtype)


def spectra_kernel(hist_ref, x_ref, taps_ref, table_ref, out_ref):
    tiles = [hist_ref[...]] + [x_ref[:, t * TAPS : (t + 1) * TAPS] for t in range(WIN // TAPS)]
    pairs = [jnp.concatenate([tiles[t], tiles[t + 1]], axis=1) for t in range(WIN // TAPS)]
    rows = jnp.dot(jnp.concatenate(pairs, axis=0), taps_ref[...], precision=HI, preferred_element_type=F32)
    rows = rows.astype(BF16)
    filtered = [rows[t * CB : (t + 1) * CB] for t in range(WIN // TAPS)]
    early = jnp.concatenate(filtered[:4], axis=1)
    late = jnp.concatenate(filtered[4:], axis=1)
    column = lax.broadcasted_iota(jnp.int32, (1, WIN), 1)
    turn = jnp.where(column % 2 == 0, 1.0, -1.0).astype(F32)
    first = jnp.dot(early, table_ref[...], preferred_element_type=F32)
    second = jnp.dot(late, table_ref[...], preferred_element_type=F32)
    out_ref[...] = (first + turn * second).astype(BF16)


def power_kernel(core_ref, s0_ref, s1_ref, keep_ref, send_ref):
    core = core_ref[0]

    def part(start):
        total = jnp.zeros((CB // 2, NF), F32)
        for ref in (s0_ref, s1_ref):
            re = ref[pl.ds(start, CB // 2), :NF].astype(F32)
            im = ref[pl.ds(start, CB // 2), NF:].astype(F32)
            total = total + (re * re + im * im)
        return total * (1.0 / WINDOWS)

    keep_ref[...] = part(pl.multiple_of(core * (CB // 2), CB // 2))
    send_ref[...] = part(pl.multiple_of((1 - core) * (CB // 2), CB // 2)).astype(BF16)


def whiten_kernel(core_ref, s0_ref, s1_ref, own_ref, other_ref, out_ref):
    core = core_ref[0]
    for half in range(2):
        rows = slice(half * CB // 2, (half + 1) * CB // 2)
        gain = jnp.where(core == half, own_ref[...], other_ref[...])
        for w, ref in enumerate((s0_ref, s1_ref)):
            for part in range(2):
                cols = slice(part * NF, (part + 1) * NF)
                out_ref[w, rows, cols] = (ref[rows, cols].astype(F32) * gain).astype(BF16)


def mask_kernel(count_ref, codes_ref, out_ref):
    row = lax.broadcasted_iota(jnp.int32, (CB, PCAP), 0)
    slot = lax.broadcasted_iota(jnp.int32, (1, PCAP), 1)
    spread = lax.broadcasted_iota(jnp.int32, (CB, CB), 1) - lax.broadcasted_iota(jnp.int32, (CB, CB), 0)
    for o in range(MEETINGS):
        codes = codes_ref[o : o + 1, :]
        first = jnp.where(slot < count_ref[o], codes >> 7, -1)
        second = codes & (CB - 1)
        pick_first = (row == first).astype(F32).astype(BF16)
        pick_second = (row == second).astype(F32).astype(BF16)
        chosen = lax.dot_general(pick_first, pick_second, (((1,), (1,)), ((), ())), preferred_element_type=F32)
        distance = spread + CB * o
        for n, k in enumerate(LEVELS[o]):
            inside = (distance >= BINW * k) & (distance < BINW * (k + 1))
            out_ref[STARTS[o] + n] = jnp.where(inside, chosen, 0.0).astype(BF16)


def cross_rows(out_ref, mask_ref, a_ref, b_ref, o, row0, scale):
    chunk = 256
    for k in range(NBIN):
        row = slice(row0 + k, row0 + k + 1)
        if k not in LEVELS[o]:
            out_ref[row, :] = jnp.zeros((1, 2 * NF), F32)
            continue
        weights = mask_ref[STARTS[o] + LEVELS[o].index(k)]
        for c in range(NF // chunk):
            re_cols = slice(c * chunk, (c + 1) * chunk)
            im_cols = slice(NF + c * chunk, NF + (c + 1) * chunk)
            sum_re = jnp.zeros((8, chunk), F32)
            sum_im = jnp.zeros((8, chunk), F32)
            for w in range(2):
                mix_re = jnp.dot(weights, b_ref[w, :, re_cols], preferred_element_type=F32)
                mix_im = jnp.dot(weights, b_ref[w, :, im_cols], preferred_element_type=F32)
                a_re = a_ref[w, :, re_cols].astype(F32)
                a_im = a_ref[w, :, im_cols].astype(F32)
                prod_re = a_re * mix_re + a_im * mix_im
                prod_im = a_re * mix_im - a_im * mix_re
                sum_re = sum_re + jnp.sum(prod_re.reshape(CB // 8, 8, chunk), axis=0)
                sum_im = sum_im + jnp.sum(prod_im.reshape(CB // 8, 8, chunk), axis=0)
            out_ref[row, re_cols] = scale * jnp.sum(sum_re, axis=0, keepdims=True)
            out_ref[row, im_cols] = scale * jnp.sum(sum_im, axis=0, keepdims=True)


def own_cross_kernel(live_ref, mask_ref, own_ref, out_ref):
    cross_rows(out_ref, mask_ref, own_ref, own_ref, 0, 0, live_ref[0])


def far_cross_kernel(live_ref, mask_ref, own_ref, before_ref, after_ref, far_ref, out_ref):
    cross_rows(out_ref, mask_ref, before_ref, own_ref, 1, 0, live_ref[1])
    cross_rows(out_ref, mask_ref, before_ref, after_ref, 2, 8, live_ref[2])
    cross_rows(out_ref, mask_ref, after_ref, far_ref, 3, 16, live_ref[3])
    cross_rows(out_ref, mask_ref, own_ref, far_ref, 4, 24, live_ref[4])


def lag_kernel(near_ref, far_ref, table_ref, out_ref):
    rows = jnp.concatenate([near_ref[...], far_ref[...]], axis=0)
    re, im = rows[:, :NF], rows[:, NF:]
    freq = lax.broadcasted_iota(jnp.int32, (1, NF), 1)
    turned = []
    for quarter in range(4):
        step = (freq * (quarter + 2)) & 3
        along = jnp.where(step == 0, 1.0, 0.0) - jnp.where(step == 2, 1.0, 0.0)
        across = jnp.where(step == 1, 1.0, 0.0) - jnp.where(step == 3, 1.0, 0.0)
        turned.append(jnp.concatenate([re * along - im * across, re * across + im * along], axis=1))
    lagged = jnp.dot(jnp.concatenate(turned, axis=0), table_ref[...], precision=HI, preferred_element_type=F32)
    for quarter in range(4):
        out_ref[quarter] = lagged[quarter * 40 : (quarter + 1) * 40]


def owner_kernel(owner_ref, parts_ref, out_ref):
    total = parts_ref[0] + parts_ref[1] + parts_ref[2] + parts_ref[3]
    out_ref[...] = jnp.zeros(out_ref.shape, F32)
    for o in range(MEETINGS):
        owner = owner_ref[o]
        out_ref[owner] = out_ref[owner] + total[o * NBIN : (o + 1) * NBIN]


def shifted(block, distance, count):
    return lax.ppermute(block, "blk", [(i, (i + distance) % count) for i in range(count)])


def crossed(block, bit):
    return lax.ppermute(block, "lag", [(i, i ^ bit) for i in range(4)])


def body(traces, owner_map, pair_codes, pair_count):
    blocks = lax.axis_size("blk")
    blk = lax.axis_index("blk")
    core = (lax.axis_index("lag") % 2).astype(jnp.int32).reshape(1)
    taps = jnp.asarray(filter_table())
    table = jnp.asarray(transform_table())

    history = lax.ppermute(traces[:, -TAPS:], "lag", [(i, i + 1) for i in range(3)])
    lists = jnp.concatenate([pair_codes, pair_count, owner_map], axis=1)
    lists = jnp.concatenate(
        [lists[:2], shifted(lists[2:3], -1, blocks), shifted(lists[3:5], -4, blocks)], axis=0
    )
    later = (blk + jnp.asarray(np.array([0, 0, 1, 4, 4], np.int32))) % blocks
    live = (later >= jnp.arange(MEETINGS, dtype=jnp.int32)).astype(F32)
    masks = call(
        mask_kernel, shape((LEVEL_COUNT, CB, CB), BF16), lists[:, PCAP], lists[:, :PCAP], smem=(0,)
    )

    spec = shape((CB, WIN), BF16)
    spectra1 = call(spectra_kernel, spec, traces[:, WIN - TAPS : WIN], traces[:, WIN:], taps, table)
    spectra0 = call(spectra_kernel, spec, history, traces[:, :WIN], taps, table)

    half = (CB // 2, NF)
    keep, send = call(power_kernel, (shape(half, F32), shape(half, BF16)), core, spectra0, spectra1, smem=(0,))
    chip = keep + crossed(send, 1).astype(F32)
    power = chip + crossed(chip.astype(BF16), 2).astype(F32)
    gain = lax.rsqrt(power + WATER)
    whitened = call(
        whiten_kernel, shape((2, CB, WIN), BF16), core, spectra0, spectra1, gain, crossed(gain, 1), smem=(0,)
    )

    before = shifted(whitened, 1, blocks)
    after = shifted(whitened, -1, blocks)
    far = shifted(whitened, -4, blocks)
    near_rows = call(own_cross_kernel, shape((NBIN, WIN), F32), live, masks, whitened, smem=(0,))
    far_rows = call(
        far_cross_kernel, shape((4 * NBIN, WIN), F32), live, masks, whitened, before, after, far, smem=(0,)
    )
    lagged = call(lag_kernel, shape((4, 5 * NBIN, LANES), F32), near_rows, far_rows, jnp.asarray(inverse_table()))
    parts = lax.all_to_all(lagged, "lag", 0, 0, tiled=True)
    slabs = call(owner_kernel, shape((blocks, NBIN, LANES), F32), lists[:, PCAP + 1], parts, smem=(0,))
    return jnp.sum(lax.all_to_all(slabs, "blk", 0, 0, tiled=True), axis=0, keepdims=True)


def solution(mesh):
    return jax.shard_map(
        body,
        mesh=mesh,
        in_specs=(P("blk", "lag"), P(None, "blk"), P(None, "blk"), P(None, "blk")),
        out_specs=P("blk", None, "lag"),
        check_vma=False,
    )
```

time: 563 us -> 113 us (0.20)
  waiting for transfers between devices: 412 us -> 24.2 us
  matrix products: 69.3 us -> 0 us
  blocking collectives: 0 us -> 45.4 us
  other arithmetic: 28.2 us -> 1.08 us
  between operations: 14.2 us -> 0.21 us
  Pallas kernels: 0 us -> 12.2 us
  starting transfers between devices: 32.8 us -> 26.7 us
    reduce_scatter x2 -> x0, waiting for transfers between devices: 405 us -> none  [the longest x1 322 us: body(): owned = lax.psum_scatter(lagged, 'blk', scatter_dimension=0, tiled=True)]
    dot_general x49 -> x0, matrix products: 69.3 us -> none  [the longest x40 41.9 us: cross_mask(): jnp.dot(weights, own_flat, preferred_element_type=jnp.float32)]
    all_to_all x0 -> x2, blocking collectives: none -> 45.4 us  [the longest x1 27.7 us: body(): lax.all_to_all(slabs, 'blk', 0, 0, tiled=True)]
    ppermute x5 -> x9, waiting for transfers between devices: 0.01 us -> 24.2 us  [the longest x5 18.9 us: shifted(): lax.ppermute(block, 'blk', [(i, (i + distance) % count) for i in range(co...]
    reduce_sum x11 -> x1, other arithmetic: 21.1 us -> 0.67 us  [body(): jnp.sum(lax.all_to_all(slabs, 'blk', 0, 0, tiled=True), axis=0, keepdims=...]
    pallas_call x0 -> x9, Pallas kernels: none -> 12.2 us  [call(): pl.pallas_call(kernel, out_shape=out_shape, in_specs=specs, out_specs=out...]
    all_to_all x1 -> x0, waiting for transfers between devices: 7.01 us -> none  [body(): lax.all_to_all(spectra, 'lag', split_axis=2, concat_axis=1, tiled=True)]
    ppermute x5 -> x9, starting transfers between devices: 29.1 us -> 26.7 us  [the longest x5 10.8 us: shifted(): lax.ppermute(block, 'blk', [(i, (i + distance) % count) for i in range(co...]
  transfers between devices with their start and end apart: 8 -> 9, of which waited for: 3 -> 4; matrix products, arithmetic and copies ran while one was open for 10% -> 2% of each run, Pallas kernels for 0% -> 3%
where the time goes in v1:
time: 113 us
  blocking collectives  45.4 us (40%)
  starting transfers between devices  26.7 us (24%)
  waiting for transfers between devices  24.2 us (21%)
  Pallas kernels  12.2 us (11%)
  local copies, waits for them, and re-layouts  3.03 us (3%)
    all_to_all x1, blocking collectives, body(): lax.all_to_all(slabs, 'blk', 0, 0, tiled=True)  27.7 us
    ppermute x5, waiting for transfers between devices, shifted(): lax.ppermute(block, 'blk', [(i, (i + distance) % count) for i in range(co...  18.9 us
    all_to_all x1, blocking collectives, body(): parts = lax.all_to_all(lagged, 'lag', 0, 0, tiled=True)  17.7 us
    pallas_call x9, Pallas kernels, call(): pl.pallas_call(kernel, out_shape=out_shape, in_specs=specs, out_specs=out...  12.2 us
    ppermute x5, starting transfers between devices, shifted(): lax.ppermute(block, 'blk', [(i, (i + distance) % count) for i in range(co...  10.8 us
    ppermute x1, starting transfers between devices, body(): lax.ppermute(traces[:, -TAPS:], 'lag', [(i, i + 1) for i in range(3)])  10.3 us
    ppermute x3, starting transfers between devices, crossed(): return lax.ppermute(block, 'lag', [(i, i ^ bit) for i in range(4)])  5.51 us
    ppermute x3, waiting for transfers between devices, crossed(): return lax.ppermute(block, 'lag', [(i, i ^ bit) for i in range(4)])  5.31 us
  transfers between devices with their start and end apart: 9, of which 4 were waited for; matrix products, arithmetic and copies ran while one was open for 2% of the time, Pallas kernels for 3%

profile of v1, /device:TPU:1, one launch (start us, length us, event | category | flops | bytes accessed | tf_op | source)
XLA Modules:
  0.0 112.8 jit_solution(653013508670222332)
XLA Ops:
  0.0 0.9 fusion.3
  0.9 0.0 copy-start
  0.9 0.0 copy-start.2
  0.9 10.3 %collective-permute-start.2 = (f32[128,128]{1,0:T(8,128)S(1)}, f32[128,128]{1,0:T(8,128)S(1)}, u32[]{:S(2)}, u32[]{:S(2)}) collective-permute-start(f32[128,128]{1,0:T(8,128)S(1)} %get-tuple-element.14), channel_id=1, source_target_pairs={{0,1},{1,2},{2,3},{4,5},{5,6},{6,7},{8,9},{9,10},{10,11},{12,13},{... | collective-permute-start | bytes 196616 | tf_op jit(solution)/shard_map/ppermute | solution.py:216
  11.3 1.3 %fusion.2 = (f32[128,1024]{1,0:T(8,128)S(1)}, f32[128,1024]{1,0:T(8,128)S(1)}) fusion(f32[128,2048]{1,0:T(8,128)} %param.8), kind=kLoop, calls=%fused_computation.16 | loop fusion | bytes 2097152 | tf_op jit(solution)/shard_map/slice | solution.py:228
  12.5 0.0 copy-done
  12.6 0.0 copy-done.2
  12.6 1.8 %shard_map.84.s1_ref = bf16[128,1024]{1,0:T(8,128)(2,1)S(1)} custom-call(f32[128,128]{1,0:T(8,128)S(1)} %get-tuple-element.13.hist_ref, f32[128,1024]{1,0:T(8,128)S(1)} %get-tuple-element.11.x_ref, f32[256,128]{1,0:T(8,128)S(1)} %copy-done.2, bf16[512,1024]{1,0:T(8,128)(2,1)S(1)} %copy-done), custom_call_target="tpu_custom_call" | custom-call | tf_op jit(solution)/shard_map/pallas_call | solution.py:69
  14.4 0.0 collective-permute-done.2.hist_ref
  14.4 1.8 %shard_map.83.s0_ref = bf16[128,1024]{1,0:T(8,128)(2,1)S(1)} custom-call(f32[128,128]{1,0:T(8,128)S(1)} %collective-permute-done.2.hist_ref, f32[128,1024]{1,0:T(8,128)S(1)} %get-tuple-element.12.x_ref, f32[256,128]{1,0:T(8,128)S(1)} %copy-done.2, bf16[512,1024]{1,0:T(8,128)(2,1)S(1)} %copy-done), custom_call_target="tpu_custom_call" | custom-call | tf_op jit(solution)/shard_map/pallas_call | solution.py:69
  16.2 0.1 shard_map.85
  16.4 0.1 collective-permute-start.3
  16.5 1.2 %collective-permute-done.3 = bf16[64,512]{1,0:T(8,128)(2,1)S(1)} collective-permute-done((bf16[64,512]{1,0:T(8,128)(2,1)S(1)}, bf16[64,512]{1,0:T(8,128)(2,1)S(1)}, u32[]{:S(2)}, u32[]{:S(2)}) %collective-permute-start.3) | collective-permute-done | bytes 65568 | tf_op jit(solution)/shard_map/ppermute | solution.py:206
  17.7 0.0 copy-start.4
  17.7 4.3 %collective-permute-start.4 = (bf16[64,512]{1,0:T(8,128)(2,1)S(1)}, bf16[64,512]{1,0:T(8,128)(2,1)S(1)}, u32[]{:S(2)}, u32[]{:S(2)}) collective-permute-start(bf16[64,512]{1,0:T(8,128)(2,1)S(1)} %fusion), channel_id=1, source_target_pairs={{0,2},{1,3},{2,0},{3,1},{4,6},{5,7},{6,4},{7,5},{8,10},{9,11},{10,... | collective-permute-start | bytes 196616 | tf_op jit(solution)/shard_map/ppermute | solution.py:206
  22.0 3.3 %collective-permute-done.4 = bf16[64,512]{1,0:T(8,128)(2,1)S(1)} collective-permute-done((bf16[64,512]{1,0:T(8,128)(2,1)S(1)}, bf16[64,512]{1,0:T(8,128)(2,1)S(1)}, u32[]{:S(2)}, u32[]{:S(2)}) %collective-permute-start.4) | collective-permute-done | bytes 65568 | tf_op jit(solution)/shard_map/ppermute | solution.py:206
  25.3 0.0 copy-start.5
  25.3 1.1 %collective-permute-start.5 = (f32[64,512]{1,0:T(8,128)S(1)}, f32[64,512]{1,0:T(8,128)S(1)}, u32[]{:S(2)}, u32[]{:S(2)}) collective-permute-start(f32[64,512]{1,0:T(8,128)S(1)} %add_rsqrt_fusion.own_ref), channel_id=1, source_target_pairs={{0,1},{1,0},{2,3},{3,2},{4,5},{5,4},{6,7},{7,6},{8,9},{9,8},{10,11... | collective-permute-start | bytes 393224 | tf_op jit(solution)/shard_map/ppermute | solution.py:206
  26.5 0.0 copy-done.4
  26.5 0.1 copy.11
  26.6 0.0 copy-done.5
  26.6 0.1 copy.12
  26.7 0.0 copy-start.3
  26.7 0.8 collective-permute-done.5.other_ref
  27.5 0.1 shard_map.86.own_ref
  27.6 1.3 %collective-permute-start.6 = (bf16[2,128,1024]{2,1,0:T(8,128)(2,1)S(1)}, bf16[2,128,1024]{2,1,0:T(8,128)(2,1)S(1)}, u32[]{:S(2)}, u32[]{:S(2)}) collective-permute-start(bf16[2,128,1024]{2,1,0:T(8,128)(2,1)S(1)} %shard_map.86.own_ref), channel_id=1, source_target_pairs={{0,4},{4,8},{8,12},{12,16},{16,20},{20,24},{24,28},{28,32},{32,36}... | collective-permute-start | bytes 1572872 | tf_op jit(solution)/shard_map/ppermute | solution.py:202
  28.9 6.3 %collective-permute-start.7 = (bf16[2,128,1024]{2,1,0:T(8,128)(2,1)S(1)}, bf16[2,128,1024]{2,1,0:T(8,128)(2,1)S(1)}, u32[]{:S(2)}, u32[]{:S(2)}) collective-permute-start(bf16[2,128,1024]{2,1,0:T(8,128)(2,1)S(1)} %shard_map.86.own_ref), channel_id=1, source_target_pairs={{0,252},{4,0},{8,4},{12,8},{16,12},{20,16},{24,20},{28,24},{32,28}... | collective-permute-start | bytes 1572872 | tf_op jit(solution)/shard_map/ppermute | solution.py:202
  35.1 0.9 collective-permute-start.8
  36.1 0.0 copy-done.3
  36.1 0.1 pad_add_fusion.4
  36.1 1.3 %collective-permute-start.1 = (s32[2,514]{1,0:T(2,128)S(1)}, s32[2,514]{1,0:T(2,128)S(1)}, u32[]{:S(2)}, u32[]{:S(2)}) collective-permute-start(s32[2,514]{1,0:T(2,128)S(1)} %get-tuple-element.16), channel_id=1, source_target_pairs={{0,240},{4,244},{8,248},{12,252},{16,0},{20,4},{24,8},{28,12},{32,... | collective-permute-start | bytes 12344 | tf_op jit(solution)/shard_map/ppermute | solution.py:202
  37.4 0.1 pad_add_fusion.5
  37.5 1.0 collective-permute-start
  38.6 0.0 copy-start.6
  38.6 0.7 copy-done.6
  39.2 18.9 %collective-permute-done = s32[1,514]{1,0:T(1,128)S(1)} collective-permute-done((s32[1,514]{1,0:T(1,128)S(1)}, s32[1,514]{1,0:T(1,128)S(1)}, u32[]{:S(2)}, u32[]{:S(2)}) %collective-permute-start) | collective-permute-done | bytes 2088 | tf_op jit(solution)/shard_map/ppermute | solution.py:202
  58.1 0.0 collective-permute-done.1
  58.1 0.2 add_reduce_fusion
  58.4 0.9 shard_map.82.mask_ref
  59.3 1.1 shard_map.87.near_ref
  60.4 0.0 copy-start.1
  60.5 0.0 collective-permute-done.6.before_ref
  60.5 0.0 collective-permute-done.7.after_ref
  60.5 0.0 collective-permute-done.8.far_ref
  60.5 4.7 %shard_map.88.far_ref = f32[32,1024]{1,0:T(8,128)S(1)} custom-call(f32[5]{0:T(128)S(1)} %compare_convert_fusion.live_ref, bf16[18,128,128]{2,1,0:T(8,128)(2,1)S(1)} %shard_map.82.mask_ref, bf16[2,128,1024]{2,1,0:T(8,128)(2,1)S(1)} %shard_map.86.own_ref, bf16[2,128,1024]{2,1,0:T(8,128)(2,1)S(1)} %collective-permute-done.6.before_ref, ...), custom_call_target="tpu_custom_call" | custom-call | tf_op jit(solution)/shard_map/pallas_call | solution.py:69
  65.2 0.0 copy-done.1
  65.2 0.9 shard_map.89
  66.2 17.7 %all_to_all.10.parts_ref = f32[4,40,256]{2,1,0:T(8,128)S(1)} all-to-all(f32[4,40,256]{2,1,0:T(8,128)S(1)} %shard_map.89), channel_id=1, replica_groups=mesh['blk'=64,'lag'=4] {'lag'}, dimensions={0} | all-to-all | bytes 327680 | tf_op jit(solution)/shard_map/all_to_all | solution.py:248
  83.9 0.6 shard_map.90
  84.5 27.7 %all_to_all.11 = f32[64,8,256]{2,1,0:T(8,128)S(1)} all-to-all(f32[64,8,256]{2,1,0:T(8,128)S(1)} %shard_map.90), channel_id=1, replica_groups=mesh['blk'=64,'lag'=4] {'blk'}, dimensions={0} | all-to-all | bytes 1048576 | tf_op jit(solution)/shard_map/all_to_all | solution.py:250
  112.1 0.7 reduce_sum.9
  (4 shorter events, 0.1 us)
Async XLA Ops:
  0.9 11.7 %copy-start = (bf16[512,1024]{1,0:T(8,128)(2,1)S(1)}, bf16[512,1024]{1,0:T(8,128)(2,1)}, u32[]{:S(2)}) copy-start(bf16[512,1024]{1,0:T(8,128)(2,1)} %constant.49.clone.table_ref) | copy-start | bytes 3145732
  0.9 11.7 %copy-start.2 = (f32[256,128]{1,0:T(8,128)S(1)}, f32[256,128]{1,0:T(8,128)}, u32[]{:S(2)}) copy-start(f32[256,128]{1,0:T(8,128)} %constant.48.clone.taps_ref) | copy-start | bytes 393220
  0.9 13.5 %collective-permute-start.2 = (f32[128,128]{1,0:T(8,128)S(1)}, f32[128,128]{1,0:T(8,128)S(1)}, u32[]{:S(2)}, u32[]{:S(2)}) collective-permute-start(f32[128,128]{1,0:T(8,128)S(1)} %get-tuple-element.14), channel_id=1, source_target_pairs={{0,1},{1,2},{2,3},{4,5},{5,6},{6,7},{8,9},{9,10},{10,11},{12,13},{... | collective-permute-start | bytes 196616 | tf_op jit(solution)/shard_map/ppermute | solution.py:216
  16.4 1.3 %collective-permute-start.3 = (bf16[64,512]{1,0:T(8,128)(2,1)S(1)}, bf16[64,512]{1,0:T(8,128)(2,1)S(1)}, u32[]{:S(2)}, u32[]{:S(2)}) collective-permute-start(bf16[64,512]{1,0:T(8,128)(2,1)S(1)} %get-tuple-element.8), channel_id=1, source_target_pairs={{0,1},{1,0},{2,3},{3,2},{4,5},{5,4},{6,7},{7,6},{8,9},{9,8},{10,11... | collective-permute-start | bytes 196616 | tf_op jit(solution)/shard_map/ppermute | solution.py:206
  17.7 8.8 %copy-start.4 = (s32[5,1]{0,1:T(1,128)S(1)}, s32[5,1]{0,1:T(1,128)}, u32[]{:S(2)}) copy-start(s32[5,1]{0,1:T(1,128)} %param.11) | copy-start | bytes 64
  17.7 7.5 %collective-permute-start.4 = (bf16[64,512]{1,0:T(8,128)(2,1)S(1)}, bf16[64,512]{1,0:T(8,128)(2,1)S(1)}, u32[]{:S(2)}, u32[]{:S(2)}) collective-permute-start(bf16[64,512]{1,0:T(8,128)(2,1)S(1)} %fusion), channel_id=1, source_target_pairs={{0,2},{1,3},{2,0},{3,1},{4,6},{5,7},{6,4},{7,5},{8,10},{9,11},{10,... | collective-permute-start | bytes 196616 | tf_op jit(solution)/shard_map/ppermute | solution.py:206
  25.3 1.3 %copy-start.5 = (s32[5,1]{0,1:T(1,128)S(1)}, s32[5,1]{0,1:T(1,128)}, u32[]{:S(2)}) copy-start(s32[5,1]{0,1:T(1,128)} %param.9) | copy-start | bytes 64
  25.3 2.1 %collective-permute-start.5 = (f32[64,512]{1,0:T(8,128)S(1)}, f32[64,512]{1,0:T(8,128)S(1)}, u32[]{:S(2)}, u32[]{:S(2)}) collective-permute-start(f32[64,512]{1,0:T(8,128)S(1)} %add_rsqrt_fusion.own_ref), channel_id=1, source_target_pairs={{0,1},{1,0},{2,3},{3,2},{4,5},{5,4},{6,7},{7,6},{8,9},{9,8},{10,11... | collective-permute-start | bytes 393224 | tf_op jit(solution)/shard_map/ppermute | solution.py:206
  26.7 9.4 %copy-start.3 = (s32[5,512]{1,0:T(8,128)S(1)}, s32[5,512]{1,0:T(8,128)}, u32[]{:S(2)}) copy-start(s32[5,512]{1,0:T(8,128)} %param.10) | copy-start | bytes 30724
  27.6 32.9 %collective-permute-start.6 = (bf16[2,128,1024]{2,1,0:T(8,128)(2,1)S(1)}, bf16[2,128,1024]{2,1,0:T(8,128)(2,1)S(1)}, u32[]{:S(2)}, u32[]{:S(2)}) collective-permute-start(bf16[2,128,1024]{2,1,0:T(8,128)(2,1)S(1)} %shard_map.86.own_ref), channel_id=1, source_target_pairs={{0,4},{4,8},{8,12},{12,16},{16,20},{20,24},{24,28},{28,32},{32,36}... | collective-permute-start | bytes 1572872 | tf_op jit(solution)/shard_map/ppermute | solution.py:202
  28.9 31.6 %collective-permute-start.7 = (bf16[2,128,1024]{2,1,0:T(8,128)(2,1)S(1)}, bf16[2,128,1024]{2,1,0:T(8,128)(2,1)S(1)}, u32[]{:S(2)}, u32[]{:S(2)}) collective-permute-start(bf16[2,128,1024]{2,1,0:T(8,128)(2,1)S(1)} %shard_map.86.own_ref), channel_id=1, source_target_pairs={{0,252},{4,0},{8,4},{12,8},{16,12},{20,16},{24,20},{28,24},{32,28}... | collective-permute-start | bytes 1572872 | tf_op jit(solution)/shard_map/ppermute | solution.py:202
  35.1 25.3 %collective-permute-start.8 = (bf16[2,128,1024]{2,1,0:T(8,128)(2,1)S(1)}, bf16[2,128,1024]{2,1,0:T(8,128)(2,1)S(1)}, u32[]{:S(2)}, u32[]{:S(2)}) collective-permute-start(bf16[2,128,1024]{2,1,0:T(8,128)(2,1)S(1)} %shard_map.86.own_ref), channel_id=1, source_target_pairs={{0,240},{4,244},{8,248},{12,252},{16,0},{20,4},{24,8},{28,12},{32,... | collective-permute-start | bytes 1572872 | tf_op jit(solution)/shard_map/ppermute | solution.py:202
  36.1 22.0 %collective-permute-start.1 = (s32[2,514]{1,0:T(2,128)S(1)}, s32[2,514]{1,0:T(2,128)S(1)}, u32[]{:S(2)}, u32[]{:S(2)}) collective-permute-start(s32[2,514]{1,0:T(2,128)S(1)} %get-tuple-element.16), channel_id=1, source_target_pairs={{0,240},{4,244},{8,248},{12,252},{16,0},{20,4},{24,8},{28,12},{32,... | collective-permute-start | bytes 12344 | tf_op jit(solution)/shard_map/ppermute | solution.py:202
  37.5 20.6 %collective-permute-start = (s32[1,514]{1,0:T(1,128)S(1)}, s32[1,514]{1,0:T(1,128)S(1)}, u32[]{:S(2)}, u32[]{:S(2)}) collective-permute-start(s32[1,514]{1,0:T(1,128)S(1)} %pad_add_fusion.5), channel_id=1, source_target_pairs={{0,252},{4,0},{8,4},{12,8},{16,12},{20,16},{24,20},{28,24},{32,28}... | collective-permute-start | bytes 6176 | tf_op jit(solution)/shard_map/ppermute | solution.py:202
  38.6 0.7 copy-start.6
  60.4 4.8 %copy-start.1 = (f32[1024,256]{1,0:T(8,128)S(1)}, f32[1024,256]{1,0:T(8,128)}, u32[]{:S(2)}) copy-start(f32[1024,256]{1,0:T(8,128)} %constant.51.clone.table_ref) | copy-start | bytes 3145732

commit v2 on v1

v2 whole, which is shorter than its diff:
```python
import math

import jax
import jax.numpy as jnp
import numpy as np
from jax import lax
from jax.experimental import pallas as pl
from jax.experimental.pallas import tpu as pltpu
from jax.sharding import Mesh
from jax.sharding import PartitionSpec as P

CB = 128
WIN = 1024
HALF = 512
NF = 512
TAPS = 128
NBIN = 8
BINW = 80
ROUNDS = 4
MEETINGS = 5
PCAP = 512
WINDOWS = 8
LANES = 256
PLANE = 16
ROWS = 4
PARTS = 8
BAND = 64
LIST_ROWS = 24

BAND_LOW = 0.02
BAND_HIGH = 0.48
WATER = 0.1

F32 = jnp.float32
BF16 = jnp.bfloat16
HI = lax.Precision.HIGHEST
VMEM_LIMIT = 48 * 1024 * 1024


def level_rows(o):
    found = []
    for k in range(NBIN):
        pairs = [
            i
            for i in range(CB)
            for j in range(CB)
            if (o > 0 or i < j) and (CB * o + j - i) // BINW == k
        ]
        if pairs:
            found.append((k, min(pairs) // 16 * 16, max(pairs) // 16 * 16 + 16))
    return tuple(found)


LEVELS = tuple(level_rows(o) for o in range(MEETINGS))
STARTS = tuple(sum(len(v) for v in LEVELS[:o]) for o in range(MEETINGS))
LEVEL_COUNT = sum(len(v) for v in LEVELS)


def filter_table():
    k = np.arange(TAPS, dtype=np.float64)
    m = k - (TAPS - 1) / 2.0
    ideal = 2 * BAND_HIGH * np.sinc(2 * BAND_HIGH * m) - 2 * BAND_LOW * np.sinc(2 * BAND_LOW * m)
    taps = ideal * (0.5 - 0.5 * np.cos(2 * np.pi * (k + 0.5) / TAPS))
    lagged = np.arange(TAPS)[None, :] - np.arange(2 * TAPS)[:, None] + TAPS
    inside = (lagged >= 0) & (lagged < TAPS)
    return np.where(inside, taps[np.clip(lagged, 0, TAPS - 1)], 0.0).astype(np.float32)


def column_order():
    column = np.arange(WIN)
    return column // (2 * BAND) * BAND + column % BAND, column // BAND % 2 == 1


def transform_table():
    freq, is_imag = column_order()
    angle = (np.arange(HALF)[:, None] * freq[None, :] % WIN) * (2 * np.pi / WIN)
    return (np.where(is_imag[None, :], -np.sin(angle), np.cos(angle)) / math.sqrt(WIN)).astype(jnp.bfloat16)


def inverse_table():
    freq, is_imag = column_order()
    angle = (freq[:, None] * np.arange(LANES)[None, :] % WIN) * (2 * np.pi / WIN)
    weight = np.where(freq == 0, 1.0, 2.0)[:, None] / (WINDOWS * math.sqrt(WIN))
    return (weight * np.where(is_imag[:, None], -np.sin(angle), np.cos(angle))).astype(np.float32)


def bin_table():
    spread = np.arange(CB)[None, :] - np.arange(CB)[:, None]
    tables = [
        ((CB * o + spread) // BINW == k).astype(jnp.bfloat16) for o in range(MEETINGS) for k, _, _ in LEVELS[o]
    ]
    return np.stack(tables)


def call(kernel, out_shape, *args, smem=(), aliases=None):
    specs = [
        pl.BlockSpec(memory_space=pltpu.SMEM) if n in smem else pl.BlockSpec(memory_space=pltpu.VMEM)
        for n in range(len(args))
    ]
    many = isinstance(out_shape, (tuple, list))
    out_specs = [pl.BlockSpec(memory_space=pltpu.VMEM)] * len(out_shape) if many else pl.BlockSpec(memory_space=pltpu.VMEM)
    return pl.pallas_call(
        kernel,
        out_shape=out_shape,
        in_specs=specs,
        out_specs=out_specs,
        input_output_aliases=aliases or {},
        compiler_params=pltpu.CompilerParams(vmem_limit_bytes=VMEM_LIMIT),
    )(*args)


def shape(dims, dtype):
    return jax.ShapeDtypeStruct(dims, dtype)


def low_lanes(width=2 * BAND):
    return lax.broadcasted_iota(jnp.int32, (1, width), 1) < BAND


def spectra_kernel(hist_ref, x_ref, taps_ref, table_ref, out_ref):
    tiles = [hist_ref[...]] + [x_ref[:, t * TAPS : (t + 1) * TAPS] for t in range(WIN // TAPS)]
    pairs = [jnp.concatenate([tiles[t], tiles[t + 1]], axis=1) for t in range(WIN // TAPS)]
    rows = jnp.dot(jnp.concatenate(pairs, axis=0), taps_ref[...], precision=HI, preferred_element_type=F32)
    rows = rows.astype(BF16)
    filtered = [rows[t * CB : (t + 1) * CB] for t in range(WIN // TAPS)]
    early = jnp.concatenate(filtered[:4], axis=1)
    late = jnp.concatenate(filtered[4:], axis=1)
    column = lax.broadcasted_iota(jnp.int32, (1, WIN), 1)
    turn = jnp.where(column % 2 == 0, 1.0, -1.0).astype(F32)
    first = jnp.dot(early, table_ref[...], preferred_element_type=F32)
    second = jnp.dot(late, table_ref[...], preferred_element_type=F32)
    out_ref[...] = (first + turn * second).astype(BF16)


def power_kernel(core_ref, s0_ref, s1_ref, keep_ref, send_ref):
    core = core_ref[0]
    low = low_lanes()

    def part(start, ref):
        for pair in range(PARTS // 2):
            both = []
            for q in (2 * pair, 2 * pair + 1):
                cols = slice(q * 2 * BAND, (q + 1) * 2 * BAND)
                square = jnp.zeros((CB // 2, 2 * BAND), F32)
                for source in (s0_ref, s1_ref):
                    values = source[pl.ds(start, CB // 2), cols].astype(F32)
                    square = square + values * values
                both.append(square + pltpu.roll(square, BAND, 1))
            merged = jnp.where(low, both[0], both[1]) * (1.0 / WINDOWS)
            ref[:, pair * 2 * BAND : (pair + 1) * 2 * BAND] = merged.astype(ref.dtype)

    part(pl.multiple_of(core * (CB // 2), CB // 2), keep_ref)
    part(pl.multiple_of((1 - core) * (CB // 2), CB // 2), send_ref)


def whiten_kernel(core_ref, s0_ref, s1_ref, own_ref, other_ref, out_ref):
    core = core_ref[0]
    low = low_lanes()
    for half in range(2):
        rows = slice(half * CB // 2, (half + 1) * CB // 2)
        for pair in range(PARTS // 2):
            cols = slice(pair * 2 * BAND, (pair + 1) * 2 * BAND)
            gain = jnp.where(core == half, own_ref[:, cols], other_ref[:, cols])
            turned = pltpu.roll(gain, BAND, 1)
            for q, spread in ((2 * pair, jnp.where(low, gain, turned)), (2 * pair + 1, jnp.where(low, turned, gain))):
                for w, ref in enumerate((s0_ref, s1_ref)):
                    values = ref[rows, q * 2 * BAND : (q + 1) * 2 * BAND].astype(F32)
                    out_ref[2 * q + w, rows, :] = (values * spread).astype(BF16)


def list_kernel(blk_ref, count_ref, owner_ref, codes_ref, out_ref):
    lane = lax.broadcasted_iota(jnp.int32, (1, CB), 1)
    rows = []
    owners = jnp.zeros((1, CB), jnp.int32)
    for o in range(MEETINGS):
        live = jnp.where(blk_ref[0] >= o, count_ref[o, 0], 0)
        for n in range(4):
            rows.append(jnp.where(lane + n * CB < live, codes_ref[o : o + 1, n * CB : (n + 1) * CB], -1))
        owners = jnp.where(lane == o, owner_ref[o, 0], owners)
    rows = rows + [owners] + [jnp.zeros((1, CB), jnp.int32)] * (LIST_ROWS - len(rows) - 1)
    block = jnp.concatenate(rows, axis=0)
    for p in range(PLANE):
        out_ref[p] = block


def chosen_kernel(lists_ref, out_ref):
    row = lax.broadcasted_iota(jnp.int32, (CB, PCAP), 0)

    def one(p, carry):
        for o in range(MEETINGS):
            pieces = [lists_ref[p, o * 4 + n : o * 4 + n + 1, :] for n in range(4)]
            codes = jnp.concatenate(pieces, axis=1)
            pick_first = jnp.where(row == (codes >> 7), 1.0, 0.0).astype(BF16)
            pick_second = jnp.where(row == (codes & (CB - 1)), 1.0, 0.0).astype(BF16)
            chosen = lax.dot_general(pick_first, pick_second, (((1,), (1,)), ((), ())), preferred_element_type=F32)
            out_ref[p, o] = chosen.astype(BF16)
        return carry

    lax.fori_loop(0, PLANE, one, 0)


def meet(out_ref, bins_ref, chosen, a_block, b_block, o, owner):
    low = low_lanes()
    sign = jnp.where(low, -1.0, 1.0)
    weights = jnp.concatenate(
        [chosen[lo:hi] * bins_ref[STARTS[o] + n, lo:hi, :] for n, (_, lo, hi) in enumerate(LEVELS[o])], axis=0
    )
    mixed = jnp.dot(weights, b_block, preferred_element_type=F32)
    straight = a_block.astype(F32)
    swapped = pltpu.roll(straight, BAND, 1) * sign
    row_id = lax.broadcasted_iota(jnp.int32, (NBIN, 2 * BAND), 0)
    real = jnp.zeros((NBIN, 2 * BAND), F32)
    imag = jnp.zeros((NBIN, 2 * BAND), F32)
    at = 0
    for k, lo, hi in LEVELS[o]:
        part = mixed[at : at + hi - lo]
        at += hi - lo
        dims = ((hi - lo) // 8, 8, 2 * BAND)
        along = jnp.sum(jnp.sum((straight[lo:hi] * part).reshape(dims), axis=0), axis=0, keepdims=True)
        across = jnp.sum(jnp.sum((swapped[lo:hi] * part).reshape(dims), axis=0), axis=0, keepdims=True)
        real = jnp.where(row_id == k, along, real)
        imag = jnp.where(row_id == k, across, imag)
    terms = jnp.where(low, real + pltpu.roll(real, BAND, 1), imag + pltpu.roll(imag, BAND, 1))
    spot = (owner % PLANE) * ROWS + owner // PLANE
    out_ref[spot] = out_ref[spot] + terms


def plane_kernel(owner_ref, bins_ref, chosen_ref, group_ref, out_ref):
    out_ref[...] = jnp.zeros(out_ref.shape, F32)
    for o in range(MEETINGS):

        def one(p, carry, o=o):
            meet(out_ref, bins_ref, chosen_ref[p, o], group_ref[p - o], group_ref[p], o, owner_ref[p, o])
            return carry

        lax.fori_loop(o, PLANE, one, 0)


def below_kernel(owner_ref, bins_ref, chosen_ref, group_ref, below_ref, sums_ref, out_ref):
    out_ref[...] = sums_ref[...]
    for o in range(1, MEETINGS):

        def one(p, carry, o=o):
            meet(out_ref, bins_ref, chosen_ref[p, o], below_ref[p - o + ROUNDS], group_ref[p], o, owner_ref[p, o])
            return carry

        lax.fori_loop(0, o, one, 0)


def lag_kernel(parts_ref, table_ref, out_ref):
    lane = lax.broadcasted_iota(jnp.int32, (1, 2 * BAND), 1)
    sign = jnp.where(lane < BAND, -1.0, 1.0)
    merged = [parts_ref[2 * q] + parts_ref[2 * q + 1] for q in range(PARTS)]
    swapped = [pltpu.roll(value, BAND, 1) for value in merged]
    turned = []
    for quarter in range(4):
        step = (lane * (quarter + 2)) & 3
        along = jnp.where(step == 0, 1.0, 0.0) - jnp.where(step == 2, 1.0, 0.0)
        across = sign * (jnp.where(step == 1, 1.0, 0.0) - jnp.where(step == 3, 1.0, 0.0))
        turned.append(jnp.concatenate([x * along + y * across for x, y in zip(merged, swapped)], axis=1))
    lagged = jnp.dot(jnp.concatenate(turned, axis=0), table_ref[...], precision=HI, preferred_element_type=F32)
    for quarter in range(4):
        for y in range(ROWS):
            at = quarter * ROWS * NBIN + y * NBIN
            out_ref[y * 4 + quarter] = lagged[at : at + NBIN]


def crossed(block, bit):
    return lax.ppermute(block, "lag", [(i, i ^ bit) for i in range(4)])


def body(traces, owner_map, pair_codes, pair_count):
    blk = lax.axis_index("row") * PLANE + lax.axis_index("plane")
    core = (lax.axis_index("lag") % 2).astype(jnp.int32).reshape(1)
    taps = jnp.asarray(filter_table())
    table = jnp.asarray(transform_table())

    history = lax.ppermute(traces[:, -TAPS:], "lag", [(i, i + 1) for i in range(3)])

    lists = call(
        list_kernel,
        shape((PLANE, LIST_ROWS, CB), jnp.int32),
        blk.astype(jnp.int32).reshape(1),
        pair_count,
        owner_map,
        pair_codes,
        smem=(0, 1, 2),
    )
    lists = lax.all_to_all(lists, "plane", 0, 0, tiled=True)

    spec = shape((CB, WIN), BF16)
    spectra1 = call(spectra_kernel, spec, traces[:, WIN - TAPS : WIN], traces[:, WIN:], taps, table)
    spectra0 = call(spectra_kernel, spec, history, traces[:, :WIN], taps, table)

    half = (CB // 2, NF)
    keep, send = call(power_kernel, (shape(half, F32), shape(half, BF16)), core, spectra0, spectra1, smem=(0,))
    send, lists = lax.optimization_barrier((send, lists))
    owners = lists[:, 4 * MEETINGS, :MEETINGS]
    chosen = call(chosen_kernel, shape((PLANE, MEETINGS, CB, CB), BF16), lists)
    chip = keep + crossed(send, 1).astype(F32)
    power = chip + crossed(chip.astype(BF16), 2).astype(F32)
    gain = lax.rsqrt(power + WATER)
    slabs = call(
        whiten_kernel, shape((PLANE, CB, CB), BF16), core, spectra0, spectra1, gain, crossed(gain, 1), smem=(0,)
    )
    group = lax.all_to_all(slabs, "plane", 0, 0, tiled=True)
    last, chosen = lax.optimization_barrier((group[PLANE - ROUNDS :], chosen))
    below = lax.ppermute(last, "row", [(i, i + 1) for i in range(ROWS - 1)])

    bins = jnp.asarray(bin_table())
    sums_shape = shape((ROWS * PLANE, NBIN, 2 * BAND), F32)
    sums = call(plane_kernel, sums_shape, owners, bins, chosen, group, smem=(0,))
    sums = call(below_kernel, sums_shape, owners, bins, chosen, group, below, sums, smem=(0,), aliases={5: 0})
    parts = lax.all_to_all(sums.reshape(PLANE, ROWS * NBIN, 2 * BAND), "plane", 0, 0, tiled=True)
    lagged = call(lag_kernel, shape((ROWS * 4, NBIN, LANES), F32), parts, jnp.asarray(inverse_table()))
    return jnp.sum(lax.all_to_all(lagged, ("row", "lag"), 0, 0, tiled=True), axis=0, keepdims=True)


def solution(mesh):
    split = Mesh(mesh.devices.reshape(ROWS, PLANE, 4), ("row", "plane", "lag"))
    owned = ("row", "plane")
    return jax.shard_map(
        body,
        mesh=split,
        in_specs=(P(owned, "lag"), P(None, owned), P(None, owned), P(None, owned)),
        out_specs=P(owned, None, "lag"),
        check_vma=False,
    )
```

time: 113 us -> 123 us (1.088)
  Pallas kernels: 12.2 us -> 35.3 us
  blocking collectives: 45.4 us -> 34.8 us
  waiting for transfers between devices: 24.2 us -> 13.8 us
  starting transfers between devices: 26.7 us -> 32.3 us
  local copies, waits for them, and re-layouts: 3.03 us -> 5.54 us
    pallas_call x9, Pallas kernels: 12.2 us -> 35.3 us  [call(): pl.pallas_call(kernel, out_shape=out_shape, in_specs=specs, out_specs=out...]
    ppermute x5 -> x1, waiting for transfers between devices: 18.9 us -> 0.01 us  [body(): below = lax.ppermute(last, 'row', [(i, i + 1) for i in range(ROWS - 1)])]
    all_to_all x0 -> x2, starting transfers between devices: none -> 16.6 us  [the longest x1 9.01 us: body(): lists = lax.all_to_all(lists, 'plane', 0, 0, tiled=True)]
    all_to_all x2, blocking collectives: 45.4 us -> 34.8 us  [the longest x1 21.2 us: body(): lax.all_to_all(lagged, ('row', 'lag'), 0, 0, tiled=True)]
    all_to_all x0 -> x2, waiting for transfers between devices: none -> 8.33 us  [the longest x1 8.33 us: body(): group = lax.all_to_all(slabs, 'plane', 0, 0, tiled=True)]
    ppermute x5 -> x1, starting transfers between devices: 10.8 us -> 3.21 us  [body(): below = lax.ppermute(last, 'row', [(i, i + 1) for i in range(ROWS - 1)])]
    ppermute x1, starting transfers between devices: 10.3 us -> 6.96 us  [body(): lax.ppermute(traces[:, -TAPS:], 'lag', [(i, i + 1) for i in range(3)])]
    unnamed x16 -> x12, local copies, waits for them, and re-layouts: 0.88 us -> 3.37 us
  transfers between devices with their start and end apart: 9 -> 7, of which waited for: 4 -> 4; matrix products, arithmetic and copies ran while one was open for 2% -> 2% of each run, Pallas kernels for 3% -> 23%
where the time goes in v2:
time: 123 us
  Pallas kernels  35.3 us (29%)
  blocking collectives  34.8 us (28%)
  starting transfers between devices  32.3 us (26%)
  waiting for transfers between devices  13.8 us (11%)
  local copies, waits for them, and re-layouts  5.54 us (5%)
    pallas_call x9, Pallas kernels, call(): pl.pallas_call(kernel, out_shape=out_shape, in_specs=specs, out_specs=out...  35.3 us
    all_to_all x1, blocking collectives, body(): lax.all_to_all(lagged, ('row', 'lag'), 0, 0, tiled=True)  21.2 us
    all_to_all x1, blocking collectives, body(): lax.all_to_all(sums.reshape(PLANE, ROWS * NBIN, 2 * BAND), 'plane', 0, 0,...  13.6 us
    all_to_all x1, starting transfers between devices, body(): lists = lax.all_to_all(lists, 'plane', 0, 0, tiled=True)  9.01 us
    all_to_all x1, waiting for transfers between devices, body(): group = lax.all_to_all(slabs, 'plane', 0, 0, tiled=True)  8.33 us
    all_to_all x1, starting transfers between devices, body(): group = lax.all_to_all(slabs, 'plane', 0, 0, tiled=True)  7.63 us
    ppermute x1, starting transfers between devices, body(): lax.ppermute(traces[:, -TAPS:], 'lag', [(i, i + 1) for i in range(3)])  6.96 us
    ppermute x3, starting transfers between devices, crossed(): return lax.ppermute(block, 'lag', [(i, i ^ bit) for i in range(4)])  5.53 us
  transfers between devices with their start and end apart: 7, of which 4 were waited for; matrix products, arithmetic and copies ran while one was open for 2% of the time, Pallas kernels for 23%

profile of v2, /device:TPU:1, one launch (start us, length us, event | category | flops | bytes accessed | tf_op | source)
XLA Modules:
  0.0 122.6 jit_solution(8612849772386303011)
XLA Ops:
  0.0 0.0 copy-start
  0.0 0.0 copy-start.3
  0.0 0.8 copy.11.owner_ref
  0.8 0.7 copy.10.count_ref
  1.6 0.0 copy-start.4
  1.6 0.7 copy-done.4
  2.3 1.4 %shard_map.85 = s32[16,24,128]{2,1,0:T(8,128)} custom-call(s32[1]{0:T(128)} %bitcast.1.blk_ref, s32[5,1]{1,0:T(8,128)S(1)} %copy.10.count_ref, s32[5,1]{1,0:T(8,128)S(1)} %copy.11.owner_ref, s32[5,512]{1,0:T(8,128)S(1)} %copy-done.4), custom_call_target="tpu_custom_call" | custom-call | tf_op jit(solution)/shard_map/pallas_call | solution.py:102
  3.7 9.0 %all-to-all-start = ((s32[16,24,128]{2,1,0:T(8,128)}), s32[16,24,128]{2,1,0:T(8,128)S(1)}, u32[]{:S(2)}, u32[]{:S(2)}) async-start(s32[16,24,128]{2,1,0:T(8,128)} %shard_map.85), calls=%async_computation | async-start | bytes 393216 | tf_op jit(solution)/shard_map/all_to_all | solution.py:289
  12.7 0.9 fusion.2
  13.6 7.0 %collective-permute-start = (f32[128,128]{1,0:T(8,128)S(1)}, f32[128,128]{1,0:T(8,128)S(1)}, u32[]{:S(2)}, u32[]{:S(2)}) collective-permute-start(f32[128,128]{1,0:T(8,128)S(1)} %get-tuple-element.20), channel_id=1, source_target_pairs={{0,1},{1,2},{2,3},{4,5},{5,6},{6,7},{8,9},{9,10},{10,11},{12,13},{... | collective-permute-start | bytes 196616 | tf_op jit(solution)/shard_map/ppermute | solution.py:278
  20.6 1.3 %fusion.1 = (f32[128,1024]{1,0:T(8,128)S(1)}, f32[128,1024]{1,0:T(8,128)S(1)}) fusion(f32[128,2048]{1,0:T(8,128)} %param.8), kind=kLoop, calls=%fused_computation.3 | loop fusion | bytes 2097152 | tf_op jit(solution)/shard_map/slice | solution.py:292
  21.8 0.0 copy-done
  21.8 0.0 copy-done.3
  21.9 1.8 %shard_map.83.s1_ref = bf16[128,1024]{1,0:T(8,128)(2,1)S(1)} custom-call(f32[128,128]{1,0:T(8,128)S(1)} %get-tuple-element.19.hist_ref, f32[128,1024]{1,0:T(8,128)S(1)} %get-tuple-element.17.x_ref, f32[256,128]{1,0:T(8,128)S(1)} %copy-done.3, bf16[512,1024]{1,0:T(8,128)(2,1)S(1)} %copy-done), custom_call_target="tpu_custom_call" | custom-call | tf_op jit(solution)/shard_map/pallas_call | solution.py:102
  23.7 0.0 collective-permute-done.hist_ref
  23.7 1.8 %shard_map.82.s0_ref = bf16[128,1024]{1,0:T(8,128)(2,1)S(1)} custom-call(f32[128,128]{1,0:T(8,128)S(1)} %collective-permute-done.hist_ref, f32[128,1024]{1,0:T(8,128)S(1)} %get-tuple-element.18.x_ref, f32[256,128]{1,0:T(8,128)S(1)} %copy-done.3, bf16[512,1024]{1,0:T(8,128)(2,1)S(1)} %copy-done), custom_call_target="tpu_custom_call" | custom-call | tf_op jit(solution)/shard_map/pallas_call | solution.py:102
  25.5 0.2 shard_map.84
  25.8 0.0 all-to-all-done.lists_ref
  25.8 0.1 collective-permute-start.1
  25.9 1.2 %collective-permute-done.1 = bf16[64,512]{1,0:T(8,128)(2,1)S(1)} collective-permute-done((bf16[64,512]{1,0:T(8,128)(2,1)S(1)}, bf16[64,512]{1,0:T(8,128)(2,1)S(1)}, u32[]{:S(2)}, u32[]{:S(2)}) %collective-permute-start.1) | collective-permute-done | bytes 65568 | tf_op jit(solution)/shard_map/ppermute | solution.py:269
  27.1 4.3 %collective-permute-start.2 = (bf16[64,512]{1,0:T(8,128)(2,1)S(1)}, bf16[64,512]{1,0:T(8,128)(2,1)S(1)}, u32[]{:S(2)}, u32[]{:S(2)}) collective-permute-start(bf16[64,512]{1,0:T(8,128)(2,1)S(1)} %fusion), channel_id=1, source_target_pairs={{0,2},{1,3},{2,0},{3,1},{4,6},{5,7},{6,4},{7,5},{8,10},{9,11},{10,... | collective-permute-start | bytes 196616 | tf_op jit(solution)/shard_map/ppermute | solution.py:269
  31.4 3.2 %collective-permute-done.2 = bf16[64,512]{1,0:T(8,128)(2,1)S(1)} collective-permute-done((bf16[64,512]{1,0:T(8,128)(2,1)S(1)}, bf16[64,512]{1,0:T(8,128)(2,1)S(1)}, u32[]{:S(2)}, u32[]{:S(2)}) %collective-permute-start.2) | collective-permute-done | bytes 65568 | tf_op jit(solution)/shard_map/ppermute | solution.py:269
  34.7 1.1 collective-permute-start.3
  35.9 1.0 collective-permute-done.3.other_ref
  36.8 1.0 shard_map.86
  37.8 7.6 %all-to-all-start.1 = ((bf16[16,128,128]{2,1,0:T(8,128)(2,1)}), bf16[16,128,128]{2,1,0:T(8,128)(2,1)S(1)}, u32[]{:S(2)}, u32[]{:S(2)}) async-start(bf16[16,128,128]{2,1,0:T(8,128)(2,1)} %shard_map.86), calls=%async_computation.1 | async-start | bytes 1048576 | tf_op jit(solution)/shard_map/all_to_all | solution.py:306
  45.4 5.8 %shard_map.87.chosen_ref = bf16[16,5,128,128]{3,2,1,0:T(8,128)(2,1)S(1)} custom-call(s32[16,24,128]{2,1,0:T(8,128)S(1)} %all-to-all-done.lists_ref), custom_call_target="tpu_custom_call" | custom-call | tf_op jit(solution)/shard_map/pallas_call | solution.py:102
  51.2 8.3 %all-to-all-done.1.group_ref = bf16[16,128,128]{2,1,0:T(8,128)(2,1)S(1)} async-done(((bf16[16,128,128]{2,1,0:T(8,128)(2,1)}), bf16[16,128,128]{2,1,0:T(8,128)(2,1)S(1)}, u32[]{:S(2)}, u32[]{:S(2)}) %all-to-all-start.1) | async-done | bytes 524320 | tf_op jit(solution)/shard_map/all_to_all | solution.py:306
  59.6 3.2 %collective-permute-start.4 = (bf16[4,128,128]{2,1,0:T(8,128)(2,1)S(1)}, bf16[4,128,128]{2,1,0:T(8,128)(2,1)S(1)}, u32[]{:S(2)}, u32[]{:S(2)}) collective-permute-start(bf16[4,128,128]{2,1,0:T(8,128)(2,1)S(1)} %slice.24), channel_id=1, source_target_pairs={{0,64},{64,128},{128,192},{1,65},{65,129},{129,193},{2,66},{66,130... | collective-permute-start | bytes 393224 | tf_op jit(solution)/shard_map/ppermute | solution.py:308
  62.8 0.0 copy-start.1
  62.8 1.1 copy-done.1
  63.9 19.1 %shard_map.88.sums_ref = f32[64,8,128]{2,1,0:T(8,128)S(1)} custom-call(s32[16,5]{1,0:T(8,128)S(1)} %bitcast.6, bf16[18,128,128]{2,1,0:T(8,128)(2,1)S(1)} %copy-done.1, bf16[16,5,128,128]{3,2,1,0:T(8,128)(2,1)S(1)} %shard_map.87.chosen_ref, bf16[16,128,128]{2,1,0:T(8,128)(2,1)S(1)} %all-to-all-done.1.group_ref), custom_call_target="tpu_custom_call" | custom-call | tf_op jit(solution)/shard_map/pallas_call | solution.py:102
  83.0 0.0 copy-start.2
  83.0 0.0 collective-permute-done.4.below_ref
  83.0 3.3 %shard_map.89 = f32[64,8,128]{2,1,0:T(8,128)S(1)} custom-call(s32[16,5]{1,0:T(8,128)S(1)} %bitcast.7, bf16[18,128,128]{2,1,0:T(8,128)(2,1)S(1)} %copy-done.1, bf16[16,5,128,128]{3,2,1,0:T(8,128)(2,1)S(1)} %shard_map.87.chosen_ref, bf16[16,128,128]{2,1,0:T(8,128)(2,1)S(1)} %all-to-all-done.1.group_ref, ...), custom_call_target="tpu_custom_call", output_to_operand_aliasing={{}: (5, {})} | custom-call | tf_op jit(solution)/shard_map/pallas_call | solution.py:102
  86.4 13.6 %all_to_all.20.parts_ref = f32[16,32,128]{2,1,0:T(8,128)S(1)} all-to-all(f32[16,32,128]{2,1,0:T(8,128)S(1)} %bitcast.5), channel_id=1, replica_groups=mesh['row'=4,'plane'=16,'lag'=4] {'plane'}, dimensions={0} | all-to-all | bytes 524288 | tf_op jit(solution)/shard_map/all_to_all | solution.py:314
  99.9 0.0 copy-done.2
  99.9 0.8 shard_map.90
  100.7 21.2 %all_to_all.21 = f32[16,8,256]{2,1,0:T(8,128)S(1)} all-to-all(f32[16,8,256]{2,1,0:T(8,128)S(1)} %shard_map.90), channel_id=1, replica_groups=mesh['row'=4,'plane'=16,'lag'=4] {'row','lag'}, dimensions={0} | all-to-all | bytes 262144 | tf_op jit(solution)/shard_map/all_to_all | solution.py:316
  121.9 0.6 reduce_sum.9
  (4 shorter events, 0.1 us)
Async XLA Ops:
  0.0 21.8 %copy-start = (bf16[512,1024]{1,0:T(8,128)(2,1)S(1)}, bf16[512,1024]{1,0:T(8,128)(2,1)}, u32[]{:S(2)}) copy-start(bf16[512,1024]{1,0:T(8,128)(2,1)} %constant.41.clone.table_ref) | copy-start | bytes 3145732
  0.0 21.8 %copy-start.3 = (f32[256,128]{1,0:T(8,128)S(1)}, f32[256,128]{1,0:T(8,128)}, u32[]{:S(2)}) copy-start(f32[256,128]{1,0:T(8,128)} %constant.40.clone.taps_ref) | copy-start | bytes 393220
  1.6 0.7 copy-start.4
  3.7 22.1 %all-to-all-start = ((s32[16,24,128]{2,1,0:T(8,128)}), s32[16,24,128]{2,1,0:T(8,128)S(1)}, u32[]{:S(2)}, u32[]{:S(2)}) async-start(s32[16,24,128]{2,1,0:T(8,128)} %shard_map.85), calls=%async_computation | async-start | bytes 393216 | tf_op jit(solution)/shard_map/all_to_all | solution.py:289
  13.6 10.1 %collective-permute-start = (f32[128,128]{1,0:T(8,128)S(1)}, f32[128,128]{1,0:T(8,128)S(1)}, u32[]{:S(2)}, u32[]{:S(2)}) collective-permute-start(f32[128,128]{1,0:T(8,128)S(1)} %get-tuple-element.20), channel_id=1, source_target_pairs={{0,1},{1,2},{2,3},{4,5},{5,6},{6,7},{8,9},{9,10},{10,11},{12,13},{... | collective-permute-start | bytes 196616 | tf_op jit(solution)/shard_map/ppermute | solution.py:278
  25.8 1.3 %collective-permute-start.1 = (bf16[64,512]{1,0:T(8,128)(2,1)S(1)}, bf16[64,512]{1,0:T(8,128)(2,1)S(1)}, u32[]{:S(2)}, u32[]{:S(2)}) collective-permute-start(bf16[64,512]{1,0:T(8,128)(2,1)S(1)} %get-tuple-element.14), channel_id=1, source_target_pairs={{0,1},{1,0},{2,3},{3,2},{4,5},{5,4},{6,7},{7,6},{8,9},{9,8},{10,11... | collective-permute-start | bytes 196616 | tf_op jit(solution)/shard_map/ppermute | solution.py:269
  27.1 7.5 %collective-permute-start.2 = (bf16[64,512]{1,0:T(8,128)(2,1)S(1)}, bf16[64,512]{1,0:T(8,128)(2,1)S(1)}, u32[]{:S(2)}, u32[]{:S(2)}) collective-permute-start(bf16[64,512]{1,0:T(8,128)(2,1)S(1)} %fusion), channel_id=1, source_target_pairs={{0,2},{1,3},{2,0},{3,1},{4,6},{5,7},{6,4},{7,5},{8,10},{9,11},{10,... | collective-permute-start | bytes 196616 | tf_op jit(solution)/shard_map/ppermute | solution.py:269
  34.7 2.1 %collective-permute-start.3 = (f32[64,512]{1,0:T(8,128)S(1)}, f32[64,512]{1,0:T(8,128)S(1)}, u32[]{:S(2)}, u32[]{:S(2)}) collective-permute-start(f32[64,512]{1,0:T(8,128)S(1)} %add_rsqrt_fusion.own_ref), channel_id=1, source_target_pairs={{0,1},{1,0},{2,3},{3,2},{4,5},{5,4},{6,7},{7,6},{8,9},{9,8},{10,11... | collective-permute-start | bytes 393224 | tf_op jit(solution)/shard_map/ppermute | solution.py:269
  37.8 21.8 %all-to-all-start.1 = ((bf16[16,128,128]{2,1,0:T(8,128)(2,1)}), bf16[16,128,128]{2,1,0:T(8,128)(2,1)S(1)}, u32[]{:S(2)}, u32[]{:S(2)}) async-start(bf16[16,128,128]{2,1,0:T(8,128)(2,1)} %shard_map.86), calls=%async_computation.1 | async-start | bytes 1048576 | tf_op jit(solution)/shard_map/all_to_all | solution.py:306
  59.6 23.4 %collective-permute-start.4 = (bf16[4,128,128]{2,1,0:T(8,128)(2,1)S(1)}, bf16[4,128,128]{2,1,0:T(8,128)(2,1)S(1)}, u32[]{:S(2)}, u32[]{:S(2)}) collective-permute-start(bf16[4,128,128]{2,1,0:T(8,128)(2,1)S(1)} %slice.24), channel_id=1, source_target_pairs={{0,64},{64,128},{128,192},{1,65},{65,129},{129,193},{2,66},{66,130... | collective-permute-start | bytes 393224 | tf_op jit(solution)/shard_map/ppermute | solution.py:308
  62.8 1.1 copy-start.1
  83.0 16.9 %copy-start.2 = (f32[1024,256]{1,0:T(8,128)S(1)}, f32[1024,256]{1,0:T(8,128)}, u32[]{:S(2)}) copy-start(f32[1024,256]{1,0:T(8,128)} %constant.43.clone.table_ref) | copy-start | bytes 3145732

commit v3 on v2

--- a/solution.py
+++ b/solution.py
@@ -34,7 +34,7 @@
 F32 = jnp.float32
 BF16 = jnp.bfloat16
 HI = lax.Precision.HIGHEST
-VMEM_LIMIT = 48 * 1024 * 1024
+VMEM_LIMIT = 16 * 1024 * 1024
 
 
 def level_rows(o):
@@ -52,8 +52,8 @@
 
 
 LEVELS = tuple(level_rows(o) for o in range(MEETINGS))
-STARTS = tuple(sum(len(v) for v in LEVELS[:o]) for o in range(MEETINGS))
-LEVEL_COUNT = sum(len(v) for v in LEVELS)
+SPANS = tuple((o, k, lo, hi) for o in range(MEETINGS) for k, lo, hi in LEVELS[o])
+SPAN_ROWS = sum(hi - lo for _, _, lo, hi in SPANS)
 
 
 def filter_table():
@@ -84,15 +84,7 @@
     return (weight * np.where(is_imag[:, None], -np.sin(angle), np.cos(angle))).astype(np.float32)
 
 
-def bin_table():
-    spread = np.arange(CB)[None, :] - np.arange(CB)[:, None]
-    tables = [
-        ((CB * o + spread) // BINW == k).astype(jnp.bfloat16) for o in range(MEETINGS) for k, _, _ in LEVELS[o]
-    ]
-    return np.stack(tables)
-
-
-def call(kernel, out_shape, *args, smem=(), aliases=None):
+def call(kernel, out_shape, *args, smem=(), aliases=None, scratch=()):
     specs = [
         pl.BlockSpec(memory_space=pltpu.SMEM) if n in smem else pl.BlockSpec(memory_space=pltpu.VMEM)
         for n in range(len(args))
@@ -105,6 +97,7 @@
         in_specs=specs,
         out_specs=out_specs,
         input_output_aliases=aliases or {},
+        scratch_shapes=list(scratch),
         compiler_params=pltpu.CompilerParams(vmem_limit_bytes=VMEM_LIMIT),
     )(*args)
 
@@ -183,68 +176,88 @@
         out_ref[p] = block
 
 
-def chosen_kernel(lists_ref, out_ref):
+def chosen_kernel(lists_ref, low_ref, high_ref):
     row = lax.broadcasted_iota(jnp.int32, (CB, PCAP), 0)
 
-    def one(p, carry):
+    def fill(p, ref, at):
         for o in range(MEETINGS):
             pieces = [lists_ref[p, o * 4 + n : o * 4 + n + 1, :] for n in range(4)]
             codes = jnp.concatenate(pieces, axis=1)
             pick_first = jnp.where(row == (codes >> 7), 1.0, 0.0).astype(BF16)
             pick_second = jnp.where(row == (codes & (CB - 1)), 1.0, 0.0).astype(BF16)
             chosen = lax.dot_general(pick_first, pick_second, (((1,), (1,)), ((), ())), preferred_element_type=F32)
-            out_ref[p, o] = chosen.astype(BF16)
+            ref[at, o] = chosen.astype(BF16)
+
+    for p in range(ROUNDS):
+        fill(p, low_ref, p)
+
+    def one(p, carry):
+        fill(p, high_ref, p - ROUNDS)
         return carry
 
-    lax.fori_loop(0, PLANE, one, 0)
-
-
-def meet(out_ref, bins_ref, chosen, a_block, b_block, o, owner):
+    lax.fori_loop(ROUNDS, PLANE, one, 0)
+
+
+def fill_bins(bins_ref):
+    spread = lax.broadcasted_iota(jnp.int32, (CB, CB), 1) - lax.broadcasted_iota(jnp.int32, (CB, CB), 0)
+    at = 0
+    for o, k, lo, hi in SPANS:
+        distance = spread[lo:hi] + CB * o
+        inside = (distance >= BINW * k) & (distance < BINW * (k + 1))
+        bins_ref[at : at + hi - lo, :] = jnp.where(inside, 1.0, 0.0).astype(BF16)
+        at += hi - lo
+
+
+def meet(out_ref, owner_ref, bins_ref, chosen_ref, at_block, block, partners, p):
     low = low_lanes()
     sign = jnp.where(low, -1.0, 1.0)
-    weights = jnp.concatenate(
-        [chosen[lo:hi] * bins_ref[STARTS[o] + n, lo:hi, :] for n, (_, lo, hi) in enumerate(LEVELS[o])], axis=0
-    )
-    mixed = jnp.dot(weights, b_block, preferred_element_type=F32)
-    straight = a_block.astype(F32)
-    swapped = pltpu.roll(straight, BAND, 1) * sign
     row_id = lax.broadcasted_iota(jnp.int32, (NBIN, 2 * BAND), 0)
-    real = jnp.zeros((NBIN, 2 * BAND), F32)
-    imag = jnp.zeros((NBIN, 2 * BAND), F32)
     at = 0
-    for k, lo, hi in LEVELS[o]:
-        part = mixed[at : at + hi - lo]
+    pieces = []
+    for o, _, lo, hi in SPANS:
+        pieces.append(chosen_ref[at_block, o, lo:hi, :] * bins_ref[at : at + hi - lo, :])
         at += hi - lo
-        dims = ((hi - lo) // 8, 8, 2 * BAND)
-        along = jnp.sum(jnp.sum((straight[lo:hi] * part).reshape(dims), axis=0), axis=0, keepdims=True)
-        across = jnp.sum(jnp.sum((swapped[lo:hi] * part).reshape(dims), axis=0), axis=0, keepdims=True)
-        real = jnp.where(row_id == k, along, real)
-        imag = jnp.where(row_id == k, across, imag)
-    terms = jnp.where(low, real + pltpu.roll(real, BAND, 1), imag + pltpu.roll(imag, BAND, 1))
-    spot = (owner % PLANE) * ROWS + owner // PLANE
-    out_ref[spot] = out_ref[spot] + terms
-
-
-def plane_kernel(owner_ref, bins_ref, chosen_ref, group_ref, out_ref):
+    mixed = jnp.dot(jnp.concatenate(pieces, axis=0), block, preferred_element_type=F32)
+    at = 0
+    found = []
+    for o in range(MEETINGS):
+        straight = partners[o].astype(F32)
+        swapped = pltpu.roll(straight, BAND, 1) * sign
+        real = jnp.zeros((NBIN, 2 * BAND), F32)
+        imag = jnp.zeros((NBIN, 2 * BAND), F32)
+        for k, lo, hi in LEVELS[o]:
+            part = mixed[at : at + hi - lo]
+            at += hi - lo
+            dims = ((hi - lo) // 8, 8, 2 * BAND)
+            along = jnp.sum(jnp.sum((straight[lo:hi] * part).reshape(dims), axis=0), axis=0, keepdims=True)
+            across = jnp.sum(jnp.sum((swapped[lo:hi] * part).reshape(dims), axis=0), axis=0, keepdims=True)
+            real = jnp.where(row_id == k, along, real)
+            imag = jnp.where(row_id == k, across, imag)
+        found.append(jnp.where(low, real + pltpu.roll(real, BAND, 1), imag + pltpu.roll(imag, BAND, 1)))
+    for o in range(MEETINGS):
+        owner = owner_ref[p, o]
+        spot = (owner % PLANE) * ROWS + owner // PLANE
+        out_ref[spot] = out_ref[spot] + found[o]
+
+
+def plane_kernel(owner_ref, chosen_ref, group_ref, out_ref, bins_ref):
     out_ref[...] = jnp.zeros(out_ref.shape, F32)
-    for o in range(MEETINGS):
-
-        def one(p, carry, o=o):
-            meet(out_ref, bins_ref, chosen_ref[p, o], group_ref[p - o], group_ref[p], o, owner_ref[p, o])
-            return carry
-
-        lax.fori_loop(o, PLANE, one, 0)
-
-
-def below_kernel(owner_ref, bins_ref, chosen_ref, group_ref, below_ref, sums_ref, out_ref):
+    fill_bins(bins_ref)
+
+    def one(p, carry):
+        partners = [group_ref[p - o] for o in range(MEETINGS)]
+        meet(out_ref, owner_ref, bins_ref, chosen_ref, p - ROUNDS, group_ref[p], partners, p)
+        return carry
+
+    lax.fori_loop(ROUNDS, PLANE, one, 0)
+
+
+def below_kernel(owner_ref, chosen_ref, group_ref, below_ref, sums_ref, out_ref, bins_ref):
     out_ref[...] = sums_ref[...]
-    for o in range(1, MEETINGS):
-
-        def one(p, carry, o=o):
-            meet(out_ref, bins_ref, chosen_ref[p, o], below_ref[p - o + ROUNDS], group_ref[p], o, owner_ref[p, o])
-            return carry
-
-        lax.fori_loop(0, o, one, 0)
+    fill_bins(bins_ref)
+    for p in range(ROUNDS):
+        partners = [group_ref[p - o] if p >= o else below_ref[p - o + ROUNDS] for o in range(MEETINGS)]
+        meet(out_ref, owner_ref, bins_ref, chosen_ref, p, group_ref[p], partners, p)
 
 
 def lag_kernel(parts_ref, table_ref, out_ref):
@@ -277,40 +290,52 @@
 
     history = lax.ppermute(traces[:, -TAPS:], "lag", [(i, i + 1) for i in range(3)])
 
+    spec = shape((CB, WIN), BF16)
+    spectra1 = call(spectra_kernel, spec, traces[:, WIN - TAPS : WIN], traces[:, WIN:], taps, table)
+    spectra0 = call(spectra_kernel, spec, history, traces[:, :WIN], taps, table)
+
+    half = (CB // 2, NF)
+    keep, send = call(power_kernel, (shape(half, F32), shape(half, BF16)), core, spectra0, spectra1, smem=(0,))
+    chip = keep + crossed(send, 1).astype(F32)
+    chip, place = lax.optimization_barrier((chip, blk.astype(jnp.int32).reshape(1)))
     lists = call(
         list_kernel,
         shape((PLANE, LIST_ROWS, CB), jnp.int32),
-        blk.astype(jnp.int32).reshape(1),
+        place,
         pair_count,
         owner_map,
         pair_codes,
         smem=(0, 1, 2),
     )
     lists = lax.all_to_all(lists, "plane", 0, 0, tiled=True)
-
-    spec = shape((CB, WIN), BF16)
-    spectra1 = call(spectra_kernel, spec, traces[:, WIN - TAPS : WIN], traces[:, WIN:], taps, table)
-    spectra0 = call(spectra_kernel, spec, history, traces[:, :WIN], taps, table)
-
-    half = (CB // 2, NF)
-    keep, send = call(power_kernel, (shape(half, F32), shape(half, BF16)), core, spectra0, spectra1, smem=(0,))
-    send, lists = lax.optimization_barrier((send, lists))
-    owners = lists[:, 4 * MEETINGS, :MEETINGS]
-    chosen = call(chosen_kernel, shape((PLANE, MEETINGS, CB, CB), BF16), lists)
-    chip = keep + crossed(send, 1).astype(F32)
     power = chip + crossed(chip.astype(BF16), 2).astype(F32)
     gain = lax.rsqrt(power + WATER)
     slabs = call(
         whiten_kernel, shape((PLANE, CB, CB), BF16), core, spectra0, spectra1, gain, crossed(gain, 1), smem=(0,)
     )
+    slabs, lists = lax.optimization_barrier((slabs, lists))
+    owners = lists[:, 4 * MEETINGS, :MEETINGS]
+    halves = tuple(shape((n, MEETINGS, CB, CB), BF16) for n in (ROUNDS, PLANE - ROUNDS))
+    chosen_low, chosen_high = call(chosen_kernel, halves, lists)
     group = lax.all_to_all(slabs, "plane", 0, 0, tiled=True)
-    last, chosen = lax.optimization_barrier((group[PLANE - ROUNDS :], chosen))
+    last, chosen_low, chosen_high = lax.optimization_barrier((group[PLANE - ROUNDS :], chosen_low, chosen_high))
     below = lax.ppermute(last, "row", [(i, i + 1) for i in range(ROWS - 1)])
 
-    bins = jnp.asarray(bin_table())
     sums_shape = shape((ROWS * PLANE, NBIN, 2 * BAND), F32)
-    sums = call(plane_kernel, sums_shape, owners, bins, chosen, group, smem=(0,))
-    sums = call(below_kernel, sums_shape, owners, bins, chosen, group, below, sums, smem=(0,), aliases={5: 0})
+    bins = pltpu.VMEM((SPAN_ROWS, CB), BF16)
+    sums = call(plane_kernel, sums_shape, owners, chosen_high, group, smem=(0,), scratch=(bins,))
+    sums = call(
+        below_kernel,
+        sums_shape,
+        owners,
+        chosen_low,
+        group,
+        below,
+        sums,
+        smem=(0,),
+        aliases={4: 0},
+        scratch=(bins,),
+    )
     parts = lax.all_to_all(sums.reshape(PLANE, ROWS * NBIN, 2 * BAND), "plane", 0, 0, tiled=True)
     lagged = call(lag_kernel, shape((ROWS * 4, NBIN, LANES), F32), parts, jnp.asarray(inverse_table()))
     return jnp.sum(lax.all_to_all(lagged, ("row", "lag"), 0, 0, tiled=True), axis=0, keepdims=True)

time: 123 us -> 101 us (0.82)
  Pallas kernels: 35.3 us -> 20.2 us
  starting transfers between devices: 32.3 us -> 28.6 us
  local copies, waits for them, and re-layouts: 5.54 us -> 2.49 us
  blocking collectives: 34.8 us -> 32.4 us
  waiting for transfers between devices: 13.8 us -> 15.9 us
    pallas_call x9, Pallas kernels: 35.3 us -> 20.2 us  [call(): pl.pallas_call(kernel, out_shape=out_shape, in_specs=specs, out_specs=out...]
    all_to_all x1, waiting for transfers between devices: 0.01 us -> 5.45 us  [body(): lists = lax.all_to_all(lists, 'plane', 0, 0, tiled=True)]
    all_to_all x1, starting transfers between devices: 9.01 us -> 5.49 us  [body(): lists = lax.all_to_all(lists, 'plane', 0, 0, tiled=True)]
    all_to_all x1, starting transfers between devices: 7.63 us -> 4.33 us  [body(): group = lax.all_to_all(slabs, 'plane', 0, 0, tiled=True)]
    ppermute x3, waiting for transfers between devices: 5.48 us -> 2.22 us  [crossed(): return lax.ppermute(block, 'lag', [(i, i ^ bit) for i in range(4)])]
    ppermute x1, starting transfers between devices: 6.96 us -> 10.2 us  [body(): lax.ppermute(traces[:, -TAPS:], 'lag', [(i, i + 1) for i in range(3)])]
    unnamed x12 -> x14, local copies, waits for them, and re-layouts: 3.37 us -> 0.22 us
    all_to_all x1, blocking collectives: 21.2 us -> 18.3 us  [body(): lax.all_to_all(lagged, ('row', 'lag'), 0, 0, tiled=True)]
  transfers between devices with their start and end apart: 7 -> 7, of which waited for: 4 -> 4; matrix products, arithmetic and copies ran while one was open for 2% -> 1% of each run, Pallas kernels for 23% -> 15%
where the time goes in v3:
time: 101 us; the launch traced here: 100 us
  blocking collectives  32.4 us (32%)
  starting transfers between devices  28.6 us (28%)
  Pallas kernels  20.2 us (20%)
  waiting for transfers between devices  15.9 us (16%)
  local copies, waits for them, and re-layouts  2.49 us (2%)
    pallas_call x9, Pallas kernels, call(): pl.pallas_call(kernel, out_shape=out_shape, in_specs=specs, out_specs=out...  20.2 us
    all_to_all x1, blocking collectives, body(): lax.all_to_all(lagged, ('row', 'lag'), 0, 0, tiled=True)  18.3 us
    all_to_all x1, blocking collectives, body(): lax.all_to_all(sums.reshape(PLANE, ROWS * NBIN, 2 * BAND), 'plane', 0, 0,...  14.1 us
    ppermute x1, starting transfers between devices, body(): lax.ppermute(traces[:, -TAPS:], 'lag', [(i, i + 1) for i in range(3)])  10.2 us
    all_to_all x1, waiting for transfers between devices, body(): group = lax.all_to_all(slabs, 'plane', 0, 0, tiled=True)  8.25 us
    all_to_all x1, starting transfers between devices, body(): lists = lax.all_to_all(lists, 'plane', 0, 0, tiled=True)  5.49 us
    all_to_all x1, waiting for transfers between devices, body(): lists = lax.all_to_all(lists, 'plane', 0, 0, tiled=True)  5.45 us
    ppermute x3, starting transfers between devices, crossed(): return lax.ppermute(block, 'lag', [(i, i ^ bit) for i in range(4)])  5.33 us
  transfers between devices with their start and end apart: 7, of which 4 were waited for; matrix products, arithmetic and copies ran while one was open for 1% of the time, Pallas kernels for 15%

profile of v3, /device:TPU:1, one launch (start us, length us, event | category | flops | bytes accessed | tf_op | source)
XLA Modules:
  0.0 100.4 jit_solution(2431861370608855493)
XLA Ops:
  0.0 0.0 copy-start
  0.0 0.0 copy-start.2
  0.0 1.0 fusion.1
  1.0 10.2 %collective-permute-start = (f32[128,128]{1,0:T(8,128)S(1)}, f32[128,128]{1,0:T(8,128)S(1)}, u32[]{:S(2)}, u32[]{:S(2)}) collective-permute-start(f32[128,128]{1,0:T(8,128)S(1)} %get-tuple-element.30), channel_id=1, source_target_pairs={{0,1},{1,2},{2,3},{4,5},{5,6},{6,7},{8,9},{9,10},{10,11},{12,13},{... | collective-permute-start | bytes 196616 | tf_op jit(solution)/shard_map/ppermute | solution.py:291
  11.2 1.3 %fusion = (f32[128,1024]{1,0:T(8,128)S(1)}, f32[128,1024]{1,0:T(8,128)S(1)}) fusion(f32[128,2048]{1,0:T(8,128)} %param.7), kind=kLoop, calls=%fused_computation.2 | loop fusion | bytes 2097152 | tf_op jit(solution)/shard_map/slice | solution.py:294
  12.5 0.0 copy-done
  12.5 0.0 copy-done.2
  12.5 1.8 %shard_map.74.s1_ref = bf16[128,1024]{1,0:T(8,128)(2,1)S(1)} custom-call(f32[128,128]{1,0:T(8,128)S(1)} %get-tuple-element.29.hist_ref, f32[128,1024]{1,0:T(8,128)S(1)} %get-tuple-element.27.x_ref, f32[256,128]{1,0:T(8,128)S(1)} %copy-done.2, bf16[512,1024]{1,0:T(8,128)(2,1)S(1)} %copy-done), custom_call_target="tpu_custom_call" | custom-call | tf_op jit(solution)/shard_map/pallas_call | solution.py:94
  14.3 0.0 copy-start.4
  14.4 0.0 copy-start.5
  14.4 0.0 copy-start.3
  14.4 0.0 collective-permute-done.hist_ref
  14.4 1.8 %shard_map.73.s0_ref = bf16[128,1024]{1,0:T(8,128)(2,1)S(1)} custom-call(f32[128,128]{1,0:T(8,128)S(1)} %collective-permute-done.hist_ref, f32[128,1024]{1,0:T(8,128)S(1)} %get-tuple-element.28.x_ref, f32[256,128]{1,0:T(8,128)S(1)} %copy-done.2, bf16[512,1024]{1,0:T(8,128)(2,1)S(1)} %copy-done), custom_call_target="tpu_custom_call" | custom-call | tf_op jit(solution)/shard_map/pallas_call | solution.py:94
  16.2 0.2 shard_map.75
  16.4 0.1 collective-permute-start.1
  16.6 1.2 %collective-permute-done.1 = bf16[64,512]{1,0:T(8,128)(2,1)S(1)} collective-permute-done((bf16[64,512]{1,0:T(8,128)(2,1)S(1)}, bf16[64,512]{1,0:T(8,128)(2,1)S(1)}, u32[]{:S(2)}, u32[]{:S(2)}) %collective-permute-start.1) | collective-permute-done | bytes 65568 | tf_op jit(solution)/shard_map/ppermute | solution.py:282
  17.8 4.2 %collective-permute-start.2 = (bf16[64,512]{1,0:T(8,128)(2,1)S(1)}, bf16[64,512]{1,0:T(8,128)(2,1)S(1)}, u32[]{:S(2)}, u32[]{:S(2)}) collective-permute-start(bf16[64,512]{1,0:T(8,128)(2,1)S(1)} %convert_element_type.10), channel_id=1, source_target_pairs={{0,2},{1,3},{2,0},{3,1},{4,6},{5,7},{6,4},{7,5},{8,10},{9,11},{10,... | collective-permute-start | bytes 196616 | tf_op jit(solution)/shard_map/ppermute | solution.py:282
  22.1 0.0 copy-done.4
  22.1 0.1 copy.10.owner_ref
  22.2 0.0 copy-done.5
  22.2 0.1 copy.9.count_ref
  22.2 0.0 copy-done.3
  22.2 1.4 %shard_map.77 = s32[16,24,128]{2,1,0:T(8,128)} custom-call(s32[1]{0:T(128)} %bitcast.1.blk_ref, s32[5,1]{1,0:T(8,128)S(1)} %copy.9.count_ref, s32[5,1]{1,0:T(8,128)S(1)} %copy.10.owner_ref, s32[5,512]{1,0:T(8,128)S(1)} %copy-done.3), custom_call_target="tpu_custom_call" | custom-call | tf_op jit(solution)/shard_map/pallas_call | solution.py:94
  23.6 5.5 %all-to-all-start = ((s32[16,24,128]{2,1,0:T(8,128)}), s32[16,24,128]{2,1,0:T(8,128)S(1)}, u32[]{:S(2)}, u32[]{:S(2)}) async-start(s32[16,24,128]{2,1,0:T(8,128)} %shard_map.77), calls=%async_computation | async-start | bytes 393216 | tf_op jit(solution)/shard_map/all_to_all | solution.py:310
  29.1 0.0 collective-permute-done.2
  29.1 1.0 collective-permute-start.3
  30.1 1.0 collective-permute-done.3.other_ref
  31.1 1.0 shard_map.76
  32.1 5.5 %all-to-all-done.lists_ref = s32[16,24,128]{2,1,0:T(8,128)S(1)} async-done(((s32[16,24,128]{2,1,0:T(8,128)}), s32[16,24,128]{2,1,0:T(8,128)S(1)}, u32[]{:S(2)}, u32[]{:S(2)}) %all-to-all-start) | async-done | bytes 196640 | tf_op jit(solution)/shard_map/all_to_all | solution.py:310
  37.6 4.3 %all-to-all-start.1 = ((bf16[16,128,128]{2,1,0:T(8,128)(2,1)}), bf16[16,128,128]{2,1,0:T(8,128)(2,1)S(1)}, u32[]{:S(2)}, u32[]{:S(2)}) async-start(bf16[16,128,128]{2,1,0:T(8,128)(2,1)} %shard_map.76), calls=%async_computation.1 | async-start | bytes 1048576 | tf_op jit(solution)/shard_map/all_to_all | solution.py:320
  41.9 5.3 %shard_map.78 = (bf16[4,5,128,128]{3,2,1,0:T(8,128)(2,1)S(1)}, bf16[12,5,128,128]{3,2,1,0:T(8,128)(2,1)S(1)}) custom-call(s32[16,24,128]{2,1,0:T(8,128)S(1)} %all-to-all-done.lists_ref), custom_call_target="tpu_custom_call" | custom-call | tf_op jit(solution)/shard_map/pallas_call | solution.py:94
  47.2 8.2 %all-to-all-done.1.group_ref = bf16[16,128,128]{2,1,0:T(8,128)(2,1)S(1)} async-done(((bf16[16,128,128]{2,1,0:T(8,128)(2,1)}), bf16[16,128,128]{2,1,0:T(8,128)(2,1)S(1)}, u32[]{:S(2)}, u32[]{:S(2)}) %all-to-all-start.1) | async-done | bytes 524320 | tf_op jit(solution)/shard_map/all_to_all | solution.py:320
  55.4 3.2 %collective-permute-start.4 = (bf16[4,128,128]{2,1,0:T(8,128)(2,1)S(1)}, bf16[4,128,128]{2,1,0:T(8,128)(2,1)S(1)}, u32[]{:S(2)}, u32[]{:S(2)}) collective-permute-start(bf16[4,128,128]{2,1,0:T(8,128)(2,1)S(1)} %slice.24), channel_id=1, source_target_pairs={{0,64},{64,128},{128,192},{1,65},{65,129},{129,193},{2,66},{66,130... | collective-permute-start | bytes 393224 | tf_op jit(solution)/shard_map/ppermute | solution.py:322
  58.7 0.0 copy-start.1
  58.7 6.0 %shard_map.79.sums_ref = f32[64,8,128]{2,1,0:T(8,128)S(1)} custom-call(s32[16,5]{1,0:T(8,128)S(1)} %bitcast.6, bf16[12,5,128,128]{3,2,1,0:T(8,128)(2,1)S(1)} %get-tuple-element.26.chosen_ref, bf16[16,128,128]{2,1,0:T(8,128)(2,1)S(1)} %all-to-all-done.1.group_ref), custom_call_target="tpu_custom_call" | custom-call | tf_op jit(solution)/shard_map/pallas_call | solution.py:94
  64.7 0.0 collective-permute-done.4.below_ref
  64.7 1.9 %shard_map.80 = f32[64,8,128]{2,1,0:T(8,128)S(1)} custom-call(s32[16,5]{1,0:T(8,128)S(1)} %bitcast.7, bf16[4,5,128,128]{3,2,1,0:T(8,128)(2,1)S(1)} %get-tuple-element.24.chosen_ref, bf16[16,128,128]{2,1,0:T(8,128)(2,1)S(1)} %all-to-all-done.1.group_ref, bf16[4,128,128]{2,1,0:T(8,128)(2,1)S(1)} %collective-permute-done.4.below_ref, ...), custom_call_target="tpu_custom_call", output_to_operand_aliasing={{}: (4, {})} | custom-call | tf_op jit(solution)/shard_map/pallas_call | solution.py:94
  66.6 14.1 %all_to_all.20.parts_ref = f32[16,32,128]{2,1,0:T(8,128)S(1)} all-to-all(f32[16,32,128]{2,1,0:T(8,128)S(1)} %bitcast.5), channel_id=1, replica_groups=mesh['row'=4,'plane'=16,'lag'=4] {'plane'}, dimensions={0} | all-to-all | bytes 524288 | tf_op jit(solution)/shard_map/all_to_all | solution.py:339
  80.7 0.0 copy-done.1
  80.7 0.8 shard_map.81
  81.6 18.3 %all_to_all.21 = f32[16,8,256]{2,1,0:T(8,128)S(1)} all-to-all(f32[16,8,256]{2,1,0:T(8,128)S(1)} %shard_map.81), channel_id=1, replica_groups=mesh['row'=4,'plane'=16,'lag'=4] {'row','lag'}, dimensions={0} | all-to-all | bytes 262144 | tf_op jit(solution)/shard_map/all_to_all | solution.py:341
  99.8 0.6 reduce_sum.9
  (5 shorter events, 0.1 us)
Async XLA Ops:
  0.0 12.5 %copy-start = (bf16[512,1024]{1,0:T(8,128)(2,1)S(1)}, bf16[512,1024]{1,0:T(8,128)(2,1)}, u32[]{:S(2)}) copy-start(bf16[512,1024]{1,0:T(8,128)(2,1)} %constant.39.clone.table_ref) | copy-start | bytes 3145732
  0.0 12.5 %copy-start.2 = (f32[256,128]{1,0:T(8,128)S(1)}, f32[256,128]{1,0:T(8,128)}, u32[]{:S(2)}) copy-start(f32[256,128]{1,0:T(8,128)} %constant.38.clone.taps_ref) | copy-start | bytes 393220
  1.0 13.4 %collective-permute-start = (f32[128,128]{1,0:T(8,128)S(1)}, f32[128,128]{1,0:T(8,128)S(1)}, u32[]{:S(2)}, u32[]{:S(2)}) collective-permute-start(f32[128,128]{1,0:T(8,128)S(1)} %get-tuple-element.30), channel_id=1, source_target_pairs={{0,1},{1,2},{2,3},{4,5},{5,6},{6,7},{8,9},{9,10},{10,11},{12,13},{... | collective-permute-start | bytes 196616 | tf_op jit(solution)/shard_map/ppermute | solution.py:291
  14.3 7.7 %copy-start.4 = (s32[5,1]{0,1:T(1,128)S(1)}, s32[5,1]{0,1:T(1,128)}, u32[]{:S(2)}) copy-start(s32[5,1]{0,1:T(1,128)} %param.8) | copy-start | bytes 64
  14.4 7.8 %copy-start.5 = (s32[5,1]{0,1:T(1,128)S(1)}, s32[5,1]{0,1:T(1,128)}, u32[]{:S(2)}) copy-start(s32[5,1]{0,1:T(1,128)} %param.10) | copy-start | bytes 64
  14.4 7.9 %copy-start.3 = (s32[5,512]{1,0:T(8,128)S(1)}, s32[5,512]{1,0:T(8,128)}, u32[]{:S(2)}) copy-start(s32[5,512]{1,0:T(8,128)} %codes_ref.1) | copy-start | bytes 30724
  16.4 1.3 %collective-permute-start.1 = (bf16[64,512]{1,0:T(8,128)(2,1)S(1)}, bf16[64,512]{1,0:T(8,128)(2,1)S(1)}, u32[]{:S(2)}, u32[]{:S(2)}) collective-permute-start(bf16[64,512]{1,0:T(8,128)(2,1)S(1)} %get-tuple-element.17), channel_id=1, source_target_pairs={{0,1},{1,0},{2,3},{3,2},{4,5},{5,4},{6,7},{7,6},{8,9},{9,8},{10,11... | collective-permute-start | bytes 196616 | tf_op jit(solution)/shard_map/ppermute | solution.py:282
  17.8 11.3 %collective-permute-start.2 = (bf16[64,512]{1,0:T(8,128)(2,1)S(1)}, bf16[64,512]{1,0:T(8,128)(2,1)S(1)}, u32[]{:S(2)}, u32[]{:S(2)}) collective-permute-start(bf16[64,512]{1,0:T(8,128)(2,1)S(1)} %convert_element_type.10), channel_id=1, source_target_pairs={{0,2},{1,3},{2,0},{3,1},{4,6},{5,7},{6,4},{7,5},{8,10},{9,11},{10,... | collective-permute-start | bytes 196616 | tf_op jit(solution)/shard_map/ppermute | solution.py:282
  23.6 14.0 %all-to-all-start = ((s32[16,24,128]{2,1,0:T(8,128)}), s32[16,24,128]{2,1,0:T(8,128)S(1)}, u32[]{:S(2)}, u32[]{:S(2)}) async-start(s32[16,24,128]{2,1,0:T(8,128)} %shard_map.77), calls=%async_computation | async-start | bytes 393216 | tf_op jit(solution)/shard_map/all_to_all | solution.py:310
  29.1 2.0 %collective-permute-start.3 = (f32[64,512]{1,0:T(8,128)S(1)}, f32[64,512]{1,0:T(8,128)S(1)}, u32[]{:S(2)}, u32[]{:S(2)}) collective-permute-start(f32[64,512]{1,0:T(8,128)S(1)} %add_rsqrt_fusion.own_ref), channel_id=1, source_target_pairs={{0,1},{1,0},{2,3},{3,2},{4,5},{5,4},{6,7},{7,6},{8,9},{9,8},{10,11... | collective-permute-start | bytes 393224 | tf_op jit(solution)/shard_map/ppermute | solution.py:282
  37.6 17.9 %all-to-all-start.1 = ((bf16[16,128,128]{2,1,0:T(8,128)(2,1)}), bf16[16,128,128]{2,1,0:T(8,128)(2,1)S(1)}, u32[]{:S(2)}, u32[]{:S(2)}) async-start(bf16[16,128,128]{2,1,0:T(8,128)(2,1)} %shard_map.76), calls=%async_computation.1 | async-start | bytes 1048576 | tf_op jit(solution)/shard_map/all_to_all | solution.py:320
  55.4 9.2 %collective-permute-start.4 = (bf16[4,128,128]{2,1,0:T(8,128)(2,1)S(1)}, bf16[4,128,128]{2,1,0:T(8,128)(2,1)S(1)}, u32[]{:S(2)}, u32[]{:S(2)}) collective-permute-start(bf16[4,128,128]{2,1,0:T(8,128)(2,1)S(1)} %slice.24), channel_id=1, source_target_pairs={{0,64},{64,128},{128,192},{1,65},{65,129},{129,193},{2,66},{66,130... | collective-permute-start | bytes 393224 | tf_op jit(solution)/shard_map/ppermute | solution.py:322
  58.7 22.1 %copy-start.1 = (f32[1024,256]{1,0:T(8,128)S(1)}, f32[1024,256]{1,0:T(8,128)}, u32[]{:S(2)}) copy-start(f32[1024,256]{1,0:T(8,128)} %constant.40.clone.table_ref) | copy-start | bytes 3145732

commit v4 on v3

v4 whole, which is shorter than its diff:
```python
import math

import jax
import jax.numpy as jnp
import numpy as np
from jax import lax
from jax.experimental import pallas as pl
from jax.experimental.pallas import tpu as pltpu
from jax.sharding import Mesh
from jax.sharding import PartitionSpec as P

CB = 128
WIN = 1024
HALF = 512
NF = 512
TAPS = 128
NBIN = 8
BINW = 80
ROUNDS = 4
MEETINGS = 5
PCAP = 512
WINDOWS = 8
LANES = 256
PLANE = 16
ROWS = 4
LAGS = 4
WIDE = 128
BAND = 8
LIST_ROWS = 24

BAND_LOW = 0.02
BAND_HIGH = 0.48
WATER = 0.1

F32 = jnp.float32
BF16 = jnp.bfloat16
HI = lax.Precision.HIGHEST
VMEM_LIMIT = 16 * 1024 * 1024


def level_rows(o):
    found = []
    for k in range(NBIN):
        pairs = [
            i
            for i in range(CB)
            for j in range(CB)
            if (o > 0 or i < j) and (CB * o + j - i) // BINW == k
        ]
        if pairs:
            found.append((k, min(pairs) // 16 * 16, max(pairs) // 16 * 16 + 16))
    return tuple(found)


LEVELS = tuple(level_rows(o) for o in range(MEETINGS))
SPANS = tuple((o, k, lo, hi) for o in range(MEETINGS) for k, lo, hi in LEVELS[o])
SPAN_ROWS = sum(hi - lo for _, _, lo, hi in SPANS)


def filter_table():
    k = np.arange(TAPS, dtype=np.float64)
    m = k - (TAPS - 1) / 2.0
    ideal = 2 * BAND_HIGH * np.sinc(2 * BAND_HIGH * m) - 2 * BAND_LOW * np.sinc(2 * BAND_LOW * m)
    taps = ideal * (0.5 - 0.5 * np.cos(2 * np.pi * (k + 0.5) / TAPS))
    lagged = np.arange(TAPS)[None, :] - np.arange(2 * TAPS)[:, None] + TAPS
    inside = (lagged >= 0) & (lagged < TAPS)
    return np.where(inside, taps[np.clip(lagged, 0, TAPS - 1)], 0.0).astype(np.float32)


def column_order():
    column = np.arange(WIN)
    return column // (2 * BAND) * BAND + column % BAND, column // BAND % 2 == 1


def transform_table():
    freq, is_imag = column_order()
    angle = (np.arange(HALF)[:, None] * freq[None, :] % WIN) * (2 * np.pi / WIN)
    return (np.where(is_imag[None, :], -np.sin(angle), np.cos(angle)) / math.sqrt(WIN)).astype(jnp.bfloat16)


def inverse_table():
    freq, is_imag = column_order()
    angle = (freq[:, None] * np.arange(LANES)[None, :] % WIN) * (2 * np.pi / WIN)
    weight = np.where(freq == 0, 1.0, 2.0)[:, None] / (WINDOWS * math.sqrt(WIN))
    table = (weight * np.where(is_imag[:, None], -np.sin(angle), np.cos(angle))).astype(np.float32)
    table = table.reshape(PLANE, LAGS, 2 * BAND, LANES).transpose(1, 0, 2, 3)
    return table.reshape(LAGS, PLANE * 2 * BAND, LANES)


def call(kernel, out_shape, *args, smem=(), aliases=None, scratch=()):
    specs = [
        pl.BlockSpec(memory_space=pltpu.SMEM) if n in smem else pl.BlockSpec(memory_space=pltpu.VMEM)
        for n in range(len(args))
    ]
    many = isinstance(out_shape, (tuple, list))
    out_specs = [pl.BlockSpec(memory_space=pltpu.VMEM)] * len(out_shape) if many else pl.BlockSpec(memory_space=pltpu.VMEM)
    return pl.pallas_call(
        kernel,
        out_shape=out_shape,
        in_specs=specs,
        out_specs=out_specs,
        input_output_aliases=aliases or {},
        scratch_shapes=list(scratch),
        compiler_params=pltpu.CompilerParams(vmem_limit_bytes=VMEM_LIMIT),
    )(*args)


def shape(dims, dtype):
    return jax.ShapeDtypeStruct(dims, dtype)


def lanes():
    return lax.broadcasted_iota(jnp.int32, (1, WIDE), 1)


def real_lanes():
    return (lanes() & BAND) == 0


def swap_parts(values):
    return jnp.where(real_lanes(), pltpu.roll(values, WIDE - BAND, 1), pltpu.roll(values, BAND, 1))


def fold(values):
    for step in (BAND, 2 * BAND, 4 * BAND, 8 * BAND):
        values = values + pltpu.roll(values, step, 1)
    return values


def transpose_pieces(arrays, width):
    bit = 1
    while bit < len(arrays):
        upper = (lanes() & (bit * width)) != 0
        out = list(arrays)
        for q in range(len(arrays)):
            if q & bit:
                continue
            a, b = arrays[q], arrays[q | bit]
            out[q] = jnp.where(upper, pltpu.roll(b, bit * width, 1), a)
            out[q | bit] = jnp.where(upper, b, pltpu.roll(a, WIDE - bit * width, 1))
        arrays = out
        bit *= 2
    return arrays


def spectra_kernel(hist_ref, x_ref, taps_ref, table_ref, out_ref):
    tiles = [hist_ref[...]] + [x_ref[:, t * TAPS : (t + 1) * TAPS] for t in range(WIN // TAPS)]
    pairs = [jnp.concatenate([tiles[t], tiles[t + 1]], axis=1) for t in range(WIN // TAPS)]
    rows = jnp.dot(jnp.concatenate(pairs, axis=0), taps_ref[...], precision=HI, preferred_element_type=F32)
    rows = rows.astype(BF16)
    filtered = [rows[t * CB : (t + 1) * CB] for t in range(WIN // TAPS)]
    early = jnp.concatenate(filtered[:4], axis=1)
    late = jnp.concatenate(filtered[4:], axis=1)
    column = lax.broadcasted_iota(jnp.int32, (1, WIN), 1)
    turn = jnp.where(column % 2 == 0, 1.0, -1.0).astype(F32)
    first = jnp.dot(early, table_ref[...], preferred_element_type=F32)
    second = jnp.dot(late, table_ref[...], preferred_element_type=F32)
    out_ref[...] = (first + turn * second).astype(BF16)


def pack_kernel(s0_ref, s1_ref, out_ref):
    for c in range(WIN // WIDE):
        cols = slice(c * WIDE, (c + 1) * WIDE)
        pieces = []
        for g in range(4):
            for ref in (s0_ref, s1_ref):
                pieces.append(ref[g * 32 : (g + 1) * 32, cols].astype(F32))
        for e, value in enumerate(transpose_pieces(pieces, 2 * BAND)):
            out_ref[c * 8 + e] = value.astype(BF16)


def whiten_kernel(slab_ref, out_ref):
    def one(p, carry):
        pieces = [slab_ref[p * LAGS + n].astype(F32) for n in range(LAGS)]
        for g, value in enumerate(transpose_pieces(pieces, 4 * BAND)):
            gain = lax.rsqrt(fold(value * value) * (1.0 / WINDOWS) + WATER)
            out_ref[p, g * 32 : (g + 1) * 32, :] = (value * gain).astype(BF16)
        return carry

    lax.fori_loop(0, PLANE, one, 0, unroll=2)


def list_kernel(blk_ref, count_ref, owner_ref, codes_ref, out_ref):
    lane = lax.broadcasted_iota(jnp.int32, (1, CB), 1)
    rows = []
    owners = jnp.zeros((1, CB), jnp.int32)
    for o in range(MEETINGS):
        live = jnp.where(blk_ref[0] >= o, count_ref[:, o : o + 1], 0)
        for n in range(4):
            rows.append(jnp.where(lane + n * CB < live, codes_ref[o : o + 1, n * CB : (n + 1) * CB], -1))
        owners = jnp.where(lane == o, owner_ref[:, o : o + 1], owners)
    rows = rows + [owners] + [jnp.zeros((1, CB), jnp.int32)] * (LIST_ROWS - len(rows) - 1)
    block = jnp.concatenate(rows, axis=0)
    for p in range(PLANE):
        out_ref[p] = block


def chosen_kernel(lists_ref, low_ref, high_ref):
    row = lax.broadcasted_iota(jnp.int32, (CB, PCAP), 0)

    def fill(p, ref, at):
        for o in range(MEETINGS):
            pieces = [lists_ref[p, o * 4 + n : o * 4 + n + 1, :] for n in range(4)]
            codes = jnp.concatenate(pieces, axis=1)
            pick_first = jnp.where(row == (codes >> 7), 1.0, 0.0).astype(BF16)
            pick_second = jnp.where(row == (codes & (CB - 1)), 1.0, 0.0).astype(BF16)
            chosen = lax.dot_general(pick_first, pick_second, (((1,), (1,)), ((), ())), preferred_element_type=F32)
            ref[at, o] = chosen.astype(BF16)

    for p in range(ROUNDS):
        fill(p, low_ref, p)

    def one(p, carry):
        fill(p, high_ref, p - ROUNDS)
        return carry

    lax.fori_loop(ROUNDS, PLANE, one, 0)


def fill_bins(bins_ref):
    spread = lax.broadcasted_iota(jnp.int32, (CB, CB), 1) - lax.broadcasted_iota(jnp.int32, (CB, CB), 0)
    at = 0
    for o, k, lo, hi in SPANS:
        distance = spread[lo:hi] + CB * o
        inside = (distance >= BINW * k) & (distance < BINW * (k + 1))
        bins_ref[at : at + hi - lo, :] = jnp.where(inside, 1.0, 0.0).astype(BF16)
        at += hi - lo


def spread(straight_ref, swapped_ref, at, block):
    values = block.astype(F32)
    straight_ref[at] = values
    swapped_ref[at] = jnp.where(real_lanes(), -1.0, 1.0) * swap_parts(values)


def meet(out_ref, owner_ref, bins_ref, chosen_ref, at_block, block, straight_ref, swapped_ref, places, p):
    row_id = lax.broadcasted_iota(jnp.int32, (NBIN, WIDE), 0)
    at = 0
    pieces = []
    for o, _, lo, hi in SPANS:
        pieces.append(chosen_ref[at_block, o, lo:hi, :] * bins_ref[at : at + hi - lo, :])
        at += hi - lo
    mixed = jnp.dot(jnp.concatenate(pieces, axis=0), block, preferred_element_type=F32)
    at = 0
    found = []
    for o in range(MEETINGS):
        real = jnp.zeros((NBIN, WIDE), F32)
        imag = jnp.zeros((NBIN, WIDE), F32)
        for k, lo, hi in LEVELS[o]:
            part = mixed[at : at + hi - lo]
            at += hi - lo
            dims = ((hi - lo) // 8, 8, WIDE)
            straight = straight_ref[places[o], lo:hi, :]
            swapped = swapped_ref[places[o], lo:hi, :]
            along = jnp.sum(jnp.sum((straight * part).reshape(dims), axis=0), axis=0, keepdims=True)
            across = jnp.sum(jnp.sum((swapped * part).reshape(dims), axis=0), axis=0, keepdims=True)
            real = jnp.where(row_id == k, along, real)
            imag = jnp.where(row_id == k, across, imag)
        found.append(jnp.where(real_lanes(), fold(real), fold(imag)))
    for o in range(MEETINGS):
        owner = owner_ref[p, o]
        spot = (owner % PLANE) * ROWS + owner // PLANE
        out_ref[spot] = out_ref[spot] + found[o]


def plane_kernel(owner_ref, chosen_ref, group_ref, out_ref, bins_ref, straight_ref, swapped_ref):
    out_ref[...] = jnp.zeros(out_ref.shape, F32)
    fill_bins(bins_ref)
    for p in range(ROUNDS):
        spread(straight_ref, swapped_ref, p, group_ref[p])

    def one(p, carry):
        spread(straight_ref, swapped_ref, p, group_ref[p])
        places = [p - o for o in range(MEETINGS)]
        meet(
            out_ref, owner_ref, bins_ref, chosen_ref, p - ROUNDS, group_ref[p], straight_ref, swapped_ref, places, p
        )
        return carry

    lax.fori_loop(ROUNDS, PLANE, one, 0)


def below_kernel(
    owner_ref, chosen_ref, group_ref, below_ref, sums_ref, out_ref, bins_ref, straight_ref, swapped_ref
):
    out_ref[...] = sums_ref[...]
    fill_bins(bins_ref)
    for p in range(ROUNDS):
        spread(straight_ref, swapped_ref, p, below_ref[p])
        spread(straight_ref, swapped_ref, p + ROUNDS, group_ref[p])
    for p in range(ROUNDS):
        places = [p + ROUNDS - o for o in range(MEETINGS)]
        meet(out_ref, owner_ref, bins_ref, chosen_ref, p, group_ref[p], straight_ref, swapped_ref, places, p)


def lag_kernel(lag_ref, parts_ref, table_ref, out_ref):
    lane = lanes()
    sign = jnp.where(real_lanes(), -1.0, 1.0)
    merged = []
    for side in range(2):
        value = jnp.zeros((ROWS * NBIN, WIDE), F32)
        for n in range(8):
            value = jnp.where((lane >> 4) == n, parts_ref[side * 8 + n], value)
        merged.append(value)
    swapped = [swap_parts(value) for value in merged]
    turned = []
    for quarter in range(4):
        step = (lane * (quarter + 2)) & 3
        along = jnp.where(step == 0, 1.0, 0.0) - jnp.where(step == 2, 1.0, 0.0)
        across = sign * (jnp.where(step == 1, 1.0, 0.0) - jnp.where(step == 3, 1.0, 0.0))
        turned.append(jnp.concatenate([x * along + y * across for x, y in zip(merged, swapped)], axis=1))
    table = table_ref[lag_ref[0]]
    lagged = jnp.dot(jnp.concatenate(turned, axis=0), table, precision=HI, preferred_element_type=F32)
    for quarter in range(4):
        for y in range(ROWS):
            at = quarter * ROWS * NBIN + y * NBIN
            out_ref[y * 4 + quarter] = lagged[at : at + NBIN]


def windows(before, before_at, traces, at, taps, table):
    return pl.pallas_call(
        spectra_kernel,
        out_shape=shape((CB, WIN), BF16),
        grid=(1,),
        in_specs=[
            pl.BlockSpec((CB, TAPS), lambda n: (0, before_at)),
            pl.BlockSpec((CB, WIN), lambda n: (0, at)),
            pl.BlockSpec((2 * TAPS, TAPS), lambda n: (0, 0)),
            pl.BlockSpec((HALF, WIN), lambda n: (0, 0)),
        ],
        out_specs=pl.BlockSpec((CB, WIN), lambda n: (0, 0)),
        compiler_params=pltpu.CompilerParams(vmem_limit_bytes=VMEM_LIMIT),
    )(before, traces, taps, table)


def body(traces, owner_map, pair_codes, pair_count):
    blk = (lax.axis_index("row") * PLANE + lax.axis_index("plane")).astype(jnp.int32).reshape(1)
    lag = lax.axis_index("lag").astype(jnp.int32).reshape(1)
    taps = jnp.asarray(filter_table())
    table = jnp.asarray(transform_table())

    history = lax.ppermute(traces[:, -TAPS:], "lag", [(i, i + 1) for i in range(3)])

    spectra1 = windows(traces, WIN // TAPS - 1, traces, 1, taps, table)
    lists_shape = shape((PLANE, LIST_ROWS, CB), jnp.int32)
    lists = call(
        list_kernel,
        lists_shape,
        blk,
        pair_count.reshape(1, MEETINGS),
        owner_map.reshape(1, MEETINGS),
        pair_codes,
        smem=(0,),
    )
    lists, history, spectra1 = lax.optimization_barrier((lists, history, spectra1))
    lists = lax.all_to_all(lists, "plane", 0, 0, tiled=True)
    spectra0 = windows(history, 0, traces, 0, taps, table)
    slabs = call(pack_kernel, shape((PLANE * LAGS, 32, WIDE), BF16), spectra0, spectra1)
    slabs, lists = lax.optimization_barrier((slabs, lists))
    owners = lists[:, 4 * MEETINGS, :MEETINGS]
    halves = tuple(shape((n, MEETINGS, CB, CB), BF16) for n in (ROUNDS, PLANE - ROUNDS))
    chosen_low, chosen_high = call(chosen_kernel, halves, lists)

    slabs = lax.all_to_all(slabs, ("plane", "lag"), 0, 0, tiled=True)
    group = call(whiten_kernel, shape((PLANE, CB, WIDE), BF16), slabs)
    last, chosen_low, chosen_high = lax.optimization_barrier((group[PLANE - ROUNDS :], chosen_low, chosen_high))
    below = lax.ppermute(last, "row", [(i, i + 1) for i in range(ROWS - 1)])

    sums_shape = shape((ROWS * PLANE, NBIN, WIDE), F32)
    bins = pltpu.VMEM((SPAN_ROWS, CB), BF16)
    spare = pltpu.VMEM((PLANE, CB, WIDE), F32)
    few = pltpu.VMEM((2 * ROUNDS, CB, WIDE), F32)
    sums = call(plane_kernel, sums_shape, owners, chosen_high, group, smem=(0,), scratch=(bins, spare, spare))
    sums = call(
        below_kernel,
        sums_shape,
        owners,
        chosen_low,
        group,
        below,
        sums,
        smem=(0,),
        aliases={4: 0},
        scratch=(bins, few, few),
    )
    parts = lax.all_to_all(sums.reshape(PLANE, ROWS * NBIN, WIDE), "plane", 0, 0, tiled=True)
    table = jnp.asarray(inverse_table())
    lagged = call(lag_kernel, shape((ROWS * LAGS, NBIN, LANES), F32), lag, parts, table, smem=(0,))
    return jnp.sum(lax.all_to_all(lagged, ("row", "lag"), 0, 0, tiled=True), axis=0, keepdims=True)


def solution(mesh):
    split = Mesh(mesh.devices.reshape(ROWS, PLANE, 4), ("row", "plane", "lag"))
    owned = ("row", "plane")
    return jax.shard_map(
        body,
        mesh=split,
        in_specs=(P(owned, "lag"), P(None, owned), P(None, owned), P(None, owned)),
        out_specs=P(owned, None, "lag"),
        check_vma=False,
    )
```

time: 101 us -> 107 us (1.059)
  blocking collectives: 32.4 us -> 17.6 us
  waiting for transfers between devices: 15.9 us -> 27.4 us
  Pallas kernels: 20.2 us -> 28.2 us
  local copies, waits for them, and re-layouts: 2.49 us -> 5.11 us
    all_to_all x1 -> x2, waiting for transfers between devices: 8.25 us -> 22.9 us  [the longest x1 12.9 us: body(): slabs = lax.all_to_all(slabs, ('plane', 'lag'), 0, 0, tiled=True)]
    all_to_all x1 -> x0, blocking collectives: 14.1 us -> none  [body(): lax.all_to_all(sums.reshape(PLANE, ROWS * NBIN, 2 * BAND), 'plane', 0, 0,...]
    ppermute x3 -> x0, starting transfers between devices: 5.33 us -> none  [crossed(): return lax.ppermute(block, 'lag', [(i, i ^ bit) for i in range(4)])]
    all_to_all x1 -> x2, starting transfers between devices: 4.33 us -> 8.74 us  [the longest x1 5.21 us: body(): slabs = lax.all_to_all(slabs, ('plane', 'lag'), 0, 0, tiled=True)]
    pallas_call x9 -> x7, Pallas kernels: 20.2 us -> 24.6 us  [call(): pl.pallas_call(kernel, out_shape=out_shape, in_specs=specs, out_specs=out...]
    unnamed x14 -> x24, local copies, waits for them, and re-layouts: 0.22 us -> 4.21 us
    pallas_call x0 -> x2, Pallas kernels: none -> 3.66 us  [windows(): pl.pallas_call(spectra_kernel, out_shape=shape((CB, WIN), BF16), grid=(1,...]
    ppermute x3 -> x0, waiting for transfers between devices: 2.22 us -> none  [crossed(): return lax.ppermute(block, 'lag', [(i, i ^ bit) for i in range(4)])]
  transfers between devices with their start and end apart: 7 -> 5, of which waited for: 4 -> 3; matrix products, arithmetic and copies ran while one was open for 1% -> 0% of each run, Pallas kernels for 15% -> 20%
where the time goes in v4:
time: 107 us
  Pallas kernels  28.2 us (26%)
  starting transfers between devices  27.6 us (26%)
  waiting for transfers between devices  27.4 us (26%)
  blocking collectives  17.6 us (16%)
  local copies, waits for them, and re-layouts  5.11 us (5%)
    pallas_call x7, Pallas kernels, call(): pl.pallas_call(kernel, out_shape=out_shape, in_specs=specs, out_specs=out...  24.6 us
    all_to_all x1, blocking collectives, body(): lax.all_to_all(lagged, ('row', 'lag'), 0, 0, tiled=True)  17.6 us
    all_to_all x1, waiting for transfers between devices, body(): slabs = lax.all_to_all(slabs, ('plane', 'lag'), 0, 0, tiled=True)  12.9 us
    ppermute x1, starting transfers between devices, body(): lax.ppermute(traces[:, -TAPS:], 'lag', [(i, i + 1) for i in range(3)])  10.2 us
    all_to_all x1, waiting for transfers between devices, body(): lax.all_to_all(sums.reshape(PLANE, ROWS * NBIN, WIDE), 'plane', 0, 0, til...  10.1 us
    all_to_all x1, starting transfers between devices, body(): lists = lax.all_to_all(lists, 'plane', 0, 0, tiled=True)  5.49 us
    all_to_all x1, starting transfers between devices, body(): slabs = lax.all_to_all(slabs, ('plane', 'lag'), 0, 0, tiled=True)  5.21 us
    all_to_all x1, waiting for transfers between devices, body(): lists = lax.all_to_all(lists, 'plane', 0, 0, tiled=True)  4.44 us
  transfers between devices with their start and end apart: 5, of which 3 were waited for; matrix products, arithmetic and copies ran while one was open for 0% of the time, Pallas kernels for 20%

profile of v4, /device:TPU:1, one launch (start us, length us, event | category | flops | bytes accessed | tf_op | source)
XLA Modules:
  0.0 106.8 jit_solution(10414307542999875074)
XLA Ops:
  0.0 0.0 copy-start.10
  0.0 0.0 copy-start.9
  0.0 0.0 copy-start.11
  0.0 0.9 slice.9
  0.9 10.2 %collective-permute-start = (f32[128,128]{1,0:T(8,128)S(1)}, f32[128,128]{1,0:T(8,128)S(1)}, u32[]{:S(2)}, u32[]{:S(2)}) collective-permute-start(f32[128,128]{1,0:T(8,128)S(1)} %slice.9), channel_id=1, source_target_pairs={{0,1},{1,2},{2,3},{4,5},{5,6},{6,7},{8,9},{9,10},{10,11},{12,13},{... | collective-permute-start | bytes 196616 | tf_op jit(solution)/shard_map/ppermute | solution.py:342
  11.1 0.0 copy-start
  11.1 1.2 %copy-done = f32[128,2048]{1,0:T(8,128)S(1)} copy-done((f32[128,2048]{1,0:T(8,128)S(1)}, f32[128,2048]{1,0:T(8,128)}, u32[]{:S(2)}) %copy-start) | copy-done | bytes 1048600
  12.3 0.0 copy-start.2
  12.3 1.2 %copy-done.2 = bf16[512,1024]{1,0:T(8,128)(2,1)S(1)} copy-done((bf16[512,1024]{1,0:T(8,128)(2,1)S(1)}, bf16[512,1024]{1,0:T(8,128)(2,1)}, u32[]{:S(2)}) %copy-start.2) | copy-done | bytes 1048600
  13.6 0.0 copy-start.7
  13.6 0.9 copy-done.7
  14.5 0.0 copy-start.1
  14.5 0.0 copy-start.3
  14.5 0.0 copy-start.8
  14.5 1.8 %shard_map.74.s1_ref = bf16[128,1024]{1,0:T(8,128)(2,1)S(1)} custom-call(f32[128,2048]{1,0:T(8,128)S(1)} %copy-done, f32[128,2048]{1,0:T(8,128)S(1)} %copy-done, f32[256,128]{1,0:T(8,128)S(1)} %copy-done.7, bf16[512,1024]{1,0:T(8,128)(2,1)S(1)} %copy-done.2), custom_call_target="tpu_custom_call" | custom-call | tf_op jit(solution)/shard_map/pallas_call | solution.py:321
  16.3 0.0 copy-done.10
  16.3 0.0 copy-done.9
  16.3 0.0 copy-done.11
  16.3 0.8 shard_map.73
  17.1 0.0 collective-permute-done.hist_ref
  17.1 5.5 %all-to-all-start = ((s32[16,24,128]{2,1,0:T(8,128)}), s32[16,24,128]{2,1,0:T(8,128)S(1)}, u32[]{:S(2)}, u32[]{:S(2)}) async-start(s32[16,24,128]{2,1,0:T(8,128)} %shard_map.73), calls=%async_computation | async-start | bytes 393216 | tf_op jit(solution)/shard_map/all_to_all | solution.py:356
  22.6 0.0 copy-done.1
  22.6 0.0 copy-done.3
  22.6 0.0 copy-done.8
  22.6 1.8 %shard_map.75.s0_ref = bf16[128,1024]{1,0:T(8,128)(2,1)S(1)} custom-call(f32[128,128]{1,0:T(8,128)S(1)} %collective-permute-done.hist_ref, f32[128,2048]{1,0:T(8,128)S(1)} %copy-done.1, f32[256,128]{1,0:T(8,128)S(1)} %copy-done.8, bf16[512,1024]{1,0:T(8,128)(2,1)S(1)} %copy-done.3), custom_call_target="tpu_custom_call" | custom-call | tf_op jit(solution)/shard_map/pallas_call | solution.py:321
  24.5 2.0 %shard_map.76 = bf16[64,32,128]{2,1,0:T(8,128)(2,1)} custom-call(bf16[128,1024]{1,0:T(8,128)(2,1)S(1)} %shard_map.75.s0_ref, bf16[128,1024]{1,0:T(8,128)(2,1)S(1)} %shard_map.74.s1_ref), custom_call_target="tpu_custom_call" | custom-call | tf_op jit(solution)/shard_map/pallas_call | solution.py:97
  26.5 4.4 %all-to-all-done.lists_ref = s32[16,24,128]{2,1,0:T(8,128)S(1)} async-done(((s32[16,24,128]{2,1,0:T(8,128)}), s32[16,24,128]{2,1,0:T(8,128)S(1)}, u32[]{:S(2)}, u32[]{:S(2)}) %all-to-all-start) | async-done | bytes 196640 | tf_op jit(solution)/shard_map/all_to_all | solution.py:356
  30.9 5.2 %all-to-all-start.1 = ((bf16[64,32,128]{2,1,0:T(8,128)(2,1)}), bf16[64,32,128]{2,1,0:T(8,128)(2,1)S(1)}, u32[]{:S(2)}, u32[]{:S(2)}) async-start(bf16[64,32,128]{2,1,0:T(8,128)(2,1)} %shard_map.76), calls=%async_computation.1 | async-start | bytes 1048576 | tf_op jit(solution)/shard_map/all_to_all | solution.py:364
  36.1 5.3 %shard_map.78 = (bf16[4,5,128,128]{3,2,1,0:T(8,128)(2,1)S(1)}, bf16[12,5,128,128]{3,2,1,0:T(8,128)(2,1)S(1)}) custom-call(s32[16,24,128]{2,1,0:T(8,128)S(1)} %all-to-all-done.lists_ref), custom_call_target="tpu_custom_call" | custom-call | tf_op jit(solution)/shard_map/pallas_call | solution.py:97
  41.4 0.0 copy-start.5
  41.4 0.8 copy-done.5
  42.3 12.9 %all-to-all-done.1.slab_ref = bf16[64,32,128]{2,1,0:T(8,128)(2,1)S(1)} async-done(((bf16[64,32,128]{2,1,0:T(8,128)(2,1)}), bf16[64,32,128]{2,1,0:T(8,128)(2,1)S(1)}, u32[]{:S(2)}, u32[]{:S(2)}) %all-to-all-start.1) | async-done | bytes 524320 | tf_op jit(solution)/shard_map/all_to_all | solution.py:364
  55.1 0.0 copy-start.6
  55.1 3.7 %shard_map.77.group_ref = bf16[16,128,128]{2,1,0:T(8,128)(2,1)S(1)} custom-call(bf16[64,32,128]{2,1,0:T(8,128)(2,1)S(1)} %all-to-all-done.1.slab_ref), custom_call_target="tpu_custom_call" | custom-call | tf_op jit(solution)/shard_map/pallas_call | solution.py:97
  58.9 3.2 %collective-permute-start.1 = (bf16[4,128,128]{2,1,0:T(8,128)(2,1)S(1)}, bf16[4,128,128]{2,1,0:T(8,128)(2,1)S(1)}, u32[]{:S(2)}, u32[]{:S(2)}) collective-permute-start(bf16[4,128,128]{2,1,0:T(8,128)(2,1)S(1)} %slice.12), channel_id=1, source_target_pairs={{0,64},{64,128},{128,192},{1,65},{65,129},{129,193},{2,66},{66,130... | collective-permute-start | bytes 393224 | tf_op jit(solution)/shard_map/ppermute | solution.py:367
  62.1 0.0 copy-start.4
  62.1 9.4 %shard_map.79.sums_ref = f32[64,8,128]{2,1,0:T(8,128)} custom-call(s32[16,5]{1,0:T(8,128)S(1)} %bitcast.7, bf16[12,5,128,128]{3,2,1,0:T(8,128)(2,1)S(1)} %get-tuple-element.24.chosen_ref, bf16[16,128,128]{2,1,0:T(8,128)(2,1)S(1)} %shard_map.77.group_ref), custom_call_target="tpu_custom_call" | custom-call | tf_op jit(solution)/shard_map/pallas_call | solution.py:97
  71.5 0.0 collective-permute-done.1.below_ref
  71.5 0.0 copy-done.6
  71.5 3.1 %shard_map.80 = f32[64,8,128]{2,1,0:T(8,128)} custom-call(s32[16,5]{1,0:T(8,128)S(1)} %bitcast.8, bf16[4,5,128,128]{3,2,1,0:T(8,128)(2,1)S(1)} %copy-done.6, bf16[16,128,128]{2,1,0:T(8,128)(2,1)S(1)} %shard_map.77.group_ref, bf16[4,128,128]{2,1,0:T(8,128)(2,1)S(1)} %collective-permute-done.1.below_ref, ...), custom_call_target="tpu_custom_call", output_to_operand_aliasing={{}: (4, {})} | custom-call | tf_op jit(solution)/shard_map/pallas_call | solution.py:97
  74.6 3.5 %all-to-all-start.2 = ((f32[16,32,128]{2,1,0:T(8,128)}), f32[16,32,128]{2,1,0:T(8,128)S(1)}, u32[]{:S(2)}, u32[]{:S(2)}) async-start(f32[16,32,128]{2,1,0:T(8,128)} %bitcast.5), calls=%async_computation.2 | async-start | bytes 524288 | tf_op jit(solution)/shard_map/all_to_all | solution.py:386
  78.1 10.1 %all-to-all-done.2.parts_ref = f32[16,32,128]{2,1,0:T(8,128)S(1)} async-done(((f32[16,32,128]{2,1,0:T(8,128)}), f32[16,32,128]{2,1,0:T(8,128)S(1)}, u32[]{:S(2)}, u32[]{:S(2)}) %all-to-all-start.2) | async-done | bytes 262176 | tf_op jit(solution)/shard_map/all_to_all | solution.py:386
  88.2 0.0 copy-done.4
  88.2 0.3 shard_map.81
  88.5 17.6 %all_to_all.20 = f32[16,8,256]{2,1,0:T(8,128)S(1)} all-to-all(f32[16,8,256]{2,1,0:T(8,128)S(1)} %shard_map.81), channel_id=1, replica_groups=mesh['row'=4,'plane'=16,'lag'=4] {'row','lag'}, dimensions={0} | all-to-all | bytes 262144 | tf_op jit(solution)/shard_map/all_to_all | solution.py:389
  106.2 0.6 reduce_sum.9
  (2 shorter events, 0.0 us)
Async XLA Ops:
  0.0 16.3 %copy-start.10 = (s32[5,1]{0,1:T(1,128)S(1)}, s32[5,1]{0,1:T(1,128)}, u32[]{:S(2)}) copy-start(s32[5,1]{0,1:T(1,128)} %param.10) | copy-start | bytes 64
  0.0 16.3 %copy-start.9 = (s32[5,512]{1,0:T(8,128)S(1)}, s32[5,512]{1,0:T(8,128)}, u32[]{:S(2)}) copy-start(s32[5,512]{1,0:T(8,128)} %codes_ref.1) | copy-start | bytes 30724
  0.0 16.3 %copy-start.11 = (s32[5,1]{0,1:T(1,128)S(1)}, s32[5,1]{0,1:T(1,128)}, u32[]{:S(2)}) copy-start(s32[5,1]{0,1:T(1,128)} %param.8) | copy-start | bytes 64
  0.9 16.2 %collective-permute-start = (f32[128,128]{1,0:T(8,128)S(1)}, f32[128,128]{1,0:T(8,128)S(1)}, u32[]{:S(2)}, u32[]{:S(2)}) collective-permute-start(f32[128,128]{1,0:T(8,128)S(1)} %slice.9), channel_id=1, source_target_pairs={{0,1},{1,2},{2,3},{4,5},{5,6},{6,7},{8,9},{9,10},{10,11},{12,13},{... | collective-permute-start | bytes 196616 | tf_op jit(solution)/shard_map/ppermute | solution.py:342
  11.1 1.2 %copy-start = (f32[128,2048]{1,0:T(8,128)S(1)}, f32[128,2048]{1,0:T(8,128)}, u32[]{:S(2)}) copy-start(f32[128,2048]{1,0:T(8,128)} %x_ref.3) | copy-start | bytes 3145732
  12.3 1.2 %copy-start.2 = (bf16[512,1024]{1,0:T(8,128)(2,1)S(1)}, bf16[512,1024]{1,0:T(8,128)(2,1)}, u32[]{:S(2)}) copy-start(bf16[512,1024]{1,0:T(8,128)(2,1)} %constant.24.clone.table_ref) | copy-start | bytes 3145732
  13.6 0.9 copy-start.7
  14.5 8.2 %copy-start.1 = (f32[128,2048]{1,0:T(8,128)S(1)}, f32[128,2048]{1,0:T(8,128)}, u32[]{:S(2)}) copy-start(f32[128,2048]{1,0:T(8,128)} %x_ref.3) | copy-start | bytes 3145732
  14.5 8.2 %copy-start.3 = (bf16[512,1024]{1,0:T(8,128)(2,1)S(1)}, bf16[512,1024]{1,0:T(8,128)(2,1)}, u32[]{:S(2)}) copy-start(bf16[512,1024]{1,0:T(8,128)(2,1)} %constant.24.clone.table_ref) | copy-start | bytes 3145732
  14.5 8.2 %copy-start.8 = (f32[256,128]{1,0:T(8,128)S(1)}, f32[256,128]{1,0:T(8,128)}, u32[]{:S(2)}) copy-start(f32[256,128]{1,0:T(8,128)} %constant.23.clone.taps_ref) | copy-start | bytes 393220
  17.1 13.8 %all-to-all-start = ((s32[16,24,128]{2,1,0:T(8,128)}), s32[16,24,128]{2,1,0:T(8,128)S(1)}, u32[]{:S(2)}, u32[]{:S(2)}) async-start(s32[16,24,128]{2,1,0:T(8,128)} %shard_map.73), calls=%async_computation | async-start | bytes 393216 | tf_op jit(solution)/shard_map/all_to_all | solution.py:356
  30.9 24.2 %all-to-all-start.1 = ((bf16[64,32,128]{2,1,0:T(8,128)(2,1)}), bf16[64,32,128]{2,1,0:T(8,128)(2,1)S(1)}, u32[]{:S(2)}, u32[]{:S(2)}) async-start(bf16[64,32,128]{2,1,0:T(8,128)(2,1)} %shard_map.76), calls=%async_computation.1 | async-start | bytes 1048576 | tf_op jit(solution)/shard_map/all_to_all | solution.py:364
  41.4 0.8 copy-start.5
  55.1 16.4 %copy-start.6 = (bf16[4,5,128,128]{3,2,1,0:T(8,128)(2,1)S(1)}, bf16[4,5,128,128]{3,2,1,0:T(8,128)(2,1)}, u32[]{:S(2)}) copy-start(bf16[4,5,128,128]{3,2,1,0:T(8,128)(2,1)} %copy-done.5) | copy-start | bytes 1966084
  58.9 12.6 %collective-permute-start.1 = (bf16[4,128,128]{2,1,0:T(8,128)(2,1)S(1)}, bf16[4,128,128]{2,1,0:T(8,128)(2,1)S(1)}, u32[]{:S(2)}, u32[]{:S(2)}) collective-permute-start(bf16[4,128,128]{2,1,0:T(8,128)(2,1)S(1)} %slice.12), channel_id=1, source_target_pairs={{0,64},{64,128},{128,192},{1,65},{65,129},{129,193},{2,66},{66,130... | collective-permute-start | bytes 393224 | tf_op jit(solution)/shard_map/ppermute | solution.py:367
  62.1 26.1 %copy-start.4 = (f32[4,256,256]{2,1,0:T(8,128)S(1)}, f32[4,256,256]{2,1,0:T(8,128)}, u32[]{:S(2)}) copy-start(f32[4,256,256]{2,1,0:T(8,128)} %constant.25.clone.table_ref) | copy-start | bytes 3145732
  74.6 13.6 %all-to-all-start.2 = ((f32[16,32,128]{2,1,0:T(8,128)}), f32[16,32,128]{2,1,0:T(8,128)S(1)}, u32[]{:S(2)}, u32[]{:S(2)}) async-start(f32[16,32,128]{2,1,0:T(8,128)} %bitcast.5), calls=%async_computation.2 | async-start | bytes 524288 | tf_op jit(solution)/shard_map/all_to_all | solution.py:386

commit v5 on v4

--- a/solution.py
+++ b/solution.py
@@ -82,9 +82,7 @@
     freq, is_imag = column_order()
     angle = (freq[:, None] * np.arange(LANES)[None, :] % WIN) * (2 * np.pi / WIN)
     weight = np.where(freq == 0, 1.0, 2.0)[:, None] / (WINDOWS * math.sqrt(WIN))
-    table = (weight * np.where(is_imag[:, None], -np.sin(angle), np.cos(angle))).astype(np.float32)
-    table = table.reshape(PLANE, LAGS, 2 * BAND, LANES).transpose(1, 0, 2, 3)
-    return table.reshape(LAGS, PLANE * 2 * BAND, LANES)
+    return (weight * np.where(is_imag[:, None], -np.sin(angle), np.cos(angle))).astype(np.float32)
 
 
 def call(kernel, out_shape, *args, smem=(), aliases=None, scratch=()):
@@ -117,14 +115,37 @@
     return (lanes() & BAND) == 0
 
 
-def swap_parts(values):
-    return jnp.where(real_lanes(), pltpu.roll(values, WIDE - BAND, 1), pltpu.roll(values, BAND, 1))
-
-
 def fold(values):
     for step in (BAND, 2 * BAND, 4 * BAND, 8 * BAND):
         values = values + pltpu.roll(values, step, 1)
     return values
+
+
+def fold_table(real, imag):
+    row = lax.broadcasted_iota(jnp.int32, (WIDE, WIDE), 0)
+    column = lax.broadcasted_iota(jnp.int32, (WIDE, WIDE), 1)
+    same = ((row ^ column) & (BAND - 1)) == 0
+    asked = jnp.where((column & BAND) == 0, real, imag)
+    return jnp.where(same, asked, 0.0).astype(BF16)
+
+
+def swap_table():
+    row = lax.broadcasted_iota(jnp.int32, (WIDE, WIDE), 0)
+    column = lax.broadcasted_iota(jnp.int32, (WIDE, WIDE), 1)
+    value = jnp.where((column & BAND) == 0, -1.0, 1.0)
+    return jnp.where(row == (column ^ BAND), value, 0.0).astype(BF16)
+
+
+def order_table():
+    row = lax.broadcasted_iota(jnp.int32, (4 * WIDE, 1), 0)
+    goal = ((row >> 5) & 3) * WIDE + (row >> 7) * 32 + (row & 31)
+    column = lax.broadcasted_iota(jnp.int32, (4 * WIDE, 4 * WIDE), 1)
+    return jnp.where(column == goal, 1.0, 0.0).astype(BF16)
+
+
+def halves_of(values):
+    high = values.astype(BF16)
+    return high, (values - high.astype(F32)).astype(BF16)
 
 
 def transpose_pieces(arrays, width):
@@ -169,15 +190,30 @@
             out_ref[c * 8 + e] = value.astype(BF16)
 
 
-def whiten_kernel(slab_ref, out_ref):
-    def one(p, carry):
-        pieces = [slab_ref[p * LAGS + n].astype(F32) for n in range(LAGS)]
-        for g, value in enumerate(transpose_pieces(pieces, 4 * BAND)):
-            gain = lax.rsqrt(fold(value * value) * (1.0 / WINDOWS) + WATER)
-            out_ref[p, g * 32 : (g + 1) * 32, :] = (value * gain).astype(BF16)
-        return carry
-
-    lax.fori_loop(0, PLANE, one, 0, unroll=2)
+def whiten_kernel(slab_ref, low_ref, high_ref, low_swapped_ref, high_swapped_ref):
+    order = order_table()
+    both = fold_table(1.0, 1.0)
+    both = jnp.concatenate([both, both], axis=0)
+    swap = swap_table()
+    batch = 4
+    for first in range(0, PLANE, batch):
+        rows = []
+        for p in range(first, first + batch):
+            rows.append(jnp.concatenate([slab_ref[p * LAGS + n] for n in range(LAGS)], axis=1))
+        values = jnp.dot(jnp.concatenate(rows, axis=0), order, preferred_element_type=F32)
+        values = jnp.concatenate([values[:, g * WIDE : (g + 1) * WIDE] for g in range(4)], axis=0)
+        high, low = halves_of(values * values)
+        power = jnp.dot(jnp.concatenate([high, low], axis=1), both, preferred_element_type=F32)
+        whitened = (values * lax.rsqrt(power * (1.0 / WINDOWS) + WATER)).astype(BF16)
+        turned = jnp.dot(whitened, swap, preferred_element_type=F32).astype(BF16)
+        for n in range(batch):
+            at_block = first + n if first < ROUNDS else first + n - ROUNDS
+            out_ref = low_ref if first < ROUNDS else high_ref
+            swapped_ref = low_swapped_ref if first < ROUNDS else high_swapped_ref
+            for g in range(4):
+                at = (g * batch + n) * 32
+                out_ref[at_block, g * 32 : (g + 1) * 32, :] = whitened[at : at + 32]
+                swapped_ref[at_block, g * 32 : (g + 1) * 32, :] = turned[at : at + 32]
 
 
 def list_kernel(blk_ref, count_ref, owner_ref, codes_ref, out_ref):
@@ -188,7 +224,8 @@
         live = jnp.where(blk_ref[0] >= o, count_ref[:, o : o + 1], 0)
         for n in range(4):
             rows.append(jnp.where(lane + n * CB < live, codes_ref[o : o + 1, n * CB : (n + 1) * CB], -1))
-        owners = jnp.where(lane == o, owner_ref[:, o : o + 1], owners)
+        owner = owner_ref[:, o : o + 1]
+        owners = jnp.where(lane == o, (owner & (PLANE - 1)) * ROWS + (owner >> 4), owners)
     rows = rows + [owners] + [jnp.zeros((1, CB), jnp.int32)] * (LIST_ROWS - len(rows) - 1)
     block = jnp.concatenate(rows, axis=0)
     for p in range(PLANE):
@@ -214,7 +251,7 @@
         fill(p, high_ref, p - ROUNDS)
         return carry
 
-    lax.fori_loop(ROUNDS, PLANE, one, 0)
+    lax.fori_loop(ROUNDS, PLANE, one, 0, unroll=4)
 
 
 def fill_bins(bins_ref):
@@ -227,13 +264,7 @@
         at += hi - lo
 
 
-def spread(straight_ref, swapped_ref, at, block):
-    values = block.astype(F32)
-    straight_ref[at] = values
-    swapped_ref[at] = jnp.where(real_lanes(), -1.0, 1.0) * swap_parts(values)
-
-
-def meet(out_ref, owner_ref, bins_ref, chosen_ref, at_block, block, straight_ref, swapped_ref, places, p):
+def meet(out_ref, owner_ref, bins_ref, chosen_ref, at_block, block, partners, p):
     row_id = lax.broadcasted_iota(jnp.int32, (NBIN, WIDE), 0)
     at = 0
     pieces = []
@@ -242,95 +273,176 @@
         at += hi - lo
     mixed = jnp.dot(jnp.concatenate(pieces, axis=0), block, preferred_element_type=F32)
     at = 0
-    found = []
+    real, imag = [], []
     for o in range(MEETINGS):
-        real = jnp.zeros((NBIN, WIDE), F32)
-        imag = jnp.zeros((NBIN, WIDE), F32)
+        straight = partners[o][0].astype(F32)
+        swapped = partners[o][1].astype(F32)
         for k, lo, hi in LEVELS[o]:
             part = mixed[at : at + hi - lo]
             at += hi - lo
             dims = ((hi - lo) // 8, 8, WIDE)
-            straight = straight_ref[places[o], lo:hi, :]
-            swapped = swapped_ref[places[o], lo:hi, :]
-            along = jnp.sum(jnp.sum((straight * part).reshape(dims), axis=0), axis=0, keepdims=True)
-            across = jnp.sum(jnp.sum((swapped * part).reshape(dims), axis=0), axis=0, keepdims=True)
-            real = jnp.where(row_id == k, along, real)
-            imag = jnp.where(row_id == k, across, imag)
-        found.append(jnp.where(real_lanes(), fold(real), fold(imag)))
+            real.append(jnp.sum((straight[lo:hi] * part).reshape(dims), axis=0))
+            imag.append(jnp.sum((swapped[lo:hi] * part).reshape(dims), axis=0))
+    at = 0
     for o in range(MEETINGS):
-        owner = owner_ref[p, o]
-        spot = (owner % PLANE) * ROWS + owner // PLANE
-        out_ref[spot] = out_ref[spot] + found[o]
-
-
-def plane_kernel(owner_ref, chosen_ref, group_ref, out_ref, bins_ref, straight_ref, swapped_ref):
+        re = jnp.zeros((NBIN, WIDE), F32)
+        im = jnp.zeros((NBIN, WIDE), F32)
+        for k, _, _ in LEVELS[o]:
+            re = jnp.where(row_id == k, jnp.sum(real[at], axis=0, keepdims=True), re)
+            im = jnp.where(row_id == k, jnp.sum(imag[at], axis=0, keepdims=True), im)
+            at += 1
+        found = jnp.where(real_lanes(), fold(re), fold(im))
+        spot = owner_ref[p, o]
+        out_ref[spot] = out_ref[spot] + found
+
+
+def plane_kernel(
+    owner_ref, chosen_ref, low_ref, high_ref, low_swapped_ref, high_swapped_ref, out_ref, bins_ref, group_ref, swapped_ref
+):
     out_ref[...] = jnp.zeros(out_ref.shape, F32)
     fill_bins(bins_ref)
+    group_ref[:ROUNDS] = low_ref[...]
+    group_ref[ROUNDS:] = high_ref[...]
+    swapped_ref[:ROUNDS] = low_swapped_ref[...]
+    swapped_ref[ROUNDS:] = high_swapped_ref[...]
+
+    def one(p, carry):
+        partners = [(group_ref[p - o], swapped_ref[p - o]) for o in range(MEETINGS)]
+        meet(out_ref, owner_ref, bins_ref, chosen_ref, p - ROUNDS, group_ref[p], partners, p)
+        return carry
+
+    lax.fori_loop(ROUNDS, PLANE, one, 0, unroll=4)
+
+
+def below_kernel(owner_ref, chosen_ref, group_ref, swapped_ref, below_ref, sums_ref, out_ref, bins_ref, total_ref):
+    total_ref[...] = sums_ref[...]
+    fill_bins(bins_ref)
+    swap = swap_table()
+    under = []
+    for n in range(ROUNDS):
+        block = below_ref[n]
+        under.append((block, jnp.dot(block, swap, preferred_element_type=F32).astype(BF16)))
     for p in range(ROUNDS):
-        spread(straight_ref, swapped_ref, p, group_ref[p])
-
-    def one(p, carry):
-        spread(straight_ref, swapped_ref, p, group_ref[p])
-        places = [p - o for o in range(MEETINGS)]
-        meet(
-            out_ref, owner_ref, bins_ref, chosen_ref, p - ROUNDS, group_ref[p], straight_ref, swapped_ref, places, p
-        )
-        return carry
-
-    lax.fori_loop(ROUNDS, PLANE, one, 0)
-
-
-def below_kernel(
-    owner_ref, chosen_ref, group_ref, below_ref, sums_ref, out_ref, bins_ref, straight_ref, swapped_ref
-):
-    out_ref[...] = sums_ref[...]
-    fill_bins(bins_ref)
-    for p in range(ROUNDS):
-        spread(straight_ref, swapped_ref, p, below_ref[p])
-        spread(straight_ref, swapped_ref, p + ROUNDS, group_ref[p])
-    for p in range(ROUNDS):
-        places = [p + ROUNDS - o for o in range(MEETINGS)]
-        meet(out_ref, owner_ref, bins_ref, chosen_ref, p, group_ref[p], straight_ref, swapped_ref, places, p)
+        partners = [
+            (group_ref[p - o], swapped_ref[p - o]) if p >= o else under[p - o + ROUNDS] for o in range(MEETINGS)
+        ]
+        meet(total_ref, owner_ref, bins_ref, chosen_ref, p, group_ref[p], partners, p)
+    row_id = lax.broadcasted_iota(jnp.int32, (NBIN, WIDE), 0)
+    own_piece = (lanes() >> 4) == row_id
+    for n in range(PLANE):
+        rows = jnp.zeros((NBIN, WIDE), F32)
+        for y in range(ROWS):
+            value = jnp.where(own_piece, total_ref[n * ROWS + y], 0.0)
+            rows = jnp.where(row_id == y, jnp.sum(value, axis=0, keepdims=True), rows)
+        for lag in range(LAGS):
+            out_ref[n * LAGS + lag] = rows
 
 
 def lag_kernel(lag_ref, parts_ref, table_ref, out_ref):
     lane = lanes()
     sign = jnp.where(real_lanes(), -1.0, 1.0)
-    merged = []
-    for side in range(2):
-        value = jnp.zeros((ROWS * NBIN, WIDE), F32)
-        for n in range(8):
-            value = jnp.where((lane >> 4) == n, parts_ref[side * 8 + n], value)
-        merged.append(value)
-    swapped = [swap_parts(value) for value in merged]
-    turned = []
-    for quarter in range(4):
-        step = (lane * (quarter + 2)) & 3
-        along = jnp.where(step == 0, 1.0, 0.0) - jnp.where(step == 2, 1.0, 0.0)
-        across = sign * (jnp.where(step == 1, 1.0, 0.0) - jnp.where(step == 3, 1.0, 0.0))
-        turned.append(jnp.concatenate([x * along + y * across for x, y in zip(merged, swapped)], axis=1))
-    table = table_ref[lag_ref[0]]
-    lagged = jnp.dot(jnp.concatenate(turned, axis=0), table, precision=HI, preferred_element_type=F32)
-    for quarter in range(4):
-        for y in range(ROWS):
-            at = quarter * ROWS * NBIN + y * NBIN
-            out_ref[y * 4 + quarter] = lagged[at : at + NBIN]
-
-
-def windows(before, before_at, traces, at, taps, table):
+    step = (lane * (lag_ref[0] + 2)) & 3
+    along = jnp.where(step == 0, 1.0, 0.0) - jnp.where(step == 2, 1.0, 0.0)
+    across = sign * (jnp.where(step == 1, 1.0, 0.0) - jnp.where(step == 3, 1.0, 0.0))
+    columns = []
+    for first in range(0, PLANE * LAGS, 8):
+        bins = transpose_pieces([parts_ref[first + n] for n in range(8)], 2 * BAND)
+        value = jnp.concatenate(bins, axis=0)
+        swapped = jnp.where(real_lanes(), pltpu.roll(value, WIDE - BAND, 1), pltpu.roll(value, BAND, 1))
+        columns.append(value * along + swapped * across)
+    lagged = jnp.dot(jnp.concatenate(columns, axis=1), table_ref[...], precision=HI, preferred_element_type=F32)
+    for y in range(ROWS):
+        for k in range(NBIN):
+            out_ref[y, k : k + 1, :] = lagged[k * 8 + y : k * 8 + y + 1]
+
+
+def later_kernel(traces_ref, taps_ref, table_ref, out_ref, x_ref, h_ref, d_ref, sems):
+    copies = [
+        pltpu.make_async_copy(traces_ref.at[:, WIN - TAPS :], x_ref, sems.at[0]),
+        pltpu.make_async_copy(taps_ref, h_ref, sems.at[1]),
+        pltpu.make_async_copy(table_ref, d_ref, sems.at[2]),
+    ]
+    for copy in copies:
+        copy.start()
+    for copy in copies:
+        copy.wait()
+    spectra_kernel(x_ref.at[:, :TAPS], x_ref.at[:, TAPS:], h_ref, d_ref, out_ref)
+
+
+def later_window(traces, taps, table):
+    return pl.pallas_call(
+        later_kernel,
+        out_shape=shape((CB, WIN), BF16),
+        in_specs=[pl.BlockSpec(memory_space=pltpu.HBM)] * 3,
+        out_specs=pl.BlockSpec(memory_space=pltpu.VMEM),
+        scratch_shapes=[
+            pltpu.VMEM((CB, WIN + TAPS), F32),
+            pltpu.VMEM((2 * TAPS, TAPS), F32),
+            pltpu.VMEM((HALF, WIN), BF16),
+            pltpu.SemaphoreType.DMA((3,)),
+        ],
+        compiler_params=pltpu.CompilerParams(vmem_limit_bytes=VMEM_LIMIT),
+    )(*[pltpu.with_memory_space_constraint(value, pltpu.HBM) for value in (traces, taps, table)])
+
+
+def first_window(history, traces, taps, table):
     return pl.pallas_call(
         spectra_kernel,
         out_shape=shape((CB, WIN), BF16),
         grid=(1,),
         in_specs=[
-            pl.BlockSpec((CB, TAPS), lambda n: (0, before_at)),
-            pl.BlockSpec((CB, WIN), lambda n: (0, at)),
+            pl.BlockSpec((CB, TAPS), lambda n: (0, 0)),
+            pl.BlockSpec((CB, WIN), lambda n: (0, 0)),
             pl.BlockSpec((2 * TAPS, TAPS), lambda n: (0, 0)),
             pl.BlockSpec((HALF, WIN), lambda n: (0, 0)),
         ],
         out_specs=pl.BlockSpec((CB, WIN), lambda n: (0, 0)),
         compiler_params=pltpu.CompilerParams(vmem_limit_bytes=VMEM_LIMIT),
-    )(before, traces, taps, table)
+    )(history, traces, taps, table)
+
+
+def row_below(blocks):
+    return lax.ppermute(blocks, "row", [(i, i + 1) for i in range(ROWS - 1)])
+
+
+def middle(lists, owners, slabs, send):
+    halves = tuple(shape((n, MEETINGS, CB, CB), BF16) for n in (ROUNDS, PLANE - ROUNDS))
+    chosen_low, chosen_high = call(chosen_kernel, halves, lists)
+    low_shape = shape((ROUNDS, CB, WIDE), BF16)
+    high_shape = shape((PLANE - ROUNDS, CB, WIDE), BF16)
+    low, high, low_swapped, high_swapped = call(
+        whiten_kernel, (low_shape, high_shape, low_shape, high_shape), slabs
+    )
+    last, chosen_low, chosen_high = lax.optimization_barrier((high[-ROUNDS:], chosen_low, chosen_high))
+    below = send(last)
+    sums_shape = shape((ROWS * PLANE, NBIN, WIDE), F32)
+    bins = pltpu.VMEM((SPAN_ROWS, CB), BF16)
+    blocks = pltpu.VMEM((PLANE, CB, WIDE), BF16)
+    sums = call(
+        plane_kernel,
+        sums_shape,
+        owners,
+        chosen_high,
+        low,
+        high,
+        low_swapped,
+        high_swapped,
+        smem=(0,),
+        scratch=(bins, blocks, blocks),
+    )
+    sums = call(
+        below_kernel,
+        sums_shape,
+        owners,
+        chosen_low,
+        low,
+        low_swapped,
+        below,
+        sums,
+        smem=(0,),
+        scratch=(bins, pltpu.VMEM(sums_shape.shape, F32)),
+    )
+    return sums, high
 
 
 def body(traces, owner_map, pair_codes, pair_count):
@@ -341,7 +453,7 @@
 
     history = lax.ppermute(traces[:, -TAPS:], "lag", [(i, i + 1) for i in range(3)])
 
-    spectra1 = windows(traces, WIN // TAPS - 1, traces, 1, taps, table)
+    spectra1 = later_window(traces, taps, table)
     lists_shape = shape((PLANE, LIST_ROWS, CB), jnp.int32)
     lists = call(
         list_kernel,
@@ -354,39 +466,16 @@
     )
     lists, history, spectra1 = lax.optimization_barrier((lists, history, spectra1))
     lists = lax.all_to_all(lists, "plane", 0, 0, tiled=True)
-    spectra0 = windows(history, 0, traces, 0, taps, table)
+    spectra0 = first_window(history, traces, taps, table)
     slabs = call(pack_kernel, shape((PLANE * LAGS, 32, WIDE), BF16), spectra0, spectra1)
     slabs, lists = lax.optimization_barrier((slabs, lists))
     owners = lists[:, 4 * MEETINGS, :MEETINGS]
-    halves = tuple(shape((n, MEETINGS, CB, CB), BF16) for n in (ROUNDS, PLANE - ROUNDS))
-    chosen_low, chosen_high = call(chosen_kernel, halves, lists)
-
     slabs = lax.all_to_all(slabs, ("plane", "lag"), 0, 0, tiled=True)
-    group = call(whiten_kernel, shape((PLANE, CB, WIDE), BF16), slabs)
-    last, chosen_low, chosen_high = lax.optimization_barrier((group[PLANE - ROUNDS :], chosen_low, chosen_high))
-    below = lax.ppermute(last, "row", [(i, i + 1) for i in range(ROWS - 1)])
-
-    sums_shape = shape((ROWS * PLANE, NBIN, WIDE), F32)
-    bins = pltpu.VMEM((SPAN_ROWS, CB), BF16)
-    spare = pltpu.VMEM((PLANE, CB, WIDE), F32)
-    few = pltpu.VMEM((2 * ROUNDS, CB, WIDE), F32)
-    sums = call(plane_kernel, sums_shape, owners, chosen_high, group, smem=(0,), scratch=(bins, spare, spare))
-    sums = call(
-        below_kernel,
-        sums_shape,
-        owners,
-        chosen_low,
-        group,
-        below,
-        sums,
-        smem=(0,),
-        aliases={4: 0},
-        scratch=(bins, few, few),
-    )
-    parts = lax.all_to_all(sums.reshape(PLANE, ROWS * NBIN, WIDE), "plane", 0, 0, tiled=True)
+    sums, _ = middle(lists, owners, slabs, row_below)
+    parts = lax.all_to_all(sums, ("plane", "lag"), 0, 0, tiled=True)
     table = jnp.asarray(inverse_table())
-    lagged = call(lag_kernel, shape((ROWS * LAGS, NBIN, LANES), F32), lag, parts, table, smem=(0,))
-    return jnp.sum(lax.all_to_all(lagged, ("row", "lag"), 0, 0, tiled=True), axis=0, keepdims=True)
+    lagged = call(lag_kernel, shape((ROWS, NBIN, LANES), F32), lag, parts, table, smem=(0,))
+    return jnp.sum(lax.all_to_all(lagged, "row", 0, 0, tiled=True), axis=0, keepdims=True)
 
 
 def solution(mesh):

time: 107 us -> 96.1 us (0.90)
  blocking collectives: 17.6 us -> 7.99 us
  Pallas kernels: 28.2 us -> 22.4 us
  waiting for transfers between devices: 27.4 us -> 32.1 us
  local copies, waits for them, and re-layouts: 5.11 us -> 1.89 us
  starting transfers between devices: 27.6 us -> 30.6 us
    all_to_all x1, blocking collectives: 17.6 us -> 7.99 us  [body(): lax.all_to_all(lagged, 'row', 0, 0, tiled=True)]
    pallas_call x7, Pallas kernels: 24.6 us -> 17.2 us  [call(): pl.pallas_call(kernel, out_shape=out_shape, in_specs=specs, out_specs=out...]
    all_to_all x1, waiting for transfers between devices: 10.1 us -> 13.5 us  [body(): parts = lax.all_to_all(sums, ('plane', 'lag'), 0, 0, tiled=True)]
    unnamed x24 -> x18, local copies, waits for them, and re-layouts: 4.21 us -> 0.87 us
    all_to_all x1, starting transfers between devices: 5.21 us -> 7.1 us  [body(): slabs = lax.all_to_all(slabs, ('plane', 'lag'), 0, 0, tiled=True)]
    pallas_call x2, Pallas kernels: 3.66 us -> 5.14 us  [the longest x1 3.31 us: later_window(): pl.pallas_call(later_kernel, out_shape=shape((CB, WIN), BF16), in_specs=[...]
    all_to_all x1, waiting for transfers between devices: 12.9 us -> 14.1 us  [body(): slabs = lax.all_to_all(slabs, ('plane', 'lag'), 0, 0, tiled=True)]
  transfers between devices with their start and end apart: 5 -> 5, of which waited for: 3 -> 3; matrix products, arithmetic and copies ran while one was open for 0% -> 0% of each run, Pallas kernels for 20% -> 17%
where the time goes in v5:
time: 96.1 us; the launch traced here: 95.7 us
  waiting for transfers between devices  32.1 us (33%)
  starting transfers between devices  30.6 us (32%)
  Pallas kernels  22.4 us (23%)
  blocking collectives  7.99 us (8%)
  local copies, waits for them, and re-layouts  1.89 us (2%)
    pallas_call x7, Pallas kernels, call(): pl.pallas_call(kernel, out_shape=out_shape, in_specs=specs, out_specs=out...  17.2 us
    all_to_all x1, waiting for transfers between devices, body(): slabs = lax.all_to_all(slabs, ('plane', 'lag'), 0, 0, tiled=True)  14.1 us
    all_to_all x1, waiting for transfers between devices, body(): parts = lax.all_to_all(sums, ('plane', 'lag'), 0, 0, tiled=True)  13.5 us
    ppermute x1, starting transfers between devices, body(): lax.ppermute(traces[:, -TAPS:], 'lag', [(i, i + 1) for i in range(3)])  10.2 us
    all_to_all x1, blocking collectives, body(): lax.all_to_all(lagged, 'row', 0, 0, tiled=True)  7.99 us
    all_to_all x1, starting transfers between devices, body(): slabs = lax.all_to_all(slabs, ('plane', 'lag'), 0, 0, tiled=True)  7.1 us
    all_to_all x1, starting transfers between devices, body(): lists = lax.all_to_all(lists, 'plane', 0, 0, tiled=True)  5.49 us
    all_to_all x1, starting transfers between devices, body(): parts = lax.all_to_all(sums, ('plane', 'lag'), 0, 0, tiled=True)  4.58 us
  transfers between devices with their start and end apart: 5, of which 3 were waited for; matrix products, arithmetic and copies ran while one was open for 0% of the time, Pallas kernels for 17%

profile of v5, /device:TPU:1, one launch (start us, length us, event | category | flops | bytes accessed | tf_op | source)
XLA Modules:
  0.0 95.7 jit_solution(8086336793097234445)
XLA Ops:
  0.0 0.0 copy-start.5
  0.0 0.0 copy-start.1
  0.0 0.0 copy-start
  0.0 0.0 copy-start.7
  0.0 0.0 copy-start.8
  0.0 0.0 copy-start.6
  0.0 1.0 %slice.9 = f32[128,128]{1,0:T(8,128)S(1)} slice(f32[128,2048]{1,0:T(8,128)} %x_ref.1), slice={[0:128], [1920:2048]} | slice | bytes 131072 | tf_op jit(solution)/shard_map/slice | solution.py:454
  1.0 10.2 %collective-permute-start = (f32[128,128]{1,0:T(8,128)S(1)}, f32[128,128]{1,0:T(8,128)S(1)}, u32[]{:S(2)}, u32[]{:S(2)}) collective-permute-start(f32[128,128]{1,0:T(8,128)S(1)} %slice.9), channel_id=1, source_target_pairs={{0,1},{1,2},{2,3},{4,5},{5,6},{6,7},{8,9},{9,10},{10,11},{12,13},{... | collective-permute-start | bytes 196616 | tf_op jit(solution)/shard_map/ppermute | solution.py:454
  11.2 3.3 %shard_map.74.s1_ref = bf16[128,1024]{1,0:T(8,128)(2,1)S(1)} custom-call(f32[128,2048]{1,0:T(8,128)} %x_ref.1, f32[256,128]{1,0:T(8,128)} %constant.23.clone.taps_ref, bf16[512,1024]{1,0:T(8,128)(2,1)} %constant.24.clone.table_ref), custom_call_target="tpu_custom_call" | custom-call | tf_op jit(solution)/shard_map/pallas_call | solution.py:373
  14.6 0.0 copy-done.7
  14.6 0.0 copy-done.8
  14.6 0.0 copy-done.6
  14.6 0.8 shard_map.73
  15.4 0.0 collective-permute-done.hist_ref
  15.4 5.5 %all-to-all-start = ((s32[16,24,128]{2,1,0:T(8,128)}), s32[16,24,128]{2,1,0:T(8,128)S(1)}, u32[]{:S(2)}, u32[]{:S(2)}) async-start(s32[16,24,128]{2,1,0:T(8,128)} %shard_map.73), calls=%async_computation | async-start | bytes 393216 | tf_op jit(solution)/shard_map/all_to_all | solution.py:468
  20.9 0.0 copy-done.5
  20.9 0.0 copy-done.1
  20.9 0.0 copy-done
  20.9 1.8 %shard_map.75.s0_ref = bf16[128,1024]{1,0:T(8,128)(2,1)S(1)} custom-call(f32[128,128]{1,0:T(8,128)S(1)} %collective-permute-done.hist_ref, f32[128,2048]{1,0:T(8,128)S(1)} %copy-done, f32[256,128]{1,0:T(8,128)S(1)} %copy-done.5, bf16[512,1024]{1,0:T(8,128)(2,1)S(1)} %copy-done.1), custom_call_target="tpu_custom_call" | custom-call | tf_op jit(solution)/shard_map/pallas_call | solution.py:389
  22.7 2.0 %shard_map.76 = bf16[64,32,128]{2,1,0:T(8,128)(2,1)} custom-call(bf16[128,1024]{1,0:T(8,128)(2,1)S(1)} %shard_map.75.s0_ref, bf16[128,1024]{1,0:T(8,128)(2,1)S(1)} %shard_map.74.s1_ref), custom_call_target="tpu_custom_call" | custom-call | tf_op jit(solution)/shard_map/pallas_call | solution.py:95
  24.7 4.4 %all-to-all-done.lists_ref = s32[16,24,128]{2,1,0:T(8,128)S(1)} async-done(((s32[16,24,128]{2,1,0:T(8,128)}), s32[16,24,128]{2,1,0:T(8,128)S(1)}, u32[]{:S(2)}, u32[]{:S(2)}) %all-to-all-start) | async-done | bytes 196640 | tf_op jit(solution)/shard_map/all_to_all | solution.py:468
  29.2 7.1 %all-to-all-start.1 = ((bf16[64,32,128]{2,1,0:T(8,128)(2,1)}), bf16[64,32,128]{2,1,0:T(8,128)(2,1)S(1)}, u32[]{:S(2)}, u32[]{:S(2)}) async-start(bf16[64,32,128]{2,1,0:T(8,128)(2,1)} %shard_map.76), calls=%async_computation.1 | async-start | bytes 1048576 | tf_op jit(solution)/shard_map/all_to_all | solution.py:473
  36.3 4.1 %shard_map.78 = (bf16[4,5,128,128]{3,2,1,0:T(8,128)(2,1)S(1)}, bf16[12,5,128,128]{3,2,1,0:T(8,128)(2,1)S(1)}) custom-call(s32[16,24,128]{2,1,0:T(8,128)S(1)} %all-to-all-done.lists_ref), custom_call_target="tpu_custom_call" | custom-call | tf_op jit(solution)/shard_map/pallas_call | solution.py:95
  40.3 0.0 copy-start.3
  40.4 0.8 copy-done.3
  41.2 14.1 %all-to-all-done.1.slab_ref = bf16[64,32,128]{2,1,0:T(8,128)(2,1)S(1)} async-done(((bf16[64,32,128]{2,1,0:T(8,128)(2,1)}), bf16[64,32,128]{2,1,0:T(8,128)(2,1)S(1)}, u32[]{:S(2)}, u32[]{:S(2)}) %all-to-all-start.1) | async-done | bytes 524320 | tf_op jit(solution)/shard_map/all_to_all | solution.py:473
  55.3 0.0 copy-start.4
  55.3 1.9 %shard_map.77 = (bf16[4,128,128]{2,1,0:T(8,128)(2,1)S(1)}, bf16[12,128,128]{2,1,0:T(8,128)(2,1)S(1)}, bf16[4,128,128]{2,1,0:T(8,128)(2,1)S(1)}, bf16[12,128,128]{2,1,0:T(8,128)(2,1)S(1)}) custom-call(bf16[64,32,128]{2,1,0:T(8,128)(2,1)S(1)} %all-to-all-done.1.slab_ref), custom_call_target="tpu_custom_call" | custom-call | tf_op jit(solution)/shard_map/pallas_call | solution.py:95
  57.2 3.2 %collective-permute-start.1 = (bf16[4,128,128]{2,1,0:T(8,128)(2,1)S(1)}, bf16[4,128,128]{2,1,0:T(8,128)(2,1)S(1)}, u32[]{:S(2)}, u32[]{:S(2)}) collective-permute-start(bf16[4,128,128]{2,1,0:T(8,128)(2,1)S(1)} %slice.11), channel_id=1, source_target_pairs={{0,64},{64,128},{128,192},{1,65},{65,129},{129,193},{2,66},{66,130... | collective-permute-start | bytes 393224 | tf_op jit(solution)/shard_map/ppermute | solution.py:405
  60.4 0.0 copy-start.2
  60.5 4.6 %shard_map.79.sums_ref = f32[64,8,128]{2,1,0:T(8,128)S(1)} custom-call(s32[16,5]{1,0:T(8,128)S(1)} %bitcast.6, bf16[12,5,128,128]{3,2,1,0:T(8,128)(2,1)S(1)} %get-tuple-element.31.chosen_ref, bf16[4,128,128]{2,1,0:T(8,128)(2,1)S(1)} %get-tuple-element.28.low_ref.group_ref, bf16[12,128,128]{2,1,0:T(8,128)(2,1)S(1)} %get-tuple-element.24.high_ref, ...), custom_call_target="tpu_custom_call" | custom-call | tf_op jit(solution)/shard_map/pallas_call | solution.py:95
  65.1 0.0 collective-permute-done.1.below_ref
  65.1 0.0 copy-done.4
  65.1 2.8 %shard_map.80 = f32[64,8,128]{2,1,0:T(8,128)} custom-call(s32[16,5]{1,0:T(8,128)S(1)} %bitcast.7, bf16[4,5,128,128]{3,2,1,0:T(8,128)(2,1)S(1)} %copy-done.4, bf16[4,128,128]{2,1,0:T(8,128)(2,1)S(1)} %get-tuple-element.28.low_ref.group_ref, bf16[4,128,128]{2,1,0:T(8,128)(2,1)S(1)} %get-tuple-element.29.low_swapped_ref.swapped_ref, ...), custom_call_target="tpu_custom_call" | custom-call | tf_op jit(solution)/shard_map/pallas_call | solution.py:95
  67.9 4.6 %all-to-all-start.2 = ((f32[64,8,128]{2,1,0:T(8,128)}), f32[64,8,128]{2,1,0:T(8,128)S(1)}, u32[]{:S(2)}, u32[]{:S(2)}) async-start(f32[64,8,128]{2,1,0:T(8,128)} %shard_map.80), calls=%async_computation.2 | async-start | bytes 524288 | tf_op jit(solution)/shard_map/all_to_all | solution.py:475
  72.5 13.5 %all-to-all-done.2.parts_ref = f32[64,8,128]{2,1,0:T(8,128)S(1)} async-done(((f32[64,8,128]{2,1,0:T(8,128)}), f32[64,8,128]{2,1,0:T(8,128)S(1)}, u32[]{:S(2)}, u32[]{:S(2)}) %all-to-all-start.2) | async-done | bytes 262176 | tf_op jit(solution)/shard_map/all_to_all | solution.py:475
  86.1 0.0 copy-done.2
  86.1 1.0 %shard_map.81 = f32[4,8,256]{2,1,0:T(8,128)S(1)} custom-call(s32[1]{0:T(128)} %bitcast.lag_ref, f32[64,8,128]{2,1,0:T(8,128)S(1)} %all-to-all-done.2.parts_ref, f32[1024,256]{1,0:T(8,128)S(1)} %copy-done.2), custom_call_target="tpu_custom_call" | custom-call | tf_op jit(solution)/shard_map/pallas_call | solution.py:95
  87.1 8.0 %all_to_all.20 = f32[4,8,256]{2,1,0:T(8,128)S(1)} all-to-all(f32[4,8,256]{2,1,0:T(8,128)S(1)} %shard_map.81), channel_id=1, replica_groups=mesh['row'=4,'plane'=16,'lag'=4] {'row'}, dimensions={0} | all-to-all | bytes 65536 | tf_op jit(solution)/shard_map/all_to_all | solution.py:478
  95.1 0.6 reduce_sum.9
  (2 shorter events, 0.0 us)
Async XLA Ops:
  0.0 20.9 %copy-start.5 = (f32[256,128]{1,0:T(8,128)S(1)}, f32[256,128]{1,0:T(8,128)}, u32[]{:S(2)}) copy-start(f32[256,128]{1,0:T(8,128)} %constant.23.clone.taps_ref) | copy-start | bytes 393220
  0.0 20.9 %copy-start.1 = (bf16[512,1024]{1,0:T(8,128)(2,1)S(1)}, bf16[512,1024]{1,0:T(8,128)(2,1)}, u32[]{:S(2)}) copy-start(bf16[512,1024]{1,0:T(8,128)(2,1)} %constant.24.clone.table_ref) | copy-start | bytes 3145732
  0.0 20.9 %copy-start = (f32[128,2048]{1,0:T(8,128)S(1)}, f32[128,2048]{1,0:T(8,128)}, u32[]{:S(2)}) copy-start(f32[128,2048]{1,0:T(8,128)} %x_ref.1) | copy-start | bytes 3145732
  0.0 14.6 %copy-start.7 = (s32[5,1]{0,1:T(1,128)S(1)}, s32[5,1]{0,1:T(1,128)}, u32[]{:S(2)}) copy-start(s32[5,1]{0,1:T(1,128)} %param.10) | copy-start | bytes 64
  0.0 14.6 %copy-start.8 = (s32[5,1]{0,1:T(1,128)S(1)}, s32[5,1]{0,1:T(1,128)}, u32[]{:S(2)}) copy-start(s32[5,1]{0,1:T(1,128)} %param.8) | copy-start | bytes 64
  0.0 14.6 %copy-start.6 = (s32[5,512]{1,0:T(8,128)S(1)}, s32[5,512]{1,0:T(8,128)}, u32[]{:S(2)}) copy-start(s32[5,512]{1,0:T(8,128)} %codes_ref.1) | copy-start | bytes 30724
  1.0 14.3 %collective-permute-start = (f32[128,128]{1,0:T(8,128)S(1)}, f32[128,128]{1,0:T(8,128)S(1)}, u32[]{:S(2)}, u32[]{:S(2)}) collective-permute-start(f32[128,128]{1,0:T(8,128)S(1)} %slice.9), channel_id=1, source_target_pairs={{0,1},{1,2},{2,3},{4,5},{5,6},{6,7},{8,9},{9,10},{10,11},{12,13},{... | collective-permute-start | bytes 196616 | tf_op jit(solution)/shard_map/ppermute | solution.py:454
  15.4 13.8 %all-to-all-start = ((s32[16,24,128]{2,1,0:T(8,128)}), s32[16,24,128]{2,1,0:T(8,128)S(1)}, u32[]{:S(2)}, u32[]{:S(2)}) async-start(s32[16,24,128]{2,1,0:T(8,128)} %shard_map.73), calls=%async_computation | async-start | bytes 393216 | tf_op jit(solution)/shard_map/all_to_all | solution.py:468
  29.2 26.1 %all-to-all-start.1 = ((bf16[64,32,128]{2,1,0:T(8,128)(2,1)}), bf16[64,32,128]{2,1,0:T(8,128)(2,1)S(1)}, u32[]{:S(2)}, u32[]{:S(2)}) async-start(bf16[64,32,128]{2,1,0:T(8,128)(2,1)} %shard_map.76), calls=%async_computation.1 | async-start | bytes 1048576 | tf_op jit(solution)/shard_map/all_to_all | solution.py:473
  40.3 0.8 copy-start.3
  55.3 9.8 %copy-start.4 = (bf16[4,5,128,128]{3,2,1,0:T(8,128)(2,1)S(1)}, bf16[4,5,128,128]{3,2,1,0:T(8,128)(2,1)}, u32[]{:S(2)}) copy-start(bf16[4,5,128,128]{3,2,1,0:T(8,128)(2,1)} %copy-done.3) | copy-start | bytes 1966084
  57.2 7.9 %collective-permute-start.1 = (bf16[4,128,128]{2,1,0:T(8,128)(2,1)S(1)}, bf16[4,128,128]{2,1,0:T(8,128)(2,1)S(1)}, u32[]{:S(2)}, u32[]{:S(2)}) collective-permute-start(bf16[4,128,128]{2,1,0:T(8,128)(2,1)S(1)} %slice.11), channel_id=1, source_target_pairs={{0,64},{64,128},{128,192},{1,65},{65,129},{129,193},{2,66},{66,130... | collective-permute-start | bytes 393224 | tf_op jit(solution)/shard_map/ppermute | solution.py:405
  60.4 25.6 %copy-start.2 = (f32[1024,256]{1,0:T(8,128)S(1)}, f32[1024,256]{1,0:T(8,128)}, u32[]{:S(2)}) copy-start(f32[1024,256]{1,0:T(8,128)} %constant.25.clone.table_ref) | copy-start | bytes 3145732
  67.9 18.1 %all-to-all-start.2 = ((f32[64,8,128]{2,1,0:T(8,128)}), f32[64,8,128]{2,1,0:T(8,128)S(1)}, u32[]{:S(2)}, u32[]{:S(2)}) async-start(f32[64,8,128]{2,1,0:T(8,128)} %shard_map.80), calls=%async_computation.2 | async-start | bytes 524288 | tf_op jit(solution)/shard_map/all_to_all | solution.py:475

commit v6 on v5

--- a/solution.py
+++ b/solution.py
@@ -26,7 +26,8 @@
 LAGS = 4
 WIDE = 128
 BAND = 8
-LIST_ROWS = 24
+DATA_ROWS = 32
+SLAB_ROWS = 40
 
 BAND_LOW = 0.02
 BAND_HIGH = 0.48
@@ -179,7 +180,29 @@
     out_ref[...] = (first + turn * second).astype(BF16)
 
 
-def pack_kernel(s0_ref, s1_ref, out_ref):
+def list_rows(place_ref, count_ref, owner_ref, codes_ref):
+    lane = lanes()
+    start = pl.multiple_of(place_ref[1] * WIDE, WIDE)
+    codes = codes_ref[:, pl.ds(start, WIDE)]
+    exponent = codes >> 8
+    value = 1.0 + (codes & (CB - 1)).astype(F32) * (1.0 / CB)
+    for bit in range(6):
+        value = jnp.where(((exponent >> bit) & 1) == 1, value * 2.0 ** (1 << bit), value)
+    value = jnp.where(((codes >> 7) & 1) == 1, -value, value)
+    rows = []
+    owners = jnp.zeros((1, WIDE), F32)
+    for o in range(MEETINGS):
+        live = jnp.where(place_ref[0] >= o, count_ref[:, o : o + 1], 0)
+        rows.append(jnp.where(lane + start < live, value[o : o + 1], 0.0))
+        owner = owner_ref[:, o : o + 1]
+        spot = (owner & (PLANE - 1)) * ROWS + (owner >> 4)
+        owners = jnp.where(lane == o, spot.astype(F32), owners)
+    rows = rows + [owners] + [jnp.zeros((1, WIDE), F32)] * (SLAB_ROWS - DATA_ROWS - MEETINGS - 1)
+    return jnp.concatenate(rows, axis=0).astype(BF16)
+
+
+def pack_kernel(place_ref, count_ref, owner_ref, codes_ref, s0_ref, s1_ref, out_ref):
+    lists = list_rows(place_ref, count_ref, owner_ref, codes_ref)
     for c in range(WIN // WIDE):
         cols = slice(c * WIDE, (c + 1) * WIDE)
         pieces = []
@@ -187,10 +210,11 @@
             for ref in (s0_ref, s1_ref):
                 pieces.append(ref[g * 32 : (g + 1) * 32, cols].astype(F32))
         for e, value in enumerate(transpose_pieces(pieces, 2 * BAND)):
-            out_ref[c * 8 + e] = value.astype(BF16)
-
-
-def whiten_kernel(slab_ref, low_ref, high_ref, low_swapped_ref, high_swapped_ref):
+            out_ref[c * 8 + e, :DATA_ROWS, :] = value.astype(BF16)
+            out_ref[c * 8 + e, DATA_ROWS:, :] = lists
+
+
+def whiten_kernel(slab_ref, out_ref, swapped_ref, last_ref):
     order = order_table()
     both = fold_table(1.0, 1.0)
     both = jnp.concatenate([both, both], axis=0)
@@ -199,7 +223,7 @@
     for first in range(0, PLANE, batch):
         rows = []
         for p in range(first, first + batch):
-            rows.append(jnp.concatenate([slab_ref[p * LAGS + n] for n in range(LAGS)], axis=1))
+            rows.append(jnp.concatenate([slab_ref[p * LAGS + n, :DATA_ROWS, :] for n in range(LAGS)], axis=1))
         values = jnp.dot(jnp.concatenate(rows, axis=0), order, preferred_element_type=F32)
         values = jnp.concatenate([values[:, g * WIDE : (g + 1) * WIDE] for g in range(4)], axis=0)
         high, low = halves_of(values * values)
@@ -207,51 +231,38 @@
         whitened = (values * lax.rsqrt(power * (1.0 / WINDOWS) + WATER)).astype(BF16)
         turned = jnp.dot(whitened, swap, preferred_element_type=F32).astype(BF16)
         for n in range(batch):
-            at_block = first + n if first < ROUNDS else first + n - ROUNDS
-            out_ref = low_ref if first < ROUNDS else high_ref
-            swapped_ref = low_swapped_ref if first < ROUNDS else high_swapped_ref
             for g in range(4):
                 at = (g * batch + n) * 32
-                out_ref[at_block, g * 32 : (g + 1) * 32, :] = whitened[at : at + 32]
-                swapped_ref[at_block, g * 32 : (g + 1) * 32, :] = turned[at : at + 32]
-
-
-def list_kernel(blk_ref, count_ref, owner_ref, codes_ref, out_ref):
-    lane = lax.broadcasted_iota(jnp.int32, (1, CB), 1)
-    rows = []
-    owners = jnp.zeros((1, CB), jnp.int32)
-    for o in range(MEETINGS):
-        live = jnp.where(blk_ref[0] >= o, count_ref[:, o : o + 1], 0)
-        for n in range(4):
-            rows.append(jnp.where(lane + n * CB < live, codes_ref[o : o + 1, n * CB : (n + 1) * CB], -1))
-        owner = owner_ref[:, o : o + 1]
-        owners = jnp.where(lane == o, (owner & (PLANE - 1)) * ROWS + (owner >> 4), owners)
-    rows = rows + [owners] + [jnp.zeros((1, CB), jnp.int32)] * (LIST_ROWS - len(rows) - 1)
-    block = jnp.concatenate(rows, axis=0)
-    for p in range(PLANE):
-        out_ref[p] = block
-
-
-def chosen_kernel(lists_ref, low_ref, high_ref):
-    row = lax.broadcasted_iota(jnp.int32, (CB, PCAP), 0)
-
-    def fill(p, ref, at):
+                out_ref[first + n, g * 32 : (g + 1) * 32, :] = whitened[at : at + 32]
+                swapped_ref[first + n, g * 32 : (g + 1) * 32, :] = turned[at : at + 32]
+                if first == PLANE - ROUNDS:
+                    last_ref[n, g * 32 : (g + 1) * 32, :] = whitened[at : at + 32]
+
+
+def chosen_kernel(slab_ref, out_ref, owner_ref):
+    row = lax.broadcasted_iota(jnp.int32, (CB, PCAP), 0).astype(F32)
+
+    def one(p, carry):
+        value = jnp.concatenate([slab_ref[p * LAGS + n, DATA_ROWS:, :] for n in range(LAGS)], axis=1).astype(F32)
+        owner_ref[pl.ds(p, 1), :] = value[MEETINGS : MEETINGS + 1, :WIDE].astype(jnp.int32)
+        odd = jnp.where(value < 0.0, 1.0, 0.0)
+        size = jnp.abs(value)
+        live = size > 0.0
+        exponent = jnp.zeros(value.shape, F32)
+        for bit in (5, 4, 3, 2, 1, 0):
+            large = size >= 2.0 ** (1 << bit)
+            size = jnp.where(large, size * 2.0 ** -(1 << bit), size)
+            exponent = jnp.where(large, exponent + 2.0**bit, exponent)
+        first = jnp.where(live, 2.0 * exponent + odd, -1.0)
+        second = (size - 1.0) * CB
         for o in range(MEETINGS):
-            pieces = [lists_ref[p, o * 4 + n : o * 4 + n + 1, :] for n in range(4)]
-            codes = jnp.concatenate(pieces, axis=1)
-            pick_first = jnp.where(row == (codes >> 7), 1.0, 0.0).astype(BF16)
-            pick_second = jnp.where(row == (codes & (CB - 1)), 1.0, 0.0).astype(BF16)
+            pick_first = jnp.where(row == first[o : o + 1], 1.0, 0.0).astype(BF16)
+            pick_second = jnp.where(row == second[o : o + 1], 1.0, 0.0).astype(BF16)
             chosen = lax.dot_general(pick_first, pick_second, (((1,), (1,)), ((), ())), preferred_element_type=F32)
-            ref[at, o] = chosen.astype(BF16)
-
-    for p in range(ROUNDS):
-        fill(p, low_ref, p)
-
-    def one(p, carry):
-        fill(p, high_ref, p - ROUNDS)
+            out_ref[p, o] = chosen.astype(BF16)
         return carry
 
-    lax.fori_loop(ROUNDS, PLANE, one, 0, unroll=4)
+    lax.fori_loop(0, PLANE, one, 0, unroll=4)
 
 
 def fill_bins(bins_ref):
@@ -296,37 +307,24 @@
         out_ref[spot] = out_ref[spot] + found
 
 
-def plane_kernel(
-    owner_ref, chosen_ref, low_ref, high_ref, low_swapped_ref, high_swapped_ref, out_ref, bins_ref, group_ref, swapped_ref
+def meetings_kernel(
+    owner_ref, chosen_ref, group_ref, swapped_ref, below_ref, out_ref, bins_ref, all_ref, turned_ref, total_ref
 ):
-    out_ref[...] = jnp.zeros(out_ref.shape, F32)
-    fill_bins(bins_ref)
-    group_ref[:ROUNDS] = low_ref[...]
-    group_ref[ROUNDS:] = high_ref[...]
-    swapped_ref[:ROUNDS] = low_swapped_ref[...]
-    swapped_ref[ROUNDS:] = high_swapped_ref[...]
-
-    def one(p, carry):
-        partners = [(group_ref[p - o], swapped_ref[p - o]) for o in range(MEETINGS)]
-        meet(out_ref, owner_ref, bins_ref, chosen_ref, p - ROUNDS, group_ref[p], partners, p)
-        return carry
-
-    lax.fori_loop(ROUNDS, PLANE, one, 0, unroll=4)
-
-
-def below_kernel(owner_ref, chosen_ref, group_ref, swapped_ref, below_ref, sums_ref, out_ref, bins_ref, total_ref):
-    total_ref[...] = sums_ref[...]
+    total_ref[...] = jnp.zeros(total_ref.shape, F32)
     fill_bins(bins_ref)
     swap = swap_table()
-    under = []
     for n in range(ROUNDS):
-        block = below_ref[n]
-        under.append((block, jnp.dot(block, swap, preferred_element_type=F32).astype(BF16)))
-    for p in range(ROUNDS):
-        partners = [
-            (group_ref[p - o], swapped_ref[p - o]) if p >= o else under[p - o + ROUNDS] for o in range(MEETINGS)
-        ]
+        all_ref[n] = below_ref[n]
+        turned_ref[n] = jnp.dot(below_ref[n], swap, preferred_element_type=F32).astype(BF16)
+    all_ref[ROUNDS:] = group_ref[...]
+    turned_ref[ROUNDS:] = swapped_ref[...]
+
+    def one(p, carry):
+        partners = [(all_ref[p + ROUNDS - o], turned_ref[p + ROUNDS - o]) for o in range(MEETINGS)]
         meet(total_ref, owner_ref, bins_ref, chosen_ref, p, group_ref[p], partners, p)
+        return carry
+
+    lax.fori_loop(0, PLANE, one, 0, unroll=4)
     row_id = lax.broadcasted_iota(jnp.int32, (NBIN, WIDE), 0)
     own_piece = (lanes() >> 4) == row_id
     for n in range(PLANE):
@@ -405,76 +403,56 @@
     return lax.ppermute(blocks, "row", [(i, i + 1) for i in range(ROWS - 1)])
 
 
-def middle(lists, owners, slabs, send):
-    halves = tuple(shape((n, MEETINGS, CB, CB), BF16) for n in (ROUNDS, PLANE - ROUNDS))
-    chosen_low, chosen_high = call(chosen_kernel, halves, lists)
-    low_shape = shape((ROUNDS, CB, WIDE), BF16)
-    high_shape = shape((PLANE - ROUNDS, CB, WIDE), BF16)
-    low, high, low_swapped, high_swapped = call(
-        whiten_kernel, (low_shape, high_shape, low_shape, high_shape), slabs
+def middle(slabs, send):
+    blocks = (PLANE, CB, WIDE)
+    group, swapped, last = call(
+        whiten_kernel, (shape(blocks, BF16), shape(blocks, BF16), shape((ROUNDS, CB, WIDE), BF16)), slabs
     )
-    last, chosen_low, chosen_high = lax.optimization_barrier((high[-ROUNDS:], chosen_low, chosen_high))
     below = send(last)
-    sums_shape = shape((ROWS * PLANE, NBIN, WIDE), F32)
-    bins = pltpu.VMEM((SPAN_ROWS, CB), BF16)
-    blocks = pltpu.VMEM((PLANE, CB, WIDE), BF16)
-    sums = call(
-        plane_kernel,
-        sums_shape,
+    chosen, owners = call(
+        chosen_kernel, (shape((PLANE, MEETINGS, CB, CB), BF16), shape((PLANE, WIDE), jnp.int32)), slabs
+    )
+    sums_shape = (ROWS * PLANE, NBIN, WIDE)
+    more = pltpu.VMEM((PLANE + ROUNDS, CB, WIDE), BF16)
+    return call(
+        meetings_kernel,
+        shape(sums_shape, F32),
         owners,
-        chosen_high,
-        low,
-        high,
-        low_swapped,
-        high_swapped,
+        chosen,
+        group,
+        swapped,
+        below,
         smem=(0,),
-        scratch=(bins, blocks, blocks),
+        scratch=(pltpu.VMEM((SPAN_ROWS, CB), BF16), more, more, pltpu.VMEM(sums_shape, F32)),
     )
-    sums = call(
-        below_kernel,
-        sums_shape,
-        owners,
-        chosen_low,
-        low,
-        low_swapped,
-        below,
-        sums,
-        smem=(0,),
-        scratch=(bins, pltpu.VMEM(sums_shape.shape, F32)),
-    )
-    return sums, high
 
 
 def body(traces, owner_map, pair_codes, pair_count):
-    blk = (lax.axis_index("row") * PLANE + lax.axis_index("plane")).astype(jnp.int32).reshape(1)
-    lag = lax.axis_index("lag").astype(jnp.int32).reshape(1)
+    blk = (lax.axis_index("row") * PLANE + lax.axis_index("plane")).astype(jnp.int32)
+    lag = lax.axis_index("lag").astype(jnp.int32)
     taps = jnp.asarray(filter_table())
     table = jnp.asarray(transform_table())
 
     history = lax.ppermute(traces[:, -TAPS:], "lag", [(i, i + 1) for i in range(3)])
 
     spectra1 = later_window(traces, taps, table)
-    lists_shape = shape((PLANE, LIST_ROWS, CB), jnp.int32)
-    lists = call(
-        list_kernel,
-        lists_shape,
-        blk,
+    spectra0 = first_window(history, traces, taps, table)
+    slabs = call(
+        pack_kernel,
+        shape((PLANE * LAGS, SLAB_ROWS, WIDE), BF16),
+        jnp.stack([blk, lag]),
         pair_count.reshape(1, MEETINGS),
         owner_map.reshape(1, MEETINGS),
         pair_codes,
+        spectra0,
+        spectra1,
         smem=(0,),
     )
-    lists, history, spectra1 = lax.optimization_barrier((lists, history, spectra1))
-    lists = lax.all_to_all(lists, "plane", 0, 0, tiled=True)
-    spectra0 = first_window(history, traces, taps, table)
-    slabs = call(pack_kernel, shape((PLANE * LAGS, 32, WIDE), BF16), spectra0, spectra1)
-    slabs, lists = lax.optimization_barrier((slabs, lists))
-    owners = lists[:, 4 * MEETINGS, :MEETINGS]
     slabs = lax.all_to_all(slabs, ("plane", "lag"), 0, 0, tiled=True)
-    sums, _ = middle(lists, owners, slabs, row_below)
+    sums = middle(slabs, row_below)
     parts = lax.all_to_all(sums, ("plane", "lag"), 0, 0, tiled=True)
     table = jnp.asarray(inverse_table())
-    lagged = call(lag_kernel, shape((ROWS, NBIN, LANES), F32), lag, parts, table, smem=(0,))
+    lagged = call(lag_kernel, shape((ROWS, NBIN, LANES), F32), lag.reshape(1), parts, table, smem=(0,))
     return jnp.sum(lax.all_to_all(lagged, "row", 0, 0, tiled=True), axis=0, keepdims=True)
 
 

time: 96.1 us -> 92.3 us (0.960)
  blocking collectives: 7.99 us -> 57.1 us
  waiting for transfers between devices: 32.1 us -> 0.01 us
  starting transfers between devices: 30.6 us -> 13.5 us
  Pallas kernels: 22.4 us -> 19.5 us
    all_to_all x0 -> x2, blocking collectives: none -> 48.3 us  [the longest x1 30.3 us: body(): slabs = lax.all_to_all(slabs, ('plane', 'lag'), 0, 0, tiled=True)]
    all_to_all x3 -> x0, waiting for transfers between devices: 32 us -> none  [the longest x1 14.1 us: body(): slabs = lax.all_to_all(slabs, ('plane', 'lag'), 0, 0, tiled=True)]
    all_to_all x3 -> x0, starting transfers between devices: 17.2 us -> none  [the longest x1 7.1 us: body(): slabs = lax.all_to_all(slabs, ('plane', 'lag'), 0, 0, tiled=True)]
    pallas_call x7 -> x5, Pallas kernels: 17.2 us -> 14.4 us  [call(): pl.pallas_call(kernel, out_shape=out_shape, in_specs=specs, out_specs=out...]
  transfers between devices with their start and end apart: 5 -> 2, of which waited for: 3 -> 0; matrix products, arithmetic and copies ran while one was open for 0% -> 0% of each run, Pallas kernels for 17% -> 7%
where the time goes in v6:
time: 92.3 us; the launch traced here: 92 us
  blocking collectives  57.1 us (62%)
  Pallas kernels  19.5 us (21%)
  starting transfers between devices  13.5 us (15%)
  local copies, waits for them, and re-layouts  1.03 us (1%)
    all_to_all x1, blocking collectives, body(): slabs = lax.all_to_all(slabs, ('plane', 'lag'), 0, 0, tiled=True)  30.3 us
    all_to_all x1, blocking collectives, body(): parts = lax.all_to_all(sums, ('plane', 'lag'), 0, 0, tiled=True)  18 us
    pallas_call x5, Pallas kernels, call(): pl.pallas_call(kernel, out_shape=out_shape, in_specs=specs, out_specs=out...  14.4 us
    ppermute x1, starting transfers between devices, body(): lax.ppermute(traces[:, -TAPS:], 'lag', [(i, i + 1) for i in range(3)])  10.2 us
    all_to_all x1, blocking collectives, body(): lax.all_to_all(lagged, 'row', 0, 0, tiled=True)  8.76 us
    ppermute x1, starting transfers between devices, row_below(): return lax.ppermute(blocks, 'row', [(i, i + 1) for i in range(ROWS - 1)])  3.34 us
    pallas_call x1, Pallas kernels, later_window(): pl.pallas_call(later_kernel, out_shape=shape((CB, WIN), BF16), in_specs=[...  3.31 us
  transfers between devices with their start and end apart: 2, of which 0 were waited for; matrix products, arithmetic and copies ran while one was open for 0% of the time, Pallas kernels for 7%

profile of v6, /device:TPU:1, one launch (start us, length us, event | category | flops | bytes accessed | tf_op | source)
XLA Modules:
  0.0 92.0 jit_solution(9343587496284015209)
XLA Ops:
  0.0 0.0 copy-start.1
  0.0 0.0 copy-start.3
  0.0 0.0 copy-start
  0.0 0.0 copy-start.5
  0.0 0.0 copy-start.4
  0.0 0.0 copy-start.6
  0.0 1.0 %slice.3 = f32[128,128]{1,0:T(8,128)S(1)} slice(f32[128,2048]{1,0:T(8,128)} %traces_ref.1), slice={[0:128], [1920:2048]} | slice | bytes 131072 | tf_op jit(solution)/shard_map/slice | solution.py:436
  1.0 10.2 %collective-permute-start = (f32[128,128]{1,0:T(8,128)S(1)}, f32[128,128]{1,0:T(8,128)S(1)}, u32[]{:S(2)}, u32[]{:S(2)}) collective-permute-start(f32[128,128]{1,0:T(8,128)S(1)} %slice.3), channel_id=1, source_target_pairs={{0,1},{1,2},{2,3},{4,5},{5,6},{6,7},{8,9},{9,10},{10,11},{12,13},{... | collective-permute-start | bytes 196616 | tf_op jit(solution)/shard_map/ppermute | solution.py:436
  11.2 3.3 %shard_map.74.s1_ref = bf16[128,1024]{1,0:T(8,128)(2,1)S(1)} custom-call(f32[128,2048]{1,0:T(8,128)} %traces_ref.1, f32[256,128]{1,0:T(8,128)} %constant.23.clone.taps_ref, bf16[512,1024]{1,0:T(8,128)(2,1)} %constant.24.clone.table_ref), custom_call_target="tpu_custom_call" | custom-call | tf_op jit(solution)/shard_map/pallas_call | solution.py:371
  14.6 0.1 pad_add_fusion.place_ref
  14.6 0.0 collective-permute-done.hist_ref
  14.6 0.0 copy-done.1
  14.6 0.0 copy-done.3
  14.7 0.0 copy-done
  14.7 1.8 %shard_map.73.s0_ref = bf16[128,1024]{1,0:T(8,128)(2,1)S(1)} custom-call(f32[128,128]{1,0:T(8,128)S(1)} %collective-permute-done.hist_ref, f32[128,2048]{1,0:T(8,128)S(1)} %copy-done, f32[256,128]{1,0:T(8,128)S(1)} %copy-done.3, bf16[512,1024]{1,0:T(8,128)(2,1)S(1)} %copy-done.1), custom_call_target="tpu_custom_call" | custom-call | tf_op jit(solution)/shard_map/pallas_call | solution.py:387
  16.5 0.0 copy-done.5
  16.5 0.0 copy-done.4
  16.5 0.0 copy-done.6
  16.5 1.8 %shard_map.75 = bf16[64,40,128]{2,1,0:T(8,128)(2,1)S(1)} custom-call(s32[2]{0:T(128)S(1)} %pad_add_fusion.place_ref, s32[1,5]{1,0:T(1,128)S(1)} %bitcast.5, s32[1,5]{1,0:T(1,128)S(1)} %bitcast.6, s32[5,512]{1,0:T(8,128)S(1)} %copy-done.4, bf16[128,1024]{1,0:T(8,128)(2,1)S(1)} %shard_map.73.s0_ref, bf16[128,1024]{1,0:T(8,128)(2,1)S(1)} %shard_map.74.s1_ref), custom_call_target="tpu_custom_call" | custom-call | tf_op jit(solution)/shard_map/pallas_call | solution.py:96
  18.3 30.3 %all_to_all.15.slab_ref = bf16[64,40,128]{2,1,0:T(8,128)(2,1)S(1)} all-to-all(bf16[64,40,128]{2,1,0:T(8,128)(2,1)S(1)} %shard_map.75), channel_id=1, replica_groups=mesh['row'=4,'plane'=16,'lag'=4] {'plane','lag'}, dimensions={0} | all-to-all | bytes 1310720 | tf_op jit(solution)/shard_map/all_to_all | solution.py:451
  48.6 1.9 %shard_map.77 = (bf16[16,128,128]{2,1,0:T(8,128)(2,1)S(1)}, bf16[16,128,128]{2,1,0:T(8,128)(2,1)S(1)}, bf16[4,128,128]{2,1,0:T(8,128)(2,1)S(1)}) custom-call(bf16[64,40,128]{2,1,0:T(8,128)(2,1)S(1)} %all_to_all.15.slab_ref), custom_call_target="tpu_custom_call" | custom-call | tf_op jit(solution)/shard_map/pallas_call | solution.py:96
  50.5 0.0 copy-start.2
  50.5 3.3 %collective-permute-start.1 = (bf16[4,128,128]{2,1,0:T(8,128)(2,1)S(1)}, bf16[4,128,128]{2,1,0:T(8,128)(2,1)S(1)}, u32[]{:S(2)}, u32[]{:S(2)}) collective-permute-start(bf16[4,128,128]{2,1,0:T(8,128)(2,1)S(1)} %get-tuple-element.14), channel_id=1, source_target_pairs={{0,64},{64,128},{128,192},{1,65},{65,129},{129,193},{2,66},{66,130... | collective-permute-start | bytes 393224 | tf_op jit(solution)/shard_map/ppermute | solution.py:403
  53.9 3.5 %shard_map.76 = (bf16[16,5,128,128]{3,2,1,0:T(8,128)(2,1)S(1)}, s32[16,128]{1,0:T(8,128)S(1)}) custom-call(bf16[64,40,128]{2,1,0:T(8,128)(2,1)S(1)} %all_to_all.15.slab_ref), custom_call_target="tpu_custom_call" | custom-call | tf_op jit(solution)/shard_map/pallas_call | solution.py:96
  57.4 0.0 collective-permute-done.1.below_ref
  57.4 6.1 %shard_map.78 = f32[64,8,128]{2,1,0:T(8,128)S(1)} custom-call(s32[16,128]{1,0:T(8,128)S(1)} %get-tuple-element.10.owner_ref, bf16[16,5,128,128]{3,2,1,0:T(8,128)(2,1)S(1)} %get-tuple-element.11.chosen_ref, bf16[16,128,128]{2,1,0:T(8,128)(2,1)S(1)} %get-tuple-element.12.group_ref, bf16[16,128,128]{2,1,0:T(8,128)(2,1)S(1)} %get-tuple-element.13.swapped_ref, ...), custom_call_target="tpu_custom_call" | custom-call | tf_op jit(solution)/shard_map/pallas_call | solution.py:96
  63.6 18.0 %all_to_all.16.parts_ref = f32[64,8,128]{2,1,0:T(8,128)S(1)} all-to-all(f32[64,8,128]{2,1,0:T(8,128)S(1)} %shard_map.78), channel_id=1, replica_groups=mesh['row'=4,'plane'=16,'lag'=4] {'plane','lag'}, dimensions={0} | all-to-all | bytes 524288 | tf_op jit(solution)/shard_map/all_to_all | solution.py:453
  81.6 0.0 copy-done.2
  81.6 1.0 %shard_map.79 = f32[4,8,256]{2,1,0:T(8,128)S(1)} custom-call(s32[1]{0:T(128)} %bitcast.lag_ref, f32[64,8,128]{2,1,0:T(8,128)S(1)} %all_to_all.16.parts_ref, f32[1024,256]{1,0:T(8,128)S(1)} %copy-done.2), custom_call_target="tpu_custom_call" | custom-call | tf_op jit(solution)/shard_map/pallas_call | solution.py:96
  82.6 8.8 %all_to_all.17 = f32[4,8,256]{2,1,0:T(8,128)S(1)} all-to-all(f32[4,8,256]{2,1,0:T(8,128)S(1)} %shard_map.79), channel_id=1, replica_groups=mesh['row'=4,'plane'=16,'lag'=4] {'row'}, dimensions={0} | all-to-all | bytes 65536 | tf_op jit(solution)/shard_map/all_to_all | solution.py:456
  91.4 0.6 reduce_sum.9
Async XLA Ops:
  0.0 14.6 %copy-start.1 = (bf16[512,1024]{1,0:T(8,128)(2,1)S(1)}, bf16[512,1024]{1,0:T(8,128)(2,1)}, u32[]{:S(2)}) copy-start(bf16[512,1024]{1,0:T(8,128)(2,1)} %constant.24.clone.table_ref) | copy-start | bytes 3145732
  0.0 14.6 %copy-start.3 = (f32[256,128]{1,0:T(8,128)S(1)}, f32[256,128]{1,0:T(8,128)}, u32[]{:S(2)}) copy-start(f32[256,128]{1,0:T(8,128)} %constant.23.clone.taps_ref) | copy-start | bytes 393220
  0.0 14.6 %copy-start = (f32[128,2048]{1,0:T(8,128)S(1)}, f32[128,2048]{1,0:T(8,128)}, u32[]{:S(2)}) copy-start(f32[128,2048]{1,0:T(8,128)} %traces_ref.1) | copy-start | bytes 3145732
  0.0 16.5 %copy-start.5 = (s32[5,1]{0,1:T(1,128)S(1)}, s32[5,1]{0,1:T(1,128)}, u32[]{:S(2)}) copy-start(s32[5,1]{0,1:T(1,128)} %param.10) | copy-start | bytes 64
  0.0 16.5 %copy-start.4 = (s32[5,512]{1,0:T(8,128)S(1)}, s32[5,512]{1,0:T(8,128)}, u32[]{:S(2)}) copy-start(s32[5,512]{1,0:T(8,128)} %codes_ref.1) | copy-start | bytes 30724
  0.0 16.5 %copy-start.6 = (s32[5,1]{0,1:T(1,128)S(1)}, s32[5,1]{0,1:T(1,128)}, u32[]{:S(2)}) copy-start(s32[5,1]{0,1:T(1,128)} %param.8) | copy-start | bytes 64
  1.0 13.6 %collective-permute-start = (f32[128,128]{1,0:T(8,128)S(1)}, f32[128,128]{1,0:T(8,128)S(1)}, u32[]{:S(2)}, u32[]{:S(2)}) collective-permute-start(f32[128,128]{1,0:T(8,128)S(1)} %slice.3), channel_id=1, source_target_pairs={{0,1},{1,2},{2,3},{4,5},{5,6},{6,7},{8,9},{9,10},{10,11},{12,13},{... | collective-permute-start | bytes 196616 | tf_op jit(solution)/shard_map/ppermute | solution.py:436
  50.5 31.0 %copy-start.2 = (f32[1024,256]{1,0:T(8,128)S(1)}, f32[1024,256]{1,0:T(8,128)}, u32[]{:S(2)}) copy-start(f32[1024,256]{1,0:T(8,128)} %constant.25.clone.table_ref) | copy-start | bytes 3145732
  50.5 6.8 %collective-permute-start.1 = (bf16[4,128,128]{2,1,0:T(8,128)(2,1)S(1)}, bf16[4,128,128]{2,1,0:T(8,128)(2,1)S(1)}, u32[]{:S(2)}, u32[]{:S(2)}) collective-permute-start(bf16[4,128,128]{2,1,0:T(8,128)(2,1)S(1)} %get-tuple-element.14), channel_id=1, source_target_pairs={{0,64},{64,128},{128,192},{1,65},{65,129},{129,193},{2,66},{66,130... | collective-permute-start | bytes 393224 | tf_op jit(solution)/shard_map/ppermute | solution.py:403

commit v7 on v6

--- a/solution.py
+++ b/solution.py
@@ -35,7 +35,6 @@
 
 F32 = jnp.float32
 BF16 = jnp.bfloat16
-HI = lax.Precision.HIGHEST
 VMEM_LIMIT = 16 * 1024 * 1024
 
 
@@ -58,6 +57,12 @@
 SPAN_ROWS = sum(hi - lo for _, _, lo, hi in SPANS)
 
 
+def two_terms(table):
+    high = table.astype(jnp.bfloat16)
+    low = (table - high.astype(np.float32)).astype(jnp.bfloat16)
+    return np.concatenate([high, low], axis=1)
+
+
 def filter_table():
     k = np.arange(TAPS, dtype=np.float64)
     m = k - (TAPS - 1) / 2.0
@@ -65,7 +70,7 @@
     taps = ideal * (0.5 - 0.5 * np.cos(2 * np.pi * (k + 0.5) / TAPS))
     lagged = np.arange(TAPS)[None, :] - np.arange(2 * TAPS)[:, None] + TAPS
     inside = (lagged >= 0) & (lagged < TAPS)
-    return np.where(inside, taps[np.clip(lagged, 0, TAPS - 1)], 0.0).astype(np.float32)
+    return two_terms(np.where(inside, taps[np.clip(lagged, 0, TAPS - 1)], 0.0).astype(np.float32))
 
 
 def column_order():
@@ -83,7 +88,7 @@
     freq, is_imag = column_order()
     angle = (freq[:, None] * np.arange(LANES)[None, :] % WIN) * (2 * np.pi / WIN)
     weight = np.where(freq == 0, 1.0, 2.0)[:, None] / (WINDOWS * math.sqrt(WIN))
-    return (weight * np.where(is_imag[:, None], -np.sin(angle), np.cos(angle))).astype(np.float32)
+    return two_terms((weight * np.where(is_imag[:, None], -np.sin(angle), np.cos(angle))).astype(np.float32))
 
 
 def call(kernel, out_shape, *args, smem=(), aliases=None, scratch=()):
@@ -149,6 +154,14 @@
     return high, (values - high.astype(F32)).astype(BF16)
 
 
+def split_dot(values, table):
+    high, low = halves_of(values)
+    count, width = values.shape[0], table.shape[1] // 2
+    out = jnp.dot(jnp.concatenate([high, low], axis=0), table, preferred_element_type=F32)
+    small = out[count:, width:] + (out[count:, :width] + out[:count, width:])
+    return small + out[:count, :width]
+
+
 def transpose_pieces(arrays, width):
     bit = 1
     while bit < len(arrays):
@@ -165,19 +178,27 @@
     return arrays
 
 
-def spectra_kernel(hist_ref, x_ref, taps_ref, table_ref, out_ref):
+def spectra_kernel(hist_ref, x_ref, taps_ref, table_ref, out_ref, ready=None):
     tiles = [hist_ref[...]] + [x_ref[:, t * TAPS : (t + 1) * TAPS] for t in range(WIN // TAPS)]
     pairs = [jnp.concatenate([tiles[t], tiles[t + 1]], axis=1) for t in range(WIN // TAPS)]
-    rows = jnp.dot(jnp.concatenate(pairs, axis=0), taps_ref[...], precision=HI, preferred_element_type=F32)
-    rows = rows.astype(BF16)
+    rows = split_dot(jnp.concatenate(pairs, axis=0), taps_ref[...]).astype(BF16)
     filtered = [rows[t * CB : (t + 1) * CB] for t in range(WIN // TAPS)]
     early = jnp.concatenate(filtered[:4], axis=1)
     late = jnp.concatenate(filtered[4:], axis=1)
+    if ready is not None:
+        ready()
     column = lax.broadcasted_iota(jnp.int32, (1, WIN), 1)
     turn = jnp.where(column % 2 == 0, 1.0, -1.0).astype(F32)
     first = jnp.dot(early, table_ref[...], preferred_element_type=F32)
     second = jnp.dot(late, table_ref[...], preferred_element_type=F32)
     out_ref[...] = (first + turn * second).astype(BF16)
+
+
+def pack_table():
+    row = lax.broadcasted_iota(jnp.int32, (4 * WIDE, 1), 0)
+    goal = ((row >> 4) & 3) * WIDE + ((row >> 6) & 1) * (WIDE // 2) + (row >> 7) * 16 + (row & 15)
+    column = lax.broadcasted_iota(jnp.int32, (4 * WIDE, 4 * WIDE), 1)
+    return jnp.where(column == goal, 1.0, 0.0).astype(BF16)
 
 
 def list_rows(place_ref, count_ref, owner_ref, codes_ref):
@@ -203,15 +224,23 @@
 
 def pack_kernel(place_ref, count_ref, owner_ref, codes_ref, s0_ref, s1_ref, out_ref):
     lists = list_rows(place_ref, count_ref, owner_ref, codes_ref)
+    order = pack_table()
     for c in range(WIN // WIDE):
         cols = slice(c * WIDE, (c + 1) * WIDE)
-        pieces = []
-        for g in range(4):
-            for ref in (s0_ref, s1_ref):
-                pieces.append(ref[g * 32 : (g + 1) * 32, cols].astype(F32))
-        for e, value in enumerate(transpose_pieces(pieces, 2 * BAND)):
-            out_ref[c * 8 + e, :DATA_ROWS, :] = value.astype(BF16)
-            out_ref[c * 8 + e, DATA_ROWS:, :] = lists
+        halves = []
+        for g in range(0, 4, 2):
+            pieces = [ref[n * 32 : (n + 1) * 32, cols] for n in (g, g + 1) for ref in (s0_ref, s1_ref)]
+            halves.append(jnp.concatenate(pieces, axis=1))
+        mixed = jnp.dot(jnp.concatenate(halves, axis=0), order, preferred_element_type=F32)
+        upper = lanes() >= WIDE // 2
+        for e in range(4):
+            first = mixed[:DATA_ROWS, e * WIDE : (e + 1) * WIDE]
+            second = mixed[DATA_ROWS:, e * WIDE : (e + 1) * WIDE]
+            low = jnp.where(upper, pltpu.roll(second, WIDE // 2, 1), first)
+            high = jnp.where(upper, second, pltpu.roll(first, WIDE // 2, 1))
+            for d, value in ((c * 8 + e, low), (c * 8 + e + 4, high)):
+                out_ref[d, :DATA_ROWS, :] = value.astype(BF16)
+                out_ref[d, DATA_ROWS:, :] = lists
 
 
 def whiten_kernel(slab_ref, out_ref, swapped_ref, last_ref):
@@ -262,7 +291,7 @@
             out_ref[p, o] = chosen.astype(BF16)
         return carry
 
-    lax.fori_loop(0, PLANE, one, 0, unroll=4)
+    lax.fori_loop(0, PLANE, one, 0, unroll=16)
 
 
 def fill_bins(bins_ref):
@@ -324,7 +353,7 @@
         meet(total_ref, owner_ref, bins_ref, chosen_ref, p, group_ref[p], partners, p)
         return carry
 
-    lax.fori_loop(0, PLANE, one, 0, unroll=4)
+    lax.fori_loop(0, PLANE, one, 0, unroll=16)
     row_id = lax.broadcasted_iota(jnp.int32, (NBIN, WIDE), 0)
     own_piece = (lanes() >> 4) == row_id
     for n in range(PLANE):
@@ -348,7 +377,7 @@
         value = jnp.concatenate(bins, axis=0)
         swapped = jnp.where(real_lanes(), pltpu.roll(value, WIDE - BAND, 1), pltpu.roll(value, BAND, 1))
         columns.append(value * along + swapped * across)
-    lagged = jnp.dot(jnp.concatenate(columns, axis=1), table_ref[...], precision=HI, preferred_element_type=F32)
+    lagged = split_dot(jnp.concatenate(columns, axis=1), table_ref[...])
     for y in range(ROWS):
         for k in range(NBIN):
             out_ref[y, k : k + 1, :] = lagged[k * 8 + y : k * 8 + y + 1]
@@ -362,9 +391,9 @@
     ]
     for copy in copies:
         copy.start()
-    for copy in copies:
-        copy.wait()
-    spectra_kernel(x_ref.at[:, :TAPS], x_ref.at[:, TAPS:], h_ref, d_ref, out_ref)
+    copies[0].wait()
+    copies[1].wait()
+    spectra_kernel(x_ref.at[:, :TAPS], x_ref.at[:, TAPS:], h_ref, d_ref, out_ref, copies[2].wait)
 
 
 def later_window(traces, taps, table):
@@ -375,7 +404,7 @@
         out_specs=pl.BlockSpec(memory_space=pltpu.VMEM),
         scratch_shapes=[
             pltpu.VMEM((CB, WIN + TAPS), F32),
-            pltpu.VMEM((2 * TAPS, TAPS), F32),
+            pltpu.VMEM((2 * TAPS, 2 * TAPS), BF16),
             pltpu.VMEM((HALF, WIN), BF16),
             pltpu.SemaphoreType.DMA((3,)),
         ],
@@ -391,7 +420,7 @@
         in_specs=[
             pl.BlockSpec((CB, TAPS), lambda n: (0, 0)),
             pl.BlockSpec((CB, WIN), lambda n: (0, 0)),
-            pl.BlockSpec((2 * TAPS, TAPS), lambda n: (0, 0)),
+            pl.BlockSpec((2 * TAPS, 2 * TAPS), lambda n: (0, 0)),
             pl.BlockSpec((HALF, WIN), lambda n: (0, 0)),
         ],
         out_specs=pl.BlockSpec((CB, WIN), lambda n: (0, 0)),

time: 92.3 us -> 89.7 us (0.972)
  Pallas kernels: 19.5 us -> 15.6 us
  blocking collectives: 57.1 us -> 58.3 us
    pallas_call x5, Pallas kernels: 14.4 us -> 11.8 us  [call(): pl.pallas_call(kernel, out_shape=out_shape, in_specs=specs, out_specs=out...]
  transfers between devices with their start and end apart: 2 -> 2, of which waited for: 0 -> 0; matrix products, arithmetic and copies ran while one was open for 0% -> 0% of each run, Pallas kernels for 7% -> 6%
where the time goes in v7:
time: 89.7 us; the launch traced here: 89.5 us
  blocking collectives  58.3 us (65%)
  Pallas kernels  15.6 us (17%)
  starting transfers between devices  13.7 us (15%)
  local copies, waits for them, and re-layouts  1.03 us (1%)
    all_to_all x1, blocking collectives, body(): slabs = lax.all_to_all(slabs, ('plane', 'lag'), 0, 0, tiled=True)  31.1 us
    all_to_all x1, blocking collectives, body(): parts = lax.all_to_all(sums, ('plane', 'lag'), 0, 0, tiled=True)  18 us
    pallas_call x5, Pallas kernels, call(): pl.pallas_call(kernel, out_shape=out_shape, in_specs=specs, out_specs=out...  11.8 us
    ppermute x1, starting transfers between devices, body(): lax.ppermute(traces[:, -TAPS:], 'lag', [(i, i + 1) for i in range(3)])  10.2 us
    all_to_all x1, blocking collectives, body(): lax.all_to_all(lagged, 'row', 0, 0, tiled=True)  9.16 us
    ppermute x1, starting transfers between devices, row_below(): return lax.ppermute(blocks, 'row', [(i, i + 1) for i in range(ROWS - 1)])  3.52 us
    pallas_call x1, Pallas kernels, later_window(): pl.pallas_call(later_kernel, out_shape=shape((CB, WIN), BF16), in_specs=[...  2.51 us
  transfers between devices with their start and end apart: 2, of which 0 were waited for; matrix products, arithmetic and copies ran while one was open for 0% of the time, Pallas kernels for 6%

profile of v7, /device:TPU:1, one launch (start us, length us, event | category | flops | bytes accessed | tf_op | source)
XLA Modules:
  0.0 89.5 jit_solution(14384707085363965358)
XLA Ops:
  0.0 0.0 copy-start.1
  0.0 0.0 copy-start.3
  0.0 0.0 copy-start
  0.0 0.0 copy-start.5
  0.0 0.0 copy-start.4
  0.0 0.0 copy-start.6
  0.0 1.0 %slice.3 = f32[128,128]{1,0:T(8,128)S(1)} slice(f32[128,2048]{1,0:T(8,128)} %traces_ref.1), slice={[0:128], [1920:2048]} | slice | bytes 131072 | tf_op jit(solution)/shard_map/slice | solution.py:465
  1.0 10.2 %collective-permute-start = (f32[128,128]{1,0:T(8,128)S(1)}, f32[128,128]{1,0:T(8,128)S(1)}, u32[]{:S(2)}, u32[]{:S(2)}) collective-permute-start(f32[128,128]{1,0:T(8,128)S(1)} %slice.3), channel_id=1, source_target_pairs={{0,1},{1,2},{2,3},{4,5},{5,6},{6,7},{8,9},{9,10},{10,11},{12,13},{... | collective-permute-start | bytes 196616 | tf_op jit(solution)/shard_map/ppermute | solution.py:465
  11.2 2.5 %shard_map.74.s1_ref = bf16[128,1024]{1,0:T(8,128)(2,1)S(1)} custom-call(f32[128,2048]{1,0:T(8,128)} %traces_ref.1, bf16[256,256]{1,0:T(8,128)(2,1)} %constant.23.clone.taps_ref, bf16[512,1024]{1,0:T(8,128)(2,1)} %constant.24.clone.table_ref), custom_call_target="tpu_custom_call" | custom-call | tf_op jit(solution)/shard_map/pallas_call | solution.py:400
  13.8 0.1 pad_add_fusion.place_ref
  13.8 0.0 collective-permute-done.hist_ref
  13.8 0.0 copy-done.1
  13.8 0.0 copy-done.3
  13.8 0.0 copy-done
  13.9 1.3 %shard_map.73.s0_ref = bf16[128,1024]{1,0:T(8,128)(2,1)S(1)} custom-call(f32[128,128]{1,0:T(8,128)S(1)} %collective-permute-done.hist_ref, f32[128,2048]{1,0:T(8,128)S(1)} %copy-done, bf16[256,256]{1,0:T(8,128)(2,1)S(1)} %copy-done.3, bf16[512,1024]{1,0:T(8,128)(2,1)S(1)} %copy-done.1), custom_call_target="tpu_custom_call" | custom-call | tf_op jit(solution)/shard_map/pallas_call | solution.py:416
  15.2 0.0 copy-done.5
  15.2 0.0 copy-done.4
  15.2 0.0 copy-done.6
  15.2 1.6 %shard_map.75 = bf16[64,40,128]{2,1,0:T(8,128)(2,1)S(1)} custom-call(s32[2]{0:T(128)S(1)} %pad_add_fusion.place_ref, s32[1,5]{1,0:T(1,128)S(1)} %bitcast.5, s32[1,5]{1,0:T(1,128)S(1)} %bitcast.6, s32[5,512]{1,0:T(8,128)S(1)} %copy-done.4, bf16[128,1024]{1,0:T(8,128)(2,1)S(1)} %shard_map.73.s0_ref, bf16[128,1024]{1,0:T(8,128)(2,1)S(1)} %shard_map.74.s1_ref), custom_call_target="tpu_custom_call" | custom-call | tf_op jit(solution)/shard_map/pallas_call | solution.py:101
  16.8 31.1 %all_to_all.15.slab_ref = bf16[64,40,128]{2,1,0:T(8,128)(2,1)S(1)} all-to-all(bf16[64,40,128]{2,1,0:T(8,128)(2,1)S(1)} %shard_map.75), channel_id=1, replica_groups=mesh['row'=4,'plane'=16,'lag'=4] {'plane','lag'}, dimensions={0} | all-to-all | bytes 1310720 | tf_op jit(solution)/shard_map/all_to_all | solution.py:480
  47.9 1.9 %shard_map.77 = (bf16[16,128,128]{2,1,0:T(8,128)(2,1)S(1)}, bf16[16,128,128]{2,1,0:T(8,128)(2,1)S(1)}, bf16[4,128,128]{2,1,0:T(8,128)(2,1)S(1)}) custom-call(bf16[64,40,128]{2,1,0:T(8,128)(2,1)S(1)} %all_to_all.15.slab_ref), custom_call_target="tpu_custom_call" | custom-call | tf_op jit(solution)/shard_map/pallas_call | solution.py:101
  49.8 0.0 copy-start.2
  49.8 3.5 %collective-permute-start.1 = (bf16[4,128,128]{2,1,0:T(8,128)(2,1)S(1)}, bf16[4,128,128]{2,1,0:T(8,128)(2,1)S(1)}, u32[]{:S(2)}, u32[]{:S(2)}) collective-permute-start(bf16[4,128,128]{2,1,0:T(8,128)(2,1)S(1)} %get-tuple-element.14), channel_id=1, source_target_pairs={{0,64},{64,128},{128,192},{1,65},{65,129},{129,193},{2,66},{66,130... | collective-permute-start | bytes 393224 | tf_op jit(solution)/shard_map/ppermute | solution.py:432
  53.4 2.9 %shard_map.76 = (bf16[16,5,128,128]{3,2,1,0:T(8,128)(2,1)S(1)}, s32[16,128]{1,0:T(8,128)S(1)}) custom-call(bf16[64,40,128]{2,1,0:T(8,128)(2,1)S(1)} %all_to_all.15.slab_ref), custom_call_target="tpu_custom_call" | custom-call | tf_op jit(solution)/shard_map/pallas_call | solution.py:101
  56.3 0.0 collective-permute-done.1.below_ref
  56.3 4.7 %shard_map.78 = f32[64,8,128]{2,1,0:T(8,128)S(1)} custom-call(s32[16,128]{1,0:T(8,128)S(1)} %get-tuple-element.10.owner_ref, bf16[16,5,128,128]{3,2,1,0:T(8,128)(2,1)S(1)} %get-tuple-element.11.chosen_ref, bf16[16,128,128]{2,1,0:T(8,128)(2,1)S(1)} %get-tuple-element.12.group_ref, bf16[16,128,128]{2,1,0:T(8,128)(2,1)S(1)} %get-tuple-element.13.swapped_ref, ...), custom_call_target="tpu_custom_call" | custom-call | tf_op jit(solution)/shard_map/pallas_call | solution.py:101
  60.9 18.0 %all_to_all.16.parts_ref = f32[64,8,128]{2,1,0:T(8,128)S(1)} all-to-all(f32[64,8,128]{2,1,0:T(8,128)S(1)} %shard_map.78), channel_id=1, replica_groups=mesh['row'=4,'plane'=16,'lag'=4] {'plane','lag'}, dimensions={0} | all-to-all | bytes 524288 | tf_op jit(solution)/shard_map/all_to_all | solution.py:482
  79.0 0.0 copy-done.2
  79.0 0.7 shard_map.79
  79.7 9.2 %all_to_all.17 = f32[4,8,256]{2,1,0:T(8,128)S(1)} all-to-all(f32[4,8,256]{2,1,0:T(8,128)S(1)} %shard_map.79), channel_id=1, replica_groups=mesh['row'=4,'plane'=16,'lag'=4] {'row'}, dimensions={0} | all-to-all | bytes 65536 | tf_op jit(solution)/shard_map/all_to_all | solution.py:485
  88.8 0.6 reduce_sum.9
Async XLA Ops:
  0.0 13.8 %copy-start.1 = (bf16[512,1024]{1,0:T(8,128)(2,1)S(1)}, bf16[512,1024]{1,0:T(8,128)(2,1)}, u32[]{:S(2)}) copy-start(bf16[512,1024]{1,0:T(8,128)(2,1)} %constant.24.clone.table_ref) | copy-start | bytes 3145732
  0.0 13.8 %copy-start.3 = (bf16[256,256]{1,0:T(8,128)(2,1)S(1)}, bf16[256,256]{1,0:T(8,128)(2,1)}, u32[]{:S(2)}) copy-start(bf16[256,256]{1,0:T(8,128)(2,1)} %constant.23.clone.taps_ref) | copy-start | bytes 393220
  0.0 13.8 %copy-start = (f32[128,2048]{1,0:T(8,128)S(1)}, f32[128,2048]{1,0:T(8,128)}, u32[]{:S(2)}) copy-start(f32[128,2048]{1,0:T(8,128)} %traces_ref.1) | copy-start | bytes 3145732
  0.0 15.2 %copy-start.5 = (s32[5,1]{0,1:T(1,128)S(1)}, s32[5,1]{0,1:T(1,128)}, u32[]{:S(2)}) copy-start(s32[5,1]{0,1:T(1,128)} %param.10) | copy-start | bytes 64
  0.0 15.2 %copy-start.4 = (s32[5,512]{1,0:T(8,128)S(1)}, s32[5,512]{1,0:T(8,128)}, u32[]{:S(2)}) copy-start(s32[5,512]{1,0:T(8,128)} %codes_ref.1) | copy-start | bytes 30724
  0.0 15.2 %copy-start.6 = (s32[5,1]{0,1:T(1,128)S(1)}, s32[5,1]{0,1:T(1,128)}, u32[]{:S(2)}) copy-start(s32[5,1]{0,1:T(1,128)} %param.8) | copy-start | bytes 64
  1.0 12.8 %collective-permute-start = (f32[128,128]{1,0:T(8,128)S(1)}, f32[128,128]{1,0:T(8,128)S(1)}, u32[]{:S(2)}, u32[]{:S(2)}) collective-permute-start(f32[128,128]{1,0:T(8,128)S(1)} %slice.3), channel_id=1, source_target_pairs={{0,1},{1,2},{2,3},{4,5},{5,6},{6,7},{8,9},{9,10},{10,11},{12,13},{... | collective-permute-start | bytes 196616 | tf_op jit(solution)/shard_map/ppermute | solution.py:465
  49.8 29.2 %copy-start.2 = (bf16[1024,512]{1,0:T(8,128)(2,1)S(1)}, bf16[1024,512]{1,0:T(8,128)(2,1)}, u32[]{:S(2)}) copy-start(bf16[1024,512]{1,0:T(8,128)(2,1)} %constant.25.clone.table_ref) | copy-start | bytes 3145732
  49.8 6.5 %collective-permute-start.1 = (bf16[4,128,128]{2,1,0:T(8,128)(2,1)S(1)}, bf16[4,128,128]{2,1,0:T(8,128)(2,1)S(1)}, u32[]{:S(2)}, u32[]{:S(2)}) collective-permute-start(bf16[4,128,128]{2,1,0:T(8,128)(2,1)S(1)} %get-tuple-element.14), channel_id=1, source_target_pairs={{0,64},{64,128},{128,192},{1,65},{65,129},{129,193},{2,66},{66,130... | collective-permute-start | bytes 393224 | tf_op jit(solution)/shard_map/ppermute | solution.py:432

commit v8 on v7

--- a/solution.py
+++ b/solution.py
@@ -216,8 +216,7 @@
         live = jnp.where(place_ref[0] >= o, count_ref[:, o : o + 1], 0)
         rows.append(jnp.where(lane + start < live, value[o : o + 1], 0.0))
         owner = owner_ref[:, o : o + 1]
-        spot = (owner & (PLANE - 1)) * ROWS + (owner >> 4)
-        owners = jnp.where(lane == o, spot.astype(F32), owners)
+        owners = jnp.where(lane == o, owner.astype(F32), owners)
     rows = rows + [owners] + [jnp.zeros((1, WIDE), F32)] * (SLAB_ROWS - DATA_ROWS - MEETINGS - 1)
     return jnp.concatenate(rows, axis=0).astype(BF16)
 
@@ -356,31 +355,31 @@
     lax.fori_loop(0, PLANE, one, 0, unroll=16)
     row_id = lax.broadcasted_iota(jnp.int32, (NBIN, WIDE), 0)
     own_piece = (lanes() >> 4) == row_id
-    for n in range(PLANE):
-        rows = jnp.zeros((NBIN, WIDE), F32)
-        for y in range(ROWS):
-            value = jnp.where(own_piece, total_ref[n * ROWS + y], 0.0)
-            rows = jnp.where(row_id == y, jnp.sum(value, axis=0, keepdims=True), rows)
-        for lag in range(LAGS):
-            out_ref[n * LAGS + lag] = rows
-
-
-def lag_kernel(lag_ref, parts_ref, table_ref, out_ref):
+    for n in range(0, ROWS * PLANE, 2):
+        pair = []
+        for owner in (n, n + 1):
+            value = jnp.where(own_piece, total_ref[owner], 0.0)
+            pair.append(jnp.sum(value, axis=0, keepdims=True))
+        out_ref[n * LAGS : (n + 2) * LAGS, :] = jnp.where(row_id < LAGS, pair[0], pair[1])
+
+
+def lag_kernel(lag_ref, parts_ref, table_ref, out_ref, order_ref):
     lane = lanes()
     sign = jnp.where(real_lanes(), -1.0, 1.0)
     step = (lane * (lag_ref[0] + 2)) & 3
     along = jnp.where(step == 0, 1.0, 0.0) - jnp.where(step == 2, 1.0, 0.0)
     across = sign * (jnp.where(step == 1, 1.0, 0.0) - jnp.where(step == 3, 1.0, 0.0))
-    columns = []
-    for first in range(0, PLANE * LAGS, 8):
-        bins = transpose_pieces([parts_ref[first + n] for n in range(8)], 2 * BAND)
-        value = jnp.concatenate(bins, axis=0)
+    pieces = []
+    for n in range(8):
+        value = parts_ref[pl.ds(n, 8, stride=8), :]
+        for y in range(1, ROWS):
+            value = value + parts_ref[pl.ds(y * PLANE * LAGS + n, 8, stride=8), :]
+        pieces.append(value)
+    for k, value in enumerate(transpose_pieces(pieces, 2 * BAND)):
         swapped = jnp.where(real_lanes(), pltpu.roll(value, WIDE - BAND, 1), pltpu.roll(value, BAND, 1))
-        columns.append(value * along + swapped * across)
-    lagged = split_dot(jnp.concatenate(columns, axis=1), table_ref[...])
-    for y in range(ROWS):
-        for k in range(NBIN):
-            out_ref[y, k : k + 1, :] = lagged[k * 8 + y : k * 8 + y + 1]
+        order_ref[pl.ds(k, 8, stride=8), :] = value * along + swapped * across
+    columns = [order_ref[n * NBIN : (n + 1) * NBIN, :] for n in range(8)]
+    out_ref[0] = split_dot(jnp.concatenate(columns, axis=1), table_ref[...])
 
 
 def later_kernel(traces_ref, taps_ref, table_ref, out_ref, x_ref, h_ref, d_ref, sems):
@@ -445,7 +444,7 @@
     more = pltpu.VMEM((PLANE + ROUNDS, CB, WIDE), BF16)
     return call(
         meetings_kernel,
-        shape(sums_shape, F32),
+        shape((ROWS * PLANE * LAGS, WIDE), F32),
         owners,
         chosen,
         group,
@@ -479,10 +478,16 @@
     )
     slabs = lax.all_to_all(slabs, ("plane", "lag"), 0, 0, tiled=True)
     sums = middle(slabs, row_below)
-    parts = lax.all_to_all(sums, ("plane", "lag"), 0, 0, tiled=True)
-    table = jnp.asarray(inverse_table())
-    lagged = call(lag_kernel, shape((ROWS, NBIN, LANES), F32), lag.reshape(1), parts, table, smem=(0,))
-    return jnp.sum(lax.all_to_all(lagged, "row", 0, 0, tiled=True), axis=0, keepdims=True)
+    parts = lax.all_to_all(sums, ("row", "plane", "lag"), 0, 0, tiled=True)
+    return call(
+        lag_kernel,
+        shape((1, NBIN, LANES), F32),
+        lag.reshape(1),
+        parts,
+        jnp.asarray(inverse_table()),
+        smem=(0,),
+        scratch=(pltpu.VMEM((8 * NBIN, WIDE), F32),),
+    )
 
 
 def solution(mesh):

time: 89.7 us -> 83.4 us (0.930)
  blocking collectives: 58.3 us -> 52.3 us
    all_to_all x2 -> x1, blocking collectives: 27.2 us -> 21.2 us  [body(): parts = lax.all_to_all(sums, ('row', 'plane', 'lag'), 0, 0, tiled=True)]
  transfers between devices with their start and end apart: 2 -> 2, of which waited for: 0 -> 0; matrix products, arithmetic and copies ran while one was open for 0% -> 0% of each run, Pallas kernels for 6% -> 7%
where the time goes in v8:
time: 83.4 us; the launch traced here: 83.2 us
  blocking collectives  52.3 us (63%)
  Pallas kernels  16 us (19%)
  starting transfers between devices  13.6 us (16%)
  local copies, waits for them, and re-layouts  1.02 us (1%)
    all_to_all x1, blocking collectives, body(): slabs = lax.all_to_all(slabs, ('plane', 'lag'), 0, 0, tiled=True)  31.1 us
    all_to_all x1, blocking collectives, body(): parts = lax.all_to_all(sums, ('row', 'plane', 'lag'), 0, 0, tiled=True)  21.2 us
    pallas_call x5, Pallas kernels, call(): pl.pallas_call(kernel, out_shape=out_shape, in_specs=specs, out_specs=out...  12.2 us
    ppermute x1, starting transfers between devices, body(): lax.ppermute(traces[:, -TAPS:], 'lag', [(i, i + 1) for i in range(3)])  10.2 us
    ppermute x1, starting transfers between devices, row_below(): return lax.ppermute(blocks, 'row', [(i, i + 1) for i in range(ROWS - 1)])  3.39 us
    pallas_call x1, Pallas kernels, later_window(): pl.pallas_call(later_kernel, out_shape=shape((CB, WIN), BF16), in_specs=[...  2.51 us
  transfers between devices with their start and end apart: 2, of which 0 were waited for; matrix products, arithmetic and copies ran while one was open for 0% of the time, Pallas kernels for 7%

profile of v8, /device:TPU:1, one launch (start us, length us, event | category | flops | bytes accessed | tf_op | source)
XLA Modules:
  0.0 83.2 jit_solution(841201806314677631)
XLA Ops:
  0.0 0.0 copy-start.1
  0.0 0.0 copy-start.3
  0.0 0.0 copy-start
  0.0 0.0 copy-start.5
  0.0 0.0 copy-start.4
  0.0 0.0 copy-start.6
  0.0 1.0 %slice.3 = f32[128,128]{1,0:T(8,128)S(1)} slice(f32[128,2048]{1,0:T(8,128)} %traces_ref.1), slice={[0:128], [1920:2048]} | slice | bytes 131072 | tf_op jit(solution)/shard_map/slice | solution.py:464
  1.0 10.2 %collective-permute-start = (f32[128,128]{1,0:T(8,128)S(1)}, f32[128,128]{1,0:T(8,128)S(1)}, u32[]{:S(2)}, u32[]{:S(2)}) collective-permute-start(f32[128,128]{1,0:T(8,128)S(1)} %slice.3), channel_id=1, source_target_pairs={{0,1},{1,2},{2,3},{4,5},{5,6},{6,7},{8,9},{9,10},{10,11},{12,13},{... | collective-permute-start | bytes 196616 | tf_op jit(solution)/shard_map/ppermute | solution.py:464
  11.2 2.5 %shard_map.74.s1_ref = bf16[128,1024]{1,0:T(8,128)(2,1)S(1)} custom-call(f32[128,2048]{1,0:T(8,128)} %traces_ref.1, bf16[256,256]{1,0:T(8,128)(2,1)} %constant.21.clone.taps_ref, bf16[512,1024]{1,0:T(8,128)(2,1)} %constant.22.clone.table_ref), custom_call_target="tpu_custom_call" | custom-call | tf_op jit(solution)/shard_map/pallas_call | solution.py:399
  13.8 0.1 pad_add_fusion.place_ref
  13.8 0.0 collective-permute-done.hist_ref
  13.8 0.0 copy-done.1
  13.8 0.0 copy-done.3
  13.8 0.0 copy-done
  13.9 1.3 %shard_map.73.s0_ref = bf16[128,1024]{1,0:T(8,128)(2,1)S(1)} custom-call(f32[128,128]{1,0:T(8,128)S(1)} %collective-permute-done.hist_ref, f32[128,2048]{1,0:T(8,128)S(1)} %copy-done, bf16[256,256]{1,0:T(8,128)(2,1)S(1)} %copy-done.3, bf16[512,1024]{1,0:T(8,128)(2,1)S(1)} %copy-done.1), custom_call_target="tpu_custom_call" | custom-call | tf_op jit(solution)/shard_map/pallas_call | solution.py:415
  15.2 0.0 copy-done.5
  15.2 0.0 copy-done.4
  15.2 0.0 copy-done.6
  15.2 1.6 %shard_map.75 = bf16[64,40,128]{2,1,0:T(8,128)(2,1)S(1)} custom-call(s32[2]{0:T(128)S(1)} %pad_add_fusion.place_ref, s32[1,5]{1,0:T(1,128)S(1)} %bitcast.10, s32[1,5]{1,0:T(1,128)S(1)} %bitcast.11, s32[5,512]{1,0:T(8,128)S(1)} %copy-done.4, bf16[128,1024]{1,0:T(8,128)(2,1)S(1)} %shard_map.73.s0_ref, bf16[128,1024]{1,0:T(8,128)(2,1)S(1)} %shard_map.74.s1_ref), custom_call_target="tpu_custom_call" | custom-call | tf_op jit(solution)/shard_map/pallas_call | solution.py:101
  16.8 31.1 %all_to_all.16.slab_ref = bf16[64,40,128]{2,1,0:T(8,128)(2,1)S(1)} all-to-all(bf16[64,40,128]{2,1,0:T(8,128)(2,1)S(1)} %shard_map.75), channel_id=1, replica_groups=mesh['row'=4,'plane'=16,'lag'=4] {'plane','lag'}, dimensions={0} | all-to-all | bytes 1310720 | tf_op jit(solution)/shard_map/all_to_all | solution.py:479
  47.9 0.0 copy-start.2
  47.9 1.9 %shard_map.77 = (bf16[16,128,128]{2,1,0:T(8,128)(2,1)S(1)}, bf16[16,128,128]{2,1,0:T(8,128)(2,1)S(1)}, bf16[4,128,128]{2,1,0:T(8,128)(2,1)S(1)}) custom-call(bf16[64,40,128]{2,1,0:T(8,128)(2,1)S(1)} %all_to_all.16.slab_ref), custom_call_target="tpu_custom_call" | custom-call | tf_op jit(solution)/shard_map/pallas_call | solution.py:101
  49.8 3.4 %collective-permute-start.1 = (bf16[4,128,128]{2,1,0:T(8,128)(2,1)S(1)}, bf16[4,128,128]{2,1,0:T(8,128)(2,1)S(1)}, u32[]{:S(2)}, u32[]{:S(2)}) collective-permute-start(bf16[4,128,128]{2,1,0:T(8,128)(2,1)S(1)} %get-tuple-element.14), channel_id=1, source_target_pairs={{0,64},{64,128},{128,192},{1,65},{65,129},{129,193},{2,66},{66,130... | collective-permute-start | bytes 393224 | tf_op jit(solution)/shard_map/ppermute | solution.py:431
  53.2 2.9 %shard_map.76 = (bf16[16,5,128,128]{3,2,1,0:T(8,128)(2,1)S(1)}, s32[16,128]{1,0:T(8,128)S(1)}) custom-call(bf16[64,40,128]{2,1,0:T(8,128)(2,1)S(1)} %all_to_all.16.slab_ref), custom_call_target="tpu_custom_call" | custom-call | tf_op jit(solution)/shard_map/pallas_call | solution.py:101
  56.1 0.0 collective-permute-done.1.below_ref
  56.1 4.7 %shard_map.78 = f32[256,128]{1,0:T(8,128)S(1)} custom-call(s32[16,128]{1,0:T(8,128)S(1)} %get-tuple-element.10.owner_ref, bf16[16,5,128,128]{3,2,1,0:T(8,128)(2,1)S(1)} %get-tuple-element.11.chosen_ref, bf16[16,128,128]{2,1,0:T(8,128)(2,1)S(1)} %get-tuple-element.12.group_ref, bf16[16,128,128]{2,1,0:T(8,128)(2,1)S(1)} %get-tuple-element.13.swapped_ref, ...), custom_call_target="tpu_custom_call" | custom-call | tf_op jit(solution)/shard_map/pallas_call | solution.py:101
  60.8 21.2 %all_to_all.17 = f32[256,1,128]{2,1,0:T(1,128)S(1)} all-to-all(f32[256,1,128]{2,1,0:T(1,128)S(1)} %bitcast.8), channel_id=1, replica_groups=mesh['row'=4,'plane'=16,'lag'=4] {'row','plane','lag'}, dimensions={0} | all-to-all | bytes 262144 | tf_op jit(solution)/shard_map/all_to_all | solution.py:481
  82.0 0.0 copy-done.2
  82.0 1.1 %shard_map.79 = f32[1,8,256]{2,1,0:T(8,128)} custom-call(s32[1]{0:T(128)} %bitcast.lag_ref, f32[256,128]{1,0:T(8,128)S(1)} %bitcast.9, bf16[1024,512]{1,0:T(8,128)(2,1)S(1)} %copy-done.2), custom_call_target="tpu_custom_call" | custom-call | tf_op jit(solution)/shard_map/pallas_call | solution.py:101
Async XLA Ops:
  0.0 13.8 %copy-start.1 = (bf16[512,1024]{1,0:T(8,128)(2,1)S(1)}, bf16[512,1024]{1,0:T(8,128)(2,1)}, u32[]{:S(2)}) copy-start(bf16[512,1024]{1,0:T(8,128)(2,1)} %constant.22.clone.table_ref) | copy-start | bytes 3145732
  0.0 13.8 %copy-start.3 = (bf16[256,256]{1,0:T(8,128)(2,1)S(1)}, bf16[256,256]{1,0:T(8,128)(2,1)}, u32[]{:S(2)}) copy-start(bf16[256,256]{1,0:T(8,128)(2,1)} %constant.21.clone.taps_ref) | copy-start | bytes 393220
  0.0 13.8 %copy-start = (f32[128,2048]{1,0:T(8,128)S(1)}, f32[128,2048]{1,0:T(8,128)}, u32[]{:S(2)}) copy-start(f32[128,2048]{1,0:T(8,128)} %traces_ref.1) | copy-start | bytes 3145732
  0.0 15.2 %copy-start.5 = (s32[5,1]{0,1:T(1,128)S(1)}, s32[5,1]{0,1:T(1,128)}, u32[]{:S(2)}) copy-start(s32[5,1]{0,1:T(1,128)} %param.10) | copy-start | bytes 64
  0.0 15.2 %copy-start.4 = (s32[5,512]{1,0:T(8,128)S(1)}, s32[5,512]{1,0:T(8,128)}, u32[]{:S(2)}) copy-start(s32[5,512]{1,0:T(8,128)} %codes_ref.1) | copy-start | bytes 30724
  0.0 15.2 %copy-start.6 = (s32[5,1]{0,1:T(1,128)S(1)}, s32[5,1]{0,1:T(1,128)}, u32[]{:S(2)}) copy-start(s32[5,1]{0,1:T(1,128)} %param.8) | copy-start | bytes 64
  1.0 12.8 %collective-permute-start = (f32[128,128]{1,0:T(8,128)S(1)}, f32[128,128]{1,0:T(8,128)S(1)}, u32[]{:S(2)}, u32[]{:S(2)}) collective-permute-start(f32[128,128]{1,0:T(8,128)S(1)} %slice.3), channel_id=1, source_target_pairs={{0,1},{1,2},{2,3},{4,5},{5,6},{6,7},{8,9},{9,10},{10,11},{12,13},{... | collective-permute-start | bytes 196616 | tf_op jit(solution)/shard_map/ppermute | solution.py:464
  47.9 34.1 %copy-start.2 = (bf16[1024,512]{1,0:T(8,128)(2,1)S(1)}, bf16[1024,512]{1,0:T(8,128)(2,1)}, u32[]{:S(2)}) copy-start(bf16[1024,512]{1,0:T(8,128)(2,1)} %constant.23.clone.table_ref) | copy-start | bytes 3145732
  49.8 6.3 %collective-permute-start.1 = (bf16[4,128,128]{2,1,0:T(8,128)(2,1)S(1)}, bf16[4,128,128]{2,1,0:T(8,128)(2,1)S(1)}, u32[]{:S(2)}, u32[]{:S(2)}) collective-permute-start(bf16[4,128,128]{2,1,0:T(8,128)(2,1)S(1)} %get-tuple-element.14), channel_id=1, source_target_pairs={{0,64},{64,128},{128,192},{1,65},{65,129},{129,193},{2,66},{66,130... | collective-permute-start | bytes 393224 | tf_op jit(solution)/shard_map/ppermute | solution.py:431

commit v9 on v8

--- a/solution.py
+++ b/solution.py
@@ -178,20 +178,52 @@
     return arrays
 
 
-def spectra_kernel(hist_ref, x_ref, taps_ref, table_ref, out_ref, ready=None):
-    tiles = [hist_ref[...]] + [x_ref[:, t * TAPS : (t + 1) * TAPS] for t in range(WIN // TAPS)]
-    pairs = [jnp.concatenate([tiles[t], tiles[t + 1]], axis=1) for t in range(WIN // TAPS)]
-    rows = split_dot(jnp.concatenate(pairs, axis=0), taps_ref[...]).astype(BF16)
-    filtered = [rows[t * CB : (t + 1) * CB] for t in range(WIN // TAPS)]
-    early = jnp.concatenate(filtered[:4], axis=1)
-    late = jnp.concatenate(filtered[4:], axis=1)
-    if ready is not None:
-        ready()
+def turns():
     column = lax.broadcasted_iota(jnp.int32, (1, WIN), 1)
-    turn = jnp.where(column % 2 == 0, 1.0, -1.0).astype(F32)
-    first = jnp.dot(early, table_ref[...], preferred_element_type=F32)
-    second = jnp.dot(late, table_ref[...], preferred_element_type=F32)
-    out_ref[...] = (first + turn * second).astype(BF16)
+    return jnp.where(column % 2 == 0, 1.0, -1.0).astype(F32)
+
+
+def early_kernel(
+    place_ref, traces_ref, taps_ref, table_ref, counts_in, owners_in, codes_in,
+    s1_ref, part_ref, head_ref, taps_out, table_out, lists_ref,
+    x_ref, h_ref, d_ref, count_ref, owner_ref, codes_ref, sems,
+):
+    late = WIN - TAPS
+    copies = [
+        pltpu.make_async_copy(traces_ref.at[:, late:], x_ref.at[:, late:], sems.at[0]),
+        pltpu.make_async_copy(taps_ref, h_ref, sems.at[1]),
+        pltpu.make_async_copy(table_ref, d_ref, sems.at[2]),
+        pltpu.make_async_copy(traces_ref.at[:, :late], x_ref.at[:, :late], sems.at[3]),
+        pltpu.make_async_copy(counts_in, count_ref, sems.at[4]),
+        pltpu.make_async_copy(owners_in, owner_ref, sems.at[5]),
+        pltpu.make_async_copy(codes_in, codes_ref, sems.at[6]),
+    ]
+    for copy in copies:
+        copy.start()
+
+    def filtered(first, last):
+        pairs = [x_ref[:, (t - 1) * TAPS : (t + 1) * TAPS] for t in range(first, last)]
+        rows = split_dot(jnp.concatenate(pairs, axis=0), h_ref[...]).astype(BF16)
+        return [rows[n * CB : (n + 1) * CB] for n in range(last - first)]
+
+    copies[0].wait()
+    copies[1].wait()
+    tiles = filtered(8, 16)
+    copies[2].wait()
+    first = jnp.dot(jnp.concatenate(tiles[:4], axis=1), d_ref[...], preferred_element_type=F32)
+    second = jnp.dot(jnp.concatenate(tiles[4:], axis=1), d_ref[...], preferred_element_type=F32)
+    s1_ref[...] = (first + turns() * second).astype(BF16)
+    copies[3].wait()
+    tiles = filtered(1, 8)
+    first = jnp.dot(jnp.concatenate(tiles[:3], axis=1), d_ref[TAPS:, :], preferred_element_type=F32)
+    second = jnp.dot(jnp.concatenate(tiles[3:], axis=1), d_ref[...], preferred_element_type=F32)
+    part_ref[...] = first + turns() * second
+    head_ref[...] = x_ref[:, :TAPS]
+    taps_out[...] = h_ref[...]
+    table_out[...] = d_ref[:TAPS, :]
+    for copy in copies[4:]:
+        copy.wait()
+    lists_ref[...] = list_rows(place_ref, count_ref, owner_ref, codes_ref)
 
 
 def pack_table():
@@ -221,14 +253,19 @@
     return jnp.concatenate(rows, axis=0).astype(BF16)
 
 
-def pack_kernel(place_ref, count_ref, owner_ref, codes_ref, s0_ref, s1_ref, out_ref):
-    lists = list_rows(place_ref, count_ref, owner_ref, codes_ref)
+def pack_kernel(
+    lists_ref, hist_ref, head_ref, taps_ref, table_ref, part_ref, s1_ref, out_ref
+):
+    rows = split_dot(jnp.concatenate([hist_ref[...], head_ref[...]], axis=1), taps_ref[...]).astype(BF16)
+    s0 = (part_ref[...] + jnp.dot(rows, table_ref[...], preferred_element_type=F32)).astype(BF16)
+    s1 = s1_ref[...]
+    lists = lists_ref[...]
     order = pack_table()
     for c in range(WIN // WIDE):
         cols = slice(c * WIDE, (c + 1) * WIDE)
         halves = []
         for g in range(0, 4, 2):
-            pieces = [ref[n * 32 : (n + 1) * 32, cols] for n in (g, g + 1) for ref in (s0_ref, s1_ref)]
+            pieces = [value[n * 32 : (n + 1) * 32, cols] for n in (g, g + 1) for value in (s0, s1)]
             halves.append(jnp.concatenate(pieces, axis=1))
         mixed = jnp.dot(jnp.concatenate(halves, axis=0), order, preferred_element_type=F32)
         upper = lanes() >= WIDE // 2
@@ -382,49 +419,31 @@
     out_ref[0] = split_dot(jnp.concatenate(columns, axis=1), table_ref[...])
 
 
-def later_kernel(traces_ref, taps_ref, table_ref, out_ref, x_ref, h_ref, d_ref, sems):
-    copies = [
-        pltpu.make_async_copy(traces_ref.at[:, WIN - TAPS :], x_ref, sems.at[0]),
-        pltpu.make_async_copy(taps_ref, h_ref, sems.at[1]),
-        pltpu.make_async_copy(table_ref, d_ref, sems.at[2]),
-    ]
-    for copy in copies:
-        copy.start()
-    copies[0].wait()
-    copies[1].wait()
-    spectra_kernel(x_ref.at[:, :TAPS], x_ref.at[:, TAPS:], h_ref, d_ref, out_ref, copies[2].wait)
-
-
-def later_window(traces, taps, table):
+def early_part(place, *inputs):
+    operands = [pltpu.with_memory_space_constraint(value, pltpu.HBM) for value in inputs]
     return pl.pallas_call(
-        later_kernel,
-        out_shape=shape((CB, WIN), BF16),
-        in_specs=[pl.BlockSpec(memory_space=pltpu.HBM)] * 3,
-        out_specs=pl.BlockSpec(memory_space=pltpu.VMEM),
+        early_kernel,
+        out_shape=(
+            shape((CB, WIN), BF16),
+            shape((CB, WIN), F32),
+            shape((CB, TAPS), F32),
+            shape((2 * TAPS, 2 * TAPS), BF16),
+            shape((TAPS, WIN), BF16),
+            shape((SLAB_ROWS - DATA_ROWS, WIDE), BF16),
+        ),
+        in_specs=[pl.BlockSpec(memory_space=pltpu.SMEM)] + [pl.BlockSpec(memory_space=pltpu.HBM)] * 6,
+        out_specs=[pl.BlockSpec(memory_space=pltpu.VMEM)] * 6,
         scratch_shapes=[
-            pltpu.VMEM((CB, WIN + TAPS), F32),
+            pltpu.VMEM((CB, 2 * WIN), F32),
             pltpu.VMEM((2 * TAPS, 2 * TAPS), BF16),
             pltpu.VMEM((HALF, WIN), BF16),
-            pltpu.SemaphoreType.DMA((3,)),
+            pltpu.VMEM((1, MEETINGS), jnp.int32),
+            pltpu.VMEM((1, MEETINGS), jnp.int32),
+            pltpu.VMEM((MEETINGS, PCAP), jnp.int32),
+            pltpu.SemaphoreType.DMA((7,)),
         ],
         compiler_params=pltpu.CompilerParams(vmem_limit_bytes=VMEM_LIMIT),
-    )(*[pltpu.with_memory_space_constraint(value, pltpu.HBM) for value in (traces, taps, table)])
-
-
-def first_window(history, traces, taps, table):
-    return pl.pallas_call(
-        spectra_kernel,
-        out_shape=shape((CB, WIN), BF16),
-        grid=(1,),
-        in_specs=[
-            pl.BlockSpec((CB, TAPS), lambda n: (0, 0)),
-            pl.BlockSpec((CB, WIN), lambda n: (0, 0)),
-            pl.BlockSpec((2 * TAPS, 2 * TAPS), lambda n: (0, 0)),
-            pl.BlockSpec((HALF, WIN), lambda n: (0, 0)),
-        ],
-        out_specs=pl.BlockSpec((CB, WIN), lambda n: (0, 0)),
-        compiler_params=pltpu.CompilerParams(vmem_limit_bytes=VMEM_LIMIT),
-    )(history, traces, taps, table)
+    )(place, *operands)
 
 
 def row_below(blocks):
@@ -463,18 +482,25 @@
 
     history = lax.ppermute(traces[:, -TAPS:], "lag", [(i, i + 1) for i in range(3)])
 
-    spectra1 = later_window(traces, taps, table)
-    spectra0 = first_window(history, traces, taps, table)
+    spectra1, part, head, taps, table, lists = early_part(
+        jnp.stack([blk, lag]),
+        traces,
+        taps,
+        table,
+        pair_count.reshape(1, MEETINGS),
+        owner_map.reshape(1, MEETINGS),
+        pair_codes,
+    )
     slabs = call(
         pack_kernel,
         shape((PLANE * LAGS, SLAB_ROWS, WIDE), BF16),
-        jnp.stack([blk, lag]),
-        pair_count.reshape(1, MEETINGS),
-        owner_map.reshape(1, MEETINGS),
-        pair_codes,
-        spectra0,
+        lists,
+        history,
+        head,
+        taps,
+        table,
+        part,
         spectra1,
-        smem=(0,),
     )
     slabs = lax.all_to_all(slabs, ("plane", "lag"), 0, 0, tiled=True)
     sums = middle(slabs, row_below)

time: 83.4 us -> 81.6 us (0.978)
  blocking collectives: 52.3 us -> 50.5 us
    all_to_all x1, blocking collectives: 31.1 us -> 29.3 us  [body(): slabs = lax.all_to_all(slabs, ('plane', 'lag'), 0, 0, tiled=True)]
    pallas_call x2 -> x1, Pallas kernels: 3.8 us -> 4.31 us  [early_part(): pl.pallas_call(early_kernel, out_shape=(shape((CB, WIN), BF16), shape((CB...]
  transfers between devices with their start and end apart: 2 -> 2, of which waited for: 0 -> 0; matrix products, arithmetic and copies ran while one was open for 0% -> 0% of each run, Pallas kernels for 7% -> 9%
where the time goes in v9:
time: 81.6 us; the launch traced here: 81.4 us
  blocking collectives  50.5 us (62%)
  Pallas kernels  16.3 us (20%)
  starting transfers between devices  13.6 us (17%)
  local copies, waits for them, and re-layouts  0.85 us (1%)
    all_to_all x1, blocking collectives, body(): slabs = lax.all_to_all(slabs, ('plane', 'lag'), 0, 0, tiled=True)  29.3 us
    all_to_all x1, blocking collectives, body(): parts = lax.all_to_all(sums, ('row', 'plane', 'lag'), 0, 0, tiled=True)  21.2 us
    pallas_call x5, Pallas kernels, call(): pl.pallas_call(kernel, out_shape=out_shape, in_specs=specs, out_specs=out...  11.9 us
    ppermute x1, starting transfers between devices, body(): lax.ppermute(traces[:, -TAPS:], 'lag', [(i, i + 1) for i in range(3)])  10.2 us
    pallas_call x1, Pallas kernels, early_part(): pl.pallas_call(early_kernel, out_shape=(shape((CB, WIN), BF16), shape((CB...  4.31 us
    ppermute x1, starting transfers between devices, row_below(): return lax.ppermute(blocks, 'row', [(i, i + 1) for i in range(ROWS - 1)])  3.39 us
  transfers between devices with their start and end apart: 2, of which 0 were waited for; matrix products, arithmetic and copies ran while one was open for 0% of the time, Pallas kernels for 9%

profile of v9, /device:TPU:1, one launch (start us, length us, event | category | flops | bytes accessed | tf_op | source)
XLA Modules:
  0.0 81.4 jit_solution(11623373676503255740)
XLA Ops:
  0.0 0.8 %slice.3 = f32[128,128]{1,0:T(8,128)S(1)} slice(f32[128,2048]{1,0:T(8,128)} %traces_ref.1), slice={[0:128], [1920:2048]} | slice | bytes 131072 | tf_op jit(solution)/shard_map/slice | solution.py:483
  0.8 10.2 %collective-permute-start = (f32[128,128]{1,0:T(8,128)S(1)}, f32[128,128]{1,0:T(8,128)S(1)}, u32[]{:S(2)}, u32[]{:S(2)}) collective-permute-start(f32[128,128]{1,0:T(8,128)S(1)} %slice.3), channel_id=1, source_target_pairs={{0,1},{1,2},{2,3},{4,5},{5,6},{6,7},{8,9},{9,10},{10,11},{12,13},{... | collective-permute-start | bytes 196616 | tf_op jit(solution)/shard_map/ppermute | solution.py:483
  11.1 0.1 pad_add_fusion.place_ref
  11.1 4.3 %shard_map.73 = (bf16[128,1024]{1,0:T(8,128)(2,1)S(1)}, f32[128,1024]{1,0:T(8,128)S(1)}, f32[128,128]{1,0:T(8,128)S(1)}, bf16[256,256]{1,0:T(8,128)(2,1)S(1)}, b...) custom-call(s32[2]{0:T(128)S(1)} %pad_add_fusion.place_ref, f32[128,2048]{1,0:T(8,128)} %traces_ref.1, ...), custom_call_target="tpu_custom_call" | custom-call | tf_op jit(solution)/shard_map/pallas_call | solution.py:424
  15.4 0.0 collective-permute-done.hist_ref
  15.5 1.3 %shard_map.74 = bf16[64,40,128]{2,1,0:T(8,128)(2,1)S(1)} custom-call(bf16[8,128]{1,0:T(8,128)(2,1)S(1)} %get-tuple-element.16.lists_ref, f32[128,128]{1,0:T(8,128)S(1)} %collective-permute-done.hist_ref, f32[128,128]{1,0:T(8,128)S(1)} %get-tuple-element.17.head_ref, bf16[256,256]{1,0:T(8,128)(2,1)S(1)} %get-tuple-element.18.taps_ref, ...), custom_call_target="tpu_custom_call" | custom-call | tf_op jit(solution)/shard_map/pallas_call | solution.py:101
  16.8 29.3 %all_to_all.16.slab_ref = bf16[64,40,128]{2,1,0:T(8,128)(2,1)S(1)} all-to-all(bf16[64,40,128]{2,1,0:T(8,128)(2,1)S(1)} %shard_map.74), channel_id=1, replica_groups=mesh['row'=4,'plane'=16,'lag'=4] {'plane','lag'}, dimensions={0} | all-to-all | bytes 1310720 | tf_op jit(solution)/shard_map/all_to_all | solution.py:505
  46.1 0.0 copy-start
  46.1 1.9 %shard_map.76 = (bf16[16,128,128]{2,1,0:T(8,128)(2,1)S(1)}, bf16[16,128,128]{2,1,0:T(8,128)(2,1)S(1)}, bf16[4,128,128]{2,1,0:T(8,128)(2,1)S(1)}) custom-call(bf16[64,40,128]{2,1,0:T(8,128)(2,1)S(1)} %all_to_all.16.slab_ref), custom_call_target="tpu_custom_call" | custom-call | tf_op jit(solution)/shard_map/pallas_call | solution.py:101
  48.0 3.4 %collective-permute-start.1 = (bf16[4,128,128]{2,1,0:T(8,128)(2,1)S(1)}, bf16[4,128,128]{2,1,0:T(8,128)(2,1)S(1)}, u32[]{:S(2)}, u32[]{:S(2)}) collective-permute-start(bf16[4,128,128]{2,1,0:T(8,128)(2,1)S(1)} %get-tuple-element.26), channel_id=1, source_target_pairs={{0,64},{64,128},{128,192},{1,65},{65,129},{129,193},{2,66},{66,130... | collective-permute-start | bytes 393224 | tf_op jit(solution)/shard_map/ppermute | solution.py:450
  51.4 2.9 %shard_map.75 = (bf16[16,5,128,128]{3,2,1,0:T(8,128)(2,1)S(1)}, s32[16,128]{1,0:T(8,128)S(1)}) custom-call(bf16[64,40,128]{2,1,0:T(8,128)(2,1)S(1)} %all_to_all.16.slab_ref), custom_call_target="tpu_custom_call" | custom-call | tf_op jit(solution)/shard_map/pallas_call | solution.py:101
  54.3 0.0 collective-permute-done.1.below_ref
  54.3 4.7 %shard_map.77 = f32[256,128]{1,0:T(8,128)S(1)} custom-call(s32[16,128]{1,0:T(8,128)S(1)} %get-tuple-element.22.owner_ref, bf16[16,5,128,128]{3,2,1,0:T(8,128)(2,1)S(1)} %get-tuple-element.23.chosen_ref, bf16[16,128,128]{2,1,0:T(8,128)(2,1)S(1)} %get-tuple-element.24.group_ref, bf16[16,128,128]{2,1,0:T(8,128)(2,1)S(1)} %get-tuple-element.25.swapped_ref, ...), custom_call_target="tpu_custom_call" | custom-call | tf_op jit(solution)/shard_map/pallas_call | solution.py:101
  59.0 21.2 %all_to_all.17 = f32[256,1,128]{2,1,0:T(1,128)S(1)} all-to-all(f32[256,1,128]{2,1,0:T(1,128)S(1)} %bitcast.8), channel_id=1, replica_groups=mesh['row'=4,'plane'=16,'lag'=4] {'row','plane','lag'}, dimensions={0} | all-to-all | bytes 262144 | tf_op jit(solution)/shard_map/all_to_all | solution.py:507
  80.2 0.0 copy-done
  80.2 1.1 %shard_map.78 = f32[1,8,256]{2,1,0:T(8,128)} custom-call(s32[1]{0:T(128)} %bitcast.lag_ref, f32[256,128]{1,0:T(8,128)S(1)} %bitcast.9, bf16[1024,512]{1,0:T(8,128)(2,1)S(1)} %copy-done), custom_call_target="tpu_custom_call" | custom-call | tf_op jit(solution)/shard_map/pallas_call | solution.py:101
Async XLA Ops:
  0.8 14.6 %collective-permute-start = (f32[128,128]{1,0:T(8,128)S(1)}, f32[128,128]{1,0:T(8,128)S(1)}, u32[]{:S(2)}, u32[]{:S(2)}) collective-permute-start(f32[128,128]{1,0:T(8,128)S(1)} %slice.3), channel_id=1, source_target_pairs={{0,1},{1,2},{2,3},{4,5},{5,6},{6,7},{8,9},{9,10},{10,11},{12,13},{... | collective-permute-start | bytes 196616 | tf_op jit(solution)/shard_map/ppermute | solution.py:483
  46.1 34.1 %copy-start = (bf16[1024,512]{1,0:T(8,128)(2,1)S(1)}, bf16[1024,512]{1,0:T(8,128)(2,1)}, u32[]{:S(2)}) copy-start(bf16[1024,512]{1,0:T(8,128)(2,1)} %constant.23.clone.table_ref) | copy-start | bytes 3145732
  48.0 6.3 %collective-permute-start.1 = (bf16[4,128,128]{2,1,0:T(8,128)(2,1)S(1)}, bf16[4,128,128]{2,1,0:T(8,128)(2,1)S(1)}, u32[]{:S(2)}, u32[]{:S(2)}) collective-permute-start(bf16[4,128,128]{2,1,0:T(8,128)(2,1)S(1)} %get-tuple-element.26), channel_id=1, source_target_pairs={{0,64},{64,128},{128,192},{1,65},{65,129},{129,193},{2,66},{66,130... | collective-permute-start | bytes 393224 | tf_op jit(solution)/shard_map/ppermute | solution.py:450

commit v10 on v9

--- a/solution.py
+++ b/solution.py
@@ -209,15 +209,15 @@
     copies[0].wait()
     copies[1].wait()
     tiles = filtered(8, 16)
+    copies[3].wait()
+    tiles = [jnp.zeros((CB, TAPS), BF16)] + filtered(1, 8) + tiles
     copies[2].wait()
-    first = jnp.dot(jnp.concatenate(tiles[:4], axis=1), d_ref[...], preferred_element_type=F32)
-    second = jnp.dot(jnp.concatenate(tiles[4:], axis=1), d_ref[...], preferred_element_type=F32)
-    s1_ref[...] = (first + turns() * second).astype(BF16)
-    copies[3].wait()
-    tiles = filtered(1, 8)
-    first = jnp.dot(jnp.concatenate(tiles[:3], axis=1), d_ref[TAPS:, :], preferred_element_type=F32)
-    second = jnp.dot(jnp.concatenate(tiles[3:], axis=1), d_ref[...], preferred_element_type=F32)
-    part_ref[...] = first + turns() * second
+    rows = [jnp.concatenate(tiles[n : n + 4], axis=1) for n in (0, 4, 8, 12)]
+    first = jnp.dot(jnp.concatenate(rows[0::2], axis=0), d_ref[...], preferred_element_type=F32)
+    second = jnp.dot(jnp.concatenate(rows[1::2], axis=0), d_ref[...], preferred_element_type=F32)
+    both = first + turns() * second
+    part_ref[...] = both[:CB]
+    s1_ref[...] = both[CB:].astype(BF16)
     head_ref[...] = x_ref[:, :TAPS]
     taps_out[...] = h_ref[...]
     table_out[...] = d_ref[:TAPS, :]

time: 81.6 us -> 81.6 us (level)
  transfers between devices with their start and end apart: 2 -> 2, of which waited for: 0 -> 0; matrix products, arithmetic and copies ran while one was open for 0% -> 0% of each run, Pallas kernels for 9% -> 8%
where the time goes in v10:
time: 81.6 us; the launch traced here: 81.4 us
  blocking collectives  51 us (63%)
  Pallas kernels  15.7 us (19%)
  starting transfers between devices  13.6 us (17%)
  local copies, waits for them, and re-layouts  0.85 us (1%)
    all_to_all x1, blocking collectives, body(): slabs = lax.all_to_all(slabs, ('plane', 'lag'), 0, 0, tiled=True)  29.8 us
    all_to_all x1, blocking collectives, body(): parts = lax.all_to_all(sums, ('row', 'plane', 'lag'), 0, 0, tiled=True)  21.2 us
    pallas_call x5, Pallas kernels, call(): pl.pallas_call(kernel, out_shape=out_shape, in_specs=specs, out_specs=out...  11.9 us
    ppermute x1, starting transfers between devices, body(): lax.ppermute(traces[:, -TAPS:], 'lag', [(i, i + 1) for i in range(3)])  10.2 us
    pallas_call x1, Pallas kernels, early_part(): pl.pallas_call(early_kernel, out_shape=(shape((CB, WIN), BF16), shape((CB...  3.81 us
    ppermute x1, starting transfers between devices, row_below(): return lax.ppermute(blocks, 'row', [(i, i + 1) for i in range(ROWS - 1)])  3.39 us
  transfers between devices with their start and end apart: 2, of which 0 were waited for; matrix products, arithmetic and copies ran while one was open for 0% of the time, Pallas kernels for 8%

profile of v10, /device:TPU:1, one launch (start us, length us, event | category | flops | bytes accessed | tf_op | source)
XLA Modules:
  0.0 81.4 jit_solution(14112408166327806496)
XLA Ops:
  0.0 0.8 %slice.3 = f32[128,128]{1,0:T(8,128)S(1)} slice(f32[128,2048]{1,0:T(8,128)} %traces_ref.1), slice={[0:128], [1920:2048]} | slice | bytes 131072 | tf_op jit(solution)/shard_map/slice | solution.py:483
  0.8 10.2 %collective-permute-start = (f32[128,128]{1,0:T(8,128)S(1)}, f32[128,128]{1,0:T(8,128)S(1)}, u32[]{:S(2)}, u32[]{:S(2)}) collective-permute-start(f32[128,128]{1,0:T(8,128)S(1)} %slice.3), channel_id=1, source_target_pairs={{0,1},{1,2},{2,3},{4,5},{5,6},{6,7},{8,9},{9,10},{10,11},{12,13},{... | collective-permute-start | bytes 196616 | tf_op jit(solution)/shard_map/ppermute | solution.py:483
  11.1 0.1 pad_add_fusion.place_ref
  11.1 3.8 %shard_map.73 = (bf16[128,1024]{1,0:T(8,128)(2,1)S(1)}, f32[128,1024]{1,0:T(8,128)S(1)}, f32[128,128]{1,0:T(8,128)S(1)}, bf16[256,256]{1,0:T(8,128)(2,1)S(1)}, b...) custom-call(s32[2]{0:T(128)S(1)} %pad_add_fusion.place_ref, f32[128,2048]{1,0:T(8,128)} %traces_ref.1, ...), custom_call_target="tpu_custom_call" | custom-call | tf_op jit(solution)/shard_map/pallas_call | solution.py:424
  14.9 0.0 collective-permute-done.hist_ref
  15.0 1.3 %shard_map.74 = bf16[64,40,128]{2,1,0:T(8,128)(2,1)S(1)} custom-call(bf16[8,128]{1,0:T(8,128)(2,1)S(1)} %get-tuple-element.16.lists_ref, f32[128,128]{1,0:T(8,128)S(1)} %collective-permute-done.hist_ref, f32[128,128]{1,0:T(8,128)S(1)} %get-tuple-element.17.head_ref, bf16[256,256]{1,0:T(8,128)(2,1)S(1)} %get-tuple-element.18.taps_ref, ...), custom_call_target="tpu_custom_call" | custom-call | tf_op jit(solution)/shard_map/pallas_call | solution.py:101
  16.3 29.8 %all_to_all.16.slab_ref = bf16[64,40,128]{2,1,0:T(8,128)(2,1)S(1)} all-to-all(bf16[64,40,128]{2,1,0:T(8,128)(2,1)S(1)} %shard_map.74), channel_id=1, replica_groups=mesh['row'=4,'plane'=16,'lag'=4] {'plane','lag'}, dimensions={0} | all-to-all | bytes 1310720 | tf_op jit(solution)/shard_map/all_to_all | solution.py:505
  46.1 0.0 copy-start
  46.1 1.9 %shard_map.76 = (bf16[16,128,128]{2,1,0:T(8,128)(2,1)S(1)}, bf16[16,128,128]{2,1,0:T(8,128)(2,1)S(1)}, bf16[4,128,128]{2,1,0:T(8,128)(2,1)S(1)}) custom-call(bf16[64,40,128]{2,1,0:T(8,128)(2,1)S(1)} %all_to_all.16.slab_ref), custom_call_target="tpu_custom_call" | custom-call | tf_op jit(solution)/shard_map/pallas_call | solution.py:101
  48.0 3.4 %collective-permute-start.1 = (bf16[4,128,128]{2,1,0:T(8,128)(2,1)S(1)}, bf16[4,128,128]{2,1,0:T(8,128)(2,1)S(1)}, u32[]{:S(2)}, u32[]{:S(2)}) collective-permute-start(bf16[4,128,128]{2,1,0:T(8,128)(2,1)S(1)} %get-tuple-element.26), channel_id=1, source_target_pairs={{0,64},{64,128},{128,192},{1,65},{65,129},{129,193},{2,66},{66,130... | collective-permute-start | bytes 393224 | tf_op jit(solution)/shard_map/ppermute | solution.py:450
  51.4 2.9 %shard_map.75 = (bf16[16,5,128,128]{3,2,1,0:T(8,128)(2,1)S(1)}, s32[16,128]{1,0:T(8,128)S(1)}) custom-call(bf16[64,40,128]{2,1,0:T(8,128)(2,1)S(1)} %all_to_all.16.slab_ref), custom_call_target="tpu_custom_call" | custom-call | tf_op jit(solution)/shard_map/pallas_call | solution.py:101
  54.3 0.0 collective-permute-done.1.below_ref
  54.3 4.6 %shard_map.77 = f32[256,128]{1,0:T(8,128)S(1)} custom-call(s32[16,128]{1,0:T(8,128)S(1)} %get-tuple-element.22.owner_ref, bf16[16,5,128,128]{3,2,1,0:T(8,128)(2,1)S(1)} %get-tuple-element.23.chosen_ref, bf16[16,128,128]{2,1,0:T(8,128)(2,1)S(1)} %get-tuple-element.24.group_ref, bf16[16,128,128]{2,1,0:T(8,128)(2,1)S(1)} %get-tuple-element.25.swapped_ref, ...), custom_call_target="tpu_custom_call" | custom-call | tf_op jit(solution)/shard_map/pallas_call | solution.py:101
  59.0 21.2 %all_to_all.17 = f32[256,1,128]{2,1,0:T(1,128)S(1)} all-to-all(f32[256,1,128]{2,1,0:T(1,128)S(1)} %bitcast.8), channel_id=1, replica_groups=mesh['row'=4,'plane'=16,'lag'=4] {'row','plane','lag'}, dimensions={0} | all-to-all | bytes 262144 | tf_op jit(solution)/shard_map/all_to_all | solution.py:507
  80.2 0.0 copy-done
  80.2 1.1 %shard_map.78 = f32[1,8,256]{2,1,0:T(8,128)} custom-call(s32[1]{0:T(128)} %bitcast.lag_ref, f32[256,128]{1,0:T(8,128)S(1)} %bitcast.9, bf16[1024,512]{1,0:T(8,128)(2,1)S(1)} %copy-done), custom_call_target="tpu_custom_call" | custom-call | tf_op jit(solution)/shard_map/pallas_call | solution.py:101
Async XLA Ops:
  0.8 14.1 %collective-permute-start = (f32[128,128]{1,0:T(8,128)S(1)}, f32[128,128]{1,0:T(8,128)S(1)}, u32[]{:S(2)}, u32[]{:S(2)}) collective-permute-start(f32[128,128]{1,0:T(8,128)S(1)} %slice.3), channel_id=1, source_target_pairs={{0,1},{1,2},{2,3},{4,5},{5,6},{6,7},{8,9},{9,10},{10,11},{12,13},{... | collective-permute-start | bytes 196616 | tf_op jit(solution)/shard_map/ppermute | solution.py:483
  46.1 34.1 %copy-start = (bf16[1024,512]{1,0:T(8,128)(2,1)S(1)}, bf16[1024,512]{1,0:T(8,128)(2,1)}, u32[]{:S(2)}) copy-start(bf16[1024,512]{1,0:T(8,128)(2,1)} %constant.23.clone.table_ref) | copy-start | bytes 3145732
  48.0 6.3 %collective-permute-start.1 = (bf16[4,128,128]{2,1,0:T(8,128)(2,1)S(1)}, bf16[4,128,128]{2,1,0:T(8,128)(2,1)S(1)}, u32[]{:S(2)}, u32[]{:S(2)}) collective-permute-start(bf16[4,128,128]{2,1,0:T(8,128)(2,1)S(1)} %get-tuple-element.26), channel_id=1, source_target_pairs={{0,64},{64,128},{128,192},{1,65},{65,129},{129,193},{2,66},{66,130... | collective-permute-start | bytes 393224 | tf_op jit(solution)/shard_map/ppermute | solution.py:450

commit v11 on v10

--- a/solution.py
+++ b/solution.py
@@ -279,11 +279,16 @@
                 out_ref[d, DATA_ROWS:, :] = lists
 
 
-def whiten_kernel(slab_ref, out_ref, swapped_ref, last_ref):
-    order = order_table()
+def tables_kernel(place_ref, order_ref, both_ref, swap_ref, bins_ref):
+    order_ref[...] = order_table()
     both = fold_table(1.0, 1.0)
-    both = jnp.concatenate([both, both], axis=0)
-    swap = swap_table()
+    both_ref[...] = jnp.concatenate([both, both], axis=0)
+    swap_ref[...] = swap_table()
+    fill_bins(bins_ref)
+
+
+def whiten_kernel(slab_ref, order_ref, both_ref, swap_ref, out_ref, swapped_ref, last_ref):
+    order, both, swap = order_ref[...], both_ref[...], swap_ref[...]
     batch = 4
     for first in range(0, PLANE, batch):
         rows = []
@@ -373,11 +378,10 @@
 
 
 def meetings_kernel(
-    owner_ref, chosen_ref, group_ref, swapped_ref, below_ref, out_ref, bins_ref, all_ref, turned_ref, total_ref
+    owner_ref, chosen_ref, group_ref, swapped_ref, below_ref, bins_ref, swap_ref, out_ref, all_ref, turned_ref, total_ref
 ):
     total_ref[...] = jnp.zeros(total_ref.shape, F32)
-    fill_bins(bins_ref)
-    swap = swap_table()
+    swap = swap_ref[...]
     for n in range(ROUNDS):
         all_ref[n] = below_ref[n]
         turned_ref[n] = jnp.dot(below_ref[n], swap, preferred_element_type=F32).astype(BF16)
@@ -450,10 +454,10 @@
     return lax.ppermute(blocks, "row", [(i, i + 1) for i in range(ROWS - 1)])
 
 
-def middle(slabs, send):
+def middle(slabs, send, order, both, swap, bins):
     blocks = (PLANE, CB, WIDE)
     group, swapped, last = call(
-        whiten_kernel, (shape(blocks, BF16), shape(blocks, BF16), shape((ROUNDS, CB, WIDE), BF16)), slabs
+        whiten_kernel, (shape(blocks, BF16), shape(blocks, BF16), shape((ROUNDS, CB, WIDE), BF16)), slabs, order, both, swap
     )
     below = send(last)
     chosen, owners = call(
@@ -469,8 +473,10 @@
         group,
         swapped,
         below,
+        bins,
+        swap,
         smem=(0,),
-        scratch=(pltpu.VMEM((SPAN_ROWS, CB), BF16), more, more, pltpu.VMEM(sums_shape, F32)),
+        scratch=(more, more, pltpu.VMEM(sums_shape, F32)),
     )
 
 
@@ -502,8 +508,12 @@
         part,
         spectra1,
     )
+    slabs, place = lax.optimization_barrier((slabs, lag.reshape(1)))
+    table_shapes = ((4 * WIDE, 4 * WIDE), (2 * WIDE, WIDE), (WIDE, WIDE), (SPAN_ROWS, CB))
+    tables = call(tables_kernel, tuple(shape(dims, BF16) for dims in table_shapes), place, smem=(0,))
     slabs = lax.all_to_all(slabs, ("plane", "lag"), 0, 0, tiled=True)
-    sums = middle(slabs, row_below)
+    slabs, *tables = lax.optimization_barrier((slabs, *tables))
+    sums = middle(slabs, row_below, *tables)
     parts = lax.all_to_all(sums, ("row", "plane", "lag"), 0, 0, tiled=True)
     return call(
         lag_kernel,

time: 81.6 us -> 82.6 us (1.012)
  blocking collectives: 51 us -> 21.2 us
  waiting for transfers between devices: 0.01 us -> 21.4 us
  starting transfers between devices: 13.6 us -> 22.1 us
  Pallas kernels: 15.7 us -> 16.7 us
    all_to_all x1 -> x0, blocking collectives: 29.8 us -> none  [body(): slabs = lax.all_to_all(slabs, ('plane', 'lag'), 0, 0, tiled=True)]
    all_to_all x0 -> x1, waiting for transfers between devices: none -> 21.4 us  [body(): slabs = lax.all_to_all(slabs, ('plane', 'lag'), 0, 0, tiled=True)]
    all_to_all x0 -> x1, starting transfers between devices: none -> 8.35 us  [body(): slabs = lax.all_to_all(slabs, ('plane', 'lag'), 0, 0, tiled=True)]
    pallas_call x5 -> x6, Pallas kernels: 11.9 us -> 12.9 us  [call(): pl.pallas_call(kernel, out_shape=out_shape, in_specs=specs, out_specs=out...]
  transfers between devices with their start and end apart: 2 -> 3, of which waited for: 0 -> 1; matrix products, arithmetic and copies ran while one was open for 0% -> 0% of each run, Pallas kernels for 8% -> 8%
where the time goes in v11:
time: 82.6 us; the launch traced here: 82.3 us
  starting transfers between devices  22.1 us (27%)
  waiting for transfers between devices  21.4 us (26%)
  blocking collectives  21.2 us (26%)
  Pallas kernels  16.7 us (20%)
  local copies, waits for them, and re-layouts  0.85 us (1%)
    all_to_all x1, waiting for transfers between devices, body(): slabs = lax.all_to_all(slabs, ('plane', 'lag'), 0, 0, tiled=True)  21.4 us
    all_to_all x1, blocking collectives, body(): parts = lax.all_to_all(sums, ('row', 'plane', 'lag'), 0, 0, tiled=True)  21.2 us
    pallas_call x6, Pallas kernels, call(): pl.pallas_call(kernel, out_shape=out_shape, in_specs=specs, out_specs=out...  12.9 us
    ppermute x1, starting transfers between devices, body(): lax.ppermute(traces[:, -TAPS:], 'lag', [(i, i + 1) for i in range(3)])  10.2 us
    all_to_all x1, starting transfers between devices, body(): slabs = lax.all_to_all(slabs, ('plane', 'lag'), 0, 0, tiled=True)  8.35 us
    pallas_call x1, Pallas kernels, early_part(): pl.pallas_call(early_kernel, out_shape=(shape((CB, WIN), BF16), shape((CB...  3.81 us
    ppermute x1, starting transfers between devices, row_below(): return lax.ppermute(blocks, 'row', [(i, i + 1) for i in range(ROWS - 1)])  3.52 us
  transfers between devices with their start and end apart: 3, of which 1 were waited for; matrix products, arithmetic and copies ran while one was open for 0% of the time, Pallas kernels for 8%

profile of v11, /device:TPU:1, one launch (start us, length us, event | category | flops | bytes accessed | tf_op | source)
XLA Modules:
  0.0 82.3 jit_solution(8790727425306921122)
XLA Ops:
  0.0 0.8 %slice.3 = f32[128,128]{1,0:T(8,128)S(1)} slice(f32[128,2048]{1,0:T(8,128)} %traces_ref.1), slice={[0:128], [1920:2048]} | slice | bytes 131072 | tf_op jit(solution)/shard_map/slice | solution.py:489
  0.8 10.2 %collective-permute-start = (f32[128,128]{1,0:T(8,128)S(1)}, f32[128,128]{1,0:T(8,128)S(1)}, u32[]{:S(2)}, u32[]{:S(2)}) collective-permute-start(f32[128,128]{1,0:T(8,128)S(1)} %slice.3), channel_id=1, source_target_pairs={{0,1},{1,2},{2,3},{4,5},{5,6},{6,7},{8,9},{9,10},{10,11},{12,13},{... | collective-permute-start | bytes 196616 | tf_op jit(solution)/shard_map/ppermute | solution.py:489
  11.1 0.1 pad_add_fusion.place_ref
  11.1 3.8 %shard_map.73 = (bf16[128,1024]{1,0:T(8,128)(2,1)S(1)}, f32[128,1024]{1,0:T(8,128)S(1)}, f32[128,128]{1,0:T(8,128)S(1)}, bf16[256,256]{1,0:T(8,128)(2,1)S(1)}, b...) custom-call(s32[2]{0:T(128)S(1)} %pad_add_fusion.place_ref, f32[128,2048]{1,0:T(8,128)} %traces_ref.1, ...), custom_call_target="tpu_custom_call" | custom-call | tf_op jit(solution)/shard_map/pallas_call | solution.py:428
  14.9 0.0 collective-permute-done.hist_ref
  15.0 2.2 %shard_map.74 = bf16[64,40,128]{2,1,0:T(8,128)(2,1)} custom-call(bf16[8,128]{1,0:T(8,128)(2,1)S(1)} %get-tuple-element.27.lists_ref, f32[128,128]{1,0:T(8,128)S(1)} %collective-permute-done.hist_ref, f32[128,128]{1,0:T(8,128)S(1)} %get-tuple-element.28.head_ref, bf16[256,256]{1,0:T(8,128)(2,1)S(1)} %get-tuple-element.29.taps_ref, ...), custom_call_target="tpu_custom_call" | custom-call | tf_op jit(solution)/shard_map/pallas_call | solution.py:101
  17.1 8.3 %all-to-all-start = ((bf16[64,40,128]{2,1,0:T(8,128)(2,1)}), bf16[64,40,128]{2,1,0:T(8,128)(2,1)S(1)}, u32[]{:S(2)}, u32[]{:S(2)}) async-start(bf16[64,40,128]{2,1,0:T(8,128)(2,1)} %shard_map.74), calls=%async_computation | async-start | bytes 1310720 | tf_op jit(solution)/shard_map/all_to_all | solution.py:514
  25.5 0.3 shard_map.75
  25.8 21.4 %all-to-all-done.slab_ref = bf16[64,40,128]{2,1,0:T(8,128)(2,1)S(1)} async-done(((bf16[64,40,128]{2,1,0:T(8,128)(2,1)}), bf16[64,40,128]{2,1,0:T(8,128)(2,1)S(1)}, u32[]{:S(2)}, u32[]{:S(2)}) %all-to-all-start) | async-done | bytes 655392 | tf_op jit(solution)/shard_map/all_to_all | solution.py:514
  47.2 1.8 %shard_map.77 = (bf16[16,128,128]{2,1,0:T(8,128)(2,1)S(1)}, bf16[16,128,128]{2,1,0:T(8,128)(2,1)S(1)}, bf16[4,128,128]{2,1,0:T(8,128)(2,1)S(1)}) custom-call(bf16[64,40,128]{2,1,0:T(8,128)(2,1)S(1)} %all-to-all-done.slab_ref, bf16[512,512]{1,0:T(8,128)(2,1)S(1)} %get-tuple-element.42.order_ref, bf16[256,128]{1,0:T(8,128)(2,1)S(1)} %get-tuple-element.43.both_ref, ...), custom_call_target="tpu_custom_call" | custom-call | tf_op jit(solution)/shard_map/pallas_call | solution.py:101
  49.0 0.0 copy-start
  49.0 3.5 %collective-permute-start.1 = (bf16[4,128,128]{2,1,0:T(8,128)(2,1)S(1)}, bf16[4,128,128]{2,1,0:T(8,128)(2,1)S(1)}, u32[]{:S(2)}, u32[]{:S(2)}) collective-permute-start(bf16[4,128,128]{2,1,0:T(8,128)(2,1)S(1)} %get-tuple-element.47), channel_id=1, source_target_pairs={{0,64},{64,128},{128,192},{1,65},{65,129},{129,193},{2,66},{66,130... | collective-permute-start | bytes 393224 | tf_op jit(solution)/shard_map/ppermute | solution.py:454
  52.5 2.9 %shard_map.76 = (bf16[16,5,128,128]{3,2,1,0:T(8,128)(2,1)S(1)}, s32[16,128]{1,0:T(8,128)S(1)}) custom-call(bf16[64,40,128]{2,1,0:T(8,128)(2,1)S(1)} %all-to-all-done.slab_ref), custom_call_target="tpu_custom_call" | custom-call | tf_op jit(solution)/shard_map/pallas_call | solution.py:101
  55.4 0.0 collective-permute-done.1.below_ref
  55.5 4.5 %shard_map.78 = f32[256,128]{1,0:T(8,128)S(1)} custom-call(s32[16,128]{1,0:T(8,128)S(1)} %get-tuple-element.40.owner_ref, bf16[16,5,128,128]{3,2,1,0:T(8,128)(2,1)S(1)} %get-tuple-element.41.chosen_ref, bf16[16,128,128]{2,1,0:T(8,128)(2,1)S(1)} %get-tuple-element.45.group_ref, bf16[16,128,128]{2,1,0:T(8,128)(2,1)S(1)} %get-tuple-element.46.swapped_ref, ...), custom_call_target="tpu_custom_call" | custom-call | tf_op jit(solution)/shard_map/pallas_call | solution.py:101
  60.0 21.2 %all_to_all.16 = f32[256,1,128]{2,1,0:T(1,128)S(1)} all-to-all(f32[256,1,128]{2,1,0:T(1,128)S(1)} %bitcast.8), channel_id=1, replica_groups=mesh['row'=4,'plane'=16,'lag'=4] {'row','plane','lag'}, dimensions={0} | all-to-all | bytes 262144 | tf_op jit(solution)/shard_map/all_to_all | solution.py:517
  81.2 0.0 copy-done
  81.2 1.1 %shard_map.79 = f32[1,8,256]{2,1,0:T(8,128)} custom-call(s32[1]{0:T(128)} %bitcast.place_ref.lag_ref, f32[256,128]{1,0:T(8,128)S(1)} %bitcast.9, bf16[1024,512]{1,0:T(8,128)(2,1)S(1)} %copy-done), custom_call_target="tpu_custom_call" | custom-call | tf_op jit(solution)/shard_map/pallas_call | solution.py:101
Async XLA Ops:
  0.8 14.1 %collective-permute-start = (f32[128,128]{1,0:T(8,128)S(1)}, f32[128,128]{1,0:T(8,128)S(1)}, u32[]{:S(2)}, u32[]{:S(2)}) collective-permute-start(f32[128,128]{1,0:T(8,128)S(1)} %slice.3), channel_id=1, source_target_pairs={{0,1},{1,2},{2,3},{4,5},{5,6},{6,7},{8,9},{9,10},{10,11},{12,13},{... | collective-permute-start | bytes 196616 | tf_op jit(solution)/shard_map/ppermute | solution.py:489
  17.1 30.0 %all-to-all-start = ((bf16[64,40,128]{2,1,0:T(8,128)(2,1)}), bf16[64,40,128]{2,1,0:T(8,128)(2,1)S(1)}, u32[]{:S(2)}, u32[]{:S(2)}) async-start(bf16[64,40,128]{2,1,0:T(8,128)(2,1)} %shard_map.74), calls=%async_computation | async-start | bytes 1310720 | tf_op jit(solution)/shard_map/all_to_all | solution.py:514
  49.0 32.2 %copy-start = (bf16[1024,512]{1,0:T(8,128)(2,1)S(1)}, bf16[1024,512]{1,0:T(8,128)(2,1)}, u32[]{:S(2)}) copy-start(bf16[1024,512]{1,0:T(8,128)(2,1)} %constant.23.clone.table_ref) | copy-start | bytes 3145732
  49.0 6.5 %collective-permute-start.1 = (bf16[4,128,128]{2,1,0:T(8,128)(2,1)S(1)}, bf16[4,128,128]{2,1,0:T(8,128)(2,1)S(1)}, u32[]{:S(2)}, u32[]{:S(2)}) collective-permute-start(bf16[4,128,128]{2,1,0:T(8,128)(2,1)S(1)} %get-tuple-element.47), channel_id=1, source_target_pairs={{0,64},{64,128},{128,192},{1,65},{65,129},{129,193},{2,66},{66,130... | collective-permute-start | bytes 393224 | tf_op jit(solution)/shard_map/ppermute | solution.py:454

commit v12 on v10

--- a/solution.py
+++ b/solution.py
@@ -185,7 +185,7 @@
 
 def early_kernel(
     place_ref, traces_ref, taps_ref, table_ref, counts_in, owners_in, codes_in,
-    s1_ref, part_ref, head_ref, taps_out, table_out, lists_ref,
+    s1_ref, part_ref, head_ref, taps_out, table_out, lists_ref, order_ref,
     x_ref, h_ref, d_ref, count_ref, owner_ref, codes_ref, sems,
 ):
     late = WIN - TAPS
@@ -200,6 +200,7 @@
     ]
     for copy in copies:
         copy.start()
+    order_ref[...] = pack_table()
 
     def filtered(first, last):
         pairs = [x_ref[:, (t - 1) * TAPS : (t + 1) * TAPS] for t in range(first, last)]
@@ -254,13 +255,13 @@
 
 
 def pack_kernel(
-    lists_ref, hist_ref, head_ref, taps_ref, table_ref, part_ref, s1_ref, out_ref
+    lists_ref, order_ref, hist_ref, head_ref, taps_ref, table_ref, part_ref, s1_ref, out_ref
 ):
     rows = split_dot(jnp.concatenate([hist_ref[...], head_ref[...]], axis=1), taps_ref[...]).astype(BF16)
     s0 = (part_ref[...] + jnp.dot(rows, table_ref[...], preferred_element_type=F32)).astype(BF16)
     s1 = s1_ref[...]
     lists = lists_ref[...]
-    order = pack_table()
+    order = order_ref[...]
     for c in range(WIN // WIDE):
         cols = slice(c * WIDE, (c + 1) * WIDE)
         halves = []
@@ -430,9 +431,10 @@
             shape((2 * TAPS, 2 * TAPS), BF16),
             shape((TAPS, WIN), BF16),
             shape((SLAB_ROWS - DATA_ROWS, WIDE), BF16),
+            shape((4 * WIDE, 4 * WIDE), BF16),
         ),
         in_specs=[pl.BlockSpec(memory_space=pltpu.SMEM)] + [pl.BlockSpec(memory_space=pltpu.HBM)] * 6,
-        out_specs=[pl.BlockSpec(memory_space=pltpu.VMEM)] * 6,
+        out_specs=[pl.BlockSpec(memory_space=pltpu.VMEM)] * 7,
         scratch_shapes=[
             pltpu.VMEM((CB, 2 * WIN), F32),
             pltpu.VMEM((2 * TAPS, 2 * TAPS), BF16),
@@ -482,7 +484,7 @@
 
     history = lax.ppermute(traces[:, -TAPS:], "lag", [(i, i + 1) for i in range(3)])
 
-    spectra1, part, head, taps, table, lists = early_part(
+    spectra1, part, head, taps, table, lists, order = early_part(
         jnp.stack([blk, lag]),
         traces,
         taps,
@@ -495,6 +497,7 @@
         pack_kernel,
         shape((PLANE * LAGS, SLAB_ROWS, WIDE), BF16),
         lists,
+        order,
         history,
         head,
         taps,

time: 81.6 us -> 81.5 us (level)
  no operation moved by 1% of the time
where the time goes in v12:
time: 81.5 us; the launch traced here: 81.3 us
  blocking collectives  51 us (63%)
  Pallas kernels  15.6 us (19%)
  starting transfers between devices  13.6 us (17%)
  local copies, waits for them, and re-layouts  0.85 us (1%)
    all_to_all x1, blocking collectives, body(): slabs = lax.all_to_all(slabs, ('plane', 'lag'), 0, 0, tiled=True)  29.8 us
    all_to_all x1, blocking collectives, body(): parts = lax.all_to_all(sums, ('row', 'plane', 'lag'), 0, 0, tiled=True)  21.2 us
    pallas_call x5, Pallas kernels, call(): pl.pallas_call(kernel, out_shape=out_shape, in_specs=specs, out_specs=out...  11.8 us
    ppermute x1, starting transfers between devices, body(): lax.ppermute(traces[:, -TAPS:], 'lag', [(i, i + 1) for i in range(3)])  10.2 us
    pallas_call x1, Pallas kernels, early_part(): pl.pallas_call(early_kernel, out_shape=(shape((CB, WIN), BF16), shape((CB...  3.81 us
    ppermute x1, starting transfers between devices, row_below(): return lax.ppermute(blocks, 'row', [(i, i + 1) for i in range(ROWS - 1)])  3.39 us
  transfers between devices with their start and end apart: 2, of which 0 were waited for; matrix products, arithmetic and copies ran while one was open for 0% of the time, Pallas kernels for 8%

profile of v12, /device:TPU:1, one launch (start us, length us, event | category | flops | bytes accessed | tf_op | source)
XLA Modules:
  0.0 81.3 jit_solution(16510753432004027418)
XLA Ops:
  0.0 0.8 %slice.3 = f32[128,128]{1,0:T(8,128)S(1)} slice(f32[128,2048]{1,0:T(8,128)} %traces_ref.1), slice={[0:128], [1920:2048]} | slice | bytes 131072 | tf_op jit(solution)/shard_map/slice | solution.py:485
  0.8 10.2 %collective-permute-start = (f32[128,128]{1,0:T(8,128)S(1)}, f32[128,128]{1,0:T(8,128)S(1)}, u32[]{:S(2)}, u32[]{:S(2)}) collective-permute-start(f32[128,128]{1,0:T(8,128)S(1)} %slice.3), channel_id=1, source_target_pairs={{0,1},{1,2},{2,3},{4,5},{5,6},{6,7},{8,9},{9,10},{10,11},{12,13},{... | collective-permute-start | bytes 196616 | tf_op jit(solution)/shard_map/ppermute | solution.py:485
  11.1 0.1 pad_add_fusion.place_ref
  11.1 3.8 %shard_map.73 = (bf16[128,1024]{1,0:T(8,128)(2,1)S(1)}, f32[128,1024]{1,0:T(8,128)S(1)}, f32[128,128]{1,0:T(8,128)S(1)}, bf16[256,256]{1,0:T(8,128)(2,1)S(1)}, b...) custom-call(s32[2]{0:T(128)S(1)} %pad_add_fusion.place_ref, ...), custom_call_target="tpu_custom_call" | custom-call | tf_op jit(solution)/shard_map/pallas_call | solution.py:425
  14.9 0.0 collective-permute-done.hist_ref
  15.0 1.2 %shard_map.74 = bf16[64,40,128]{2,1,0:T(8,128)(2,1)S(1)} custom-call(bf16[8,128]{1,0:T(8,128)(2,1)S(1)} %get-tuple-element.17.lists_ref, bf16[512,512]{1,0:T(8,128)(2,1)S(1)} %get-tuple-element.18.order_ref, f32[128,128]{1,0:T(8,128)S(1)} %collective-permute-done.hist_ref, f32[128,128]{1,0:T(8,128)S(1)} %get-tuple-element.19.head_ref, ...), custom_call_target="tpu_custom_call" | custom-call | tf_op jit(solution)/shard_map/pallas_call | solution.py:101
  16.2 29.8 %all_to_all.16.slab_ref = bf16[64,40,128]{2,1,0:T(8,128)(2,1)S(1)} all-to-all(bf16[64,40,128]{2,1,0:T(8,128)(2,1)S(1)} %shard_map.74), channel_id=1, replica_groups=mesh['row'=4,'plane'=16,'lag'=4] {'plane','lag'}, dimensions={0} | all-to-all | bytes 1310720 | tf_op jit(solution)/shard_map/all_to_all | solution.py:508
  46.0 0.0 copy-start
  46.0 1.9 %shard_map.76 = (bf16[16,128,128]{2,1,0:T(8,128)(2,1)S(1)}, bf16[16,128,128]{2,1,0:T(8,128)(2,1)S(1)}, bf16[4,128,128]{2,1,0:T(8,128)(2,1)S(1)}) custom-call(bf16[64,40,128]{2,1,0:T(8,128)(2,1)S(1)} %all_to_all.16.slab_ref), custom_call_target="tpu_custom_call" | custom-call | tf_op jit(solution)/shard_map/pallas_call | solution.py:101
  47.9 3.4 %collective-permute-start.1 = (bf16[4,128,128]{2,1,0:T(8,128)(2,1)S(1)}, bf16[4,128,128]{2,1,0:T(8,128)(2,1)S(1)}, u32[]{:S(2)}, u32[]{:S(2)}) collective-permute-start(bf16[4,128,128]{2,1,0:T(8,128)(2,1)S(1)} %get-tuple-element.28), channel_id=1, source_target_pairs={{0,64},{64,128},{128,192},{1,65},{65,129},{129,193},{2,66},{66,130... | collective-permute-start | bytes 393224 | tf_op jit(solution)/shard_map/ppermute | solution.py:452
  51.3 2.9 %shard_map.75 = (bf16[16,5,128,128]{3,2,1,0:T(8,128)(2,1)S(1)}, s32[16,128]{1,0:T(8,128)S(1)}) custom-call(bf16[64,40,128]{2,1,0:T(8,128)(2,1)S(1)} %all_to_all.16.slab_ref), custom_call_target="tpu_custom_call" | custom-call | tf_op jit(solution)/shard_map/pallas_call | solution.py:101
  54.2 0.0 collective-permute-done.1.below_ref
  54.2 4.7 %shard_map.77 = f32[256,128]{1,0:T(8,128)S(1)} custom-call(s32[16,128]{1,0:T(8,128)S(1)} %get-tuple-element.24.owner_ref, bf16[16,5,128,128]{3,2,1,0:T(8,128)(2,1)S(1)} %get-tuple-element.25.chosen_ref, bf16[16,128,128]{2,1,0:T(8,128)(2,1)S(1)} %get-tuple-element.26.group_ref, bf16[16,128,128]{2,1,0:T(8,128)(2,1)S(1)} %get-tuple-element.27.swapped_ref, ...), custom_call_target="tpu_custom_call" | custom-call | tf_op jit(solution)/shard_map/pallas_call | solution.py:101
  58.9 21.2 %all_to_all.17 = f32[256,1,128]{2,1,0:T(1,128)S(1)} all-to-all(f32[256,1,128]{2,1,0:T(1,128)S(1)} %bitcast.8), channel_id=1, replica_groups=mesh['row'=4,'plane'=16,'lag'=4] {'row','plane','lag'}, dimensions={0} | all-to-all | bytes 262144 | tf_op jit(solution)/shard_map/all_to_all | solution.py:510
  80.1 0.0 copy-done
  80.1 1.1 %shard_map.78 = f32[1,8,256]{2,1,0:T(8,128)} custom-call(s32[1]{0:T(128)} %bitcast.lag_ref, f32[256,128]{1,0:T(8,128)S(1)} %bitcast.9, bf16[1024,512]{1,0:T(8,128)(2,1)S(1)} %copy-done), custom_call_target="tpu_custom_call" | custom-call | tf_op jit(solution)/shard_map/pallas_call | solution.py:101
Async XLA Ops:
  0.8 14.1 %collective-permute-start = (f32[128,128]{1,0:T(8,128)S(1)}, f32[128,128]{1,0:T(8,128)S(1)}, u32[]{:S(2)}, u32[]{:S(2)}) collective-permute-start(f32[128,128]{1,0:T(8,128)S(1)} %slice.3), channel_id=1, source_target_pairs={{0,1},{1,2},{2,3},{4,5},{5,6},{6,7},{8,9},{9,10},{10,11},{12,13},{... | collective-permute-start | bytes 196616 | tf_op jit(solution)/shard_map/ppermute | solution.py:485
  46.0 34.1 %copy-start = (bf16[1024,512]{1,0:T(8,128)(2,1)S(1)}, bf16[1024,512]{1,0:T(8,128)(2,1)}, u32[]{:S(2)}) copy-start(bf16[1024,512]{1,0:T(8,128)(2,1)} %constant.23.clone.table_ref) | copy-start | bytes 3145732
  47.9 6.3 %collective-permute-start.1 = (bf16[4,128,128]{2,1,0:T(8,128)(2,1)S(1)}, bf16[4,128,128]{2,1,0:T(8,128)(2,1)S(1)}, u32[]{:S(2)}, u32[]{:S(2)}) collective-permute-start(bf16[4,128,128]{2,1,0:T(8,128)(2,1)S(1)} %get-tuple-element.28), channel_id=1, source_target_pairs={{0,64},{64,128},{128,192},{1,65},{65,129},{129,193},{2,66},{66,130... | collective-permute-start | bytes 393224 | tf_op jit(solution)/shard_map/ppermute | solution.py:452

commit v13 on v12

--- a/solution.py
+++ b/solution.py
@@ -185,7 +185,7 @@
 
 def early_kernel(
     place_ref, traces_ref, taps_ref, table_ref, counts_in, owners_in, codes_in,
-    s1_ref, part_ref, head_ref, taps_out, table_out, lists_ref, order_ref,
+    s1_ref, part_ref, head_ref, taps_out, table_out, lists_ref, order_ref, bins_out,
     x_ref, h_ref, d_ref, count_ref, owner_ref, codes_ref, sems,
 ):
     late = WIN - TAPS
@@ -201,6 +201,7 @@
     for copy in copies:
         copy.start()
     order_ref[...] = pack_table()
+    fill_bins(bins_out)
 
     def filtered(first, last):
         pairs = [x_ref[:, (t - 1) * TAPS : (t + 1) * TAPS] for t in range(first, last)]
@@ -374,10 +375,9 @@
 
 
 def meetings_kernel(
-    owner_ref, chosen_ref, group_ref, swapped_ref, below_ref, out_ref, bins_ref, all_ref, turned_ref, total_ref
+    owner_ref, chosen_ref, group_ref, swapped_ref, below_ref, bins_ref, out_ref, all_ref, turned_ref, total_ref
 ):
     total_ref[...] = jnp.zeros(total_ref.shape, F32)
-    fill_bins(bins_ref)
     swap = swap_table()
     for n in range(ROUNDS):
         all_ref[n] = below_ref[n]
@@ -432,9 +432,10 @@
             shape((TAPS, WIN), BF16),
             shape((SLAB_ROWS - DATA_ROWS, WIDE), BF16),
             shape((4 * WIDE, 4 * WIDE), BF16),
+            shape((SPAN_ROWS, CB), BF16),
         ),
         in_specs=[pl.BlockSpec(memory_space=pltpu.SMEM)] + [pl.BlockSpec(memory_space=pltpu.HBM)] * 6,
-        out_specs=[pl.BlockSpec(memory_space=pltpu.VMEM)] * 7,
+        out_specs=[pl.BlockSpec(memory_space=pltpu.VMEM)] * 8,
         scratch_shapes=[
             pltpu.VMEM((CB, 2 * WIN), F32),
             pltpu.VMEM((2 * TAPS, 2 * TAPS), BF16),
@@ -452,7 +453,7 @@
     return lax.ppermute(blocks, "row", [(i, i + 1) for i in range(ROWS - 1)])
 
 
-def middle(slabs, send):
+def middle(slabs, send, bins):
     blocks = (PLANE, CB, WIDE)
     group, swapped, last = call(
         whiten_kernel, (shape(blocks, BF16), shape(blocks, BF16), shape((ROUNDS, CB, WIDE), BF16)), slabs
@@ -471,8 +472,9 @@
         group,
         swapped,
         below,
+        bins,
         smem=(0,),
-        scratch=(pltpu.VMEM((SPAN_ROWS, CB), BF16), more, more, pltpu.VMEM(sums_shape, F32)),
+        scratch=(more, more, pltpu.VMEM(sums_shape, F32)),
     )
 
 
@@ -484,7 +486,7 @@
 
     history = lax.ppermute(traces[:, -TAPS:], "lag", [(i, i + 1) for i in range(3)])
 
-    spectra1, part, head, taps, table, lists, order = early_part(
+    spectra1, part, head, taps, table, lists, order, bins = early_part(
         jnp.stack([blk, lag]),
         traces,
         taps,
@@ -506,7 +508,7 @@
         spectra1,
     )
     slabs = lax.all_to_all(slabs, ("plane", "lag"), 0, 0, tiled=True)
-    sums = middle(slabs, row_below)
+    sums = middle(slabs, row_below, bins)
     parts = lax.all_to_all(sums, ("row", "plane", "lag"), 0, 0, tiled=True)
     return call(
         lag_kernel,

time: 81.5 us -> 81.8 us (level)
  no operation moved by 1% of the time
where the time goes in v13:
time: 81.8 us; the launch traced here: 81.6 us
  blocking collectives  51 us (62%)
  Pallas kernels  15.8 us (19%)
  starting transfers between devices  13.7 us (17%)
  local copies, waits for them, and re-layouts  0.85 us (1%)
    all_to_all x1, blocking collectives, body(): slabs = lax.all_to_all(slabs, ('plane', 'lag'), 0, 0, tiled=True)  29.8 us
    all_to_all x1, blocking collectives, body(): parts = lax.all_to_all(sums, ('row', 'plane', 'lag'), 0, 0, tiled=True)  21.2 us
    pallas_call x5, Pallas kernels, call(): pl.pallas_call(kernel, out_shape=out_shape, in_specs=specs, out_specs=out...  12 us
    ppermute x1, starting transfers between devices, body(): lax.ppermute(traces[:, -TAPS:], 'lag', [(i, i + 1) for i in range(3)])  10.2 us
    pallas_call x1, Pallas kernels, early_part(): pl.pallas_call(early_kernel, out_shape=(shape((CB, WIN), BF16), shape((CB...  3.81 us
    ppermute x1, starting transfers between devices, row_below(): return lax.ppermute(blocks, 'row', [(i, i + 1) for i in range(ROWS - 1)])  3.52 us
  transfers between devices with their start and end apart: 2, of which 0 were waited for; matrix products, arithmetic and copies ran while one was open for 0% of the time, Pallas kernels for 8%

profile of v13, /device:TPU:1, one launch (start us, length us, event | category | flops | bytes accessed | tf_op | source)
XLA Modules:
  0.0 81.6 jit_solution(3405845685456351414)
XLA Ops:
  0.0 0.8 %slice.3 = f32[128,128]{1,0:T(8,128)S(1)} slice(f32[128,2048]{1,0:T(8,128)} %traces_ref.1), slice={[0:128], [1920:2048]} | slice | bytes 131072 | tf_op jit(solution)/shard_map/slice | solution.py:487
  0.8 10.2 %collective-permute-start = (f32[128,128]{1,0:T(8,128)S(1)}, f32[128,128]{1,0:T(8,128)S(1)}, u32[]{:S(2)}, u32[]{:S(2)}) collective-permute-start(f32[128,128]{1,0:T(8,128)S(1)} %slice.3), channel_id=1, source_target_pairs={{0,1},{1,2},{2,3},{4,5},{5,6},{6,7},{8,9},{9,10},{10,11},{12,13},{... | collective-permute-start | bytes 196616 | tf_op jit(solution)/shard_map/ppermute | solution.py:487
  11.1 0.1 pad_add_fusion.place_ref
  11.1 3.8 %shard_map.73 = (bf16[128,1024]{1,0:T(8,128)(2,1)S(1)}, f32[128,1024]{1,0:T(8,128)S(1)}, f32[128,128]{1,0:T(8,128)S(1)}, bf16[256,256]{1,0:T(8,128)(2,1)S(1)}, b...) custom-call(s32[2]{0:T(128)S(1)} %pad_add_fusion.place_ref, ...), custom_call_target="tpu_custom_call" | custom-call | tf_op jit(solution)/shard_map/pallas_call | solution.py:425
  14.9 0.0 collective-permute-done.hist_ref
  15.0 1.2 %shard_map.74 = bf16[64,40,128]{2,1,0:T(8,128)(2,1)S(1)} custom-call(bf16[8,128]{1,0:T(8,128)(2,1)S(1)} %get-tuple-element.18.lists_ref, bf16[512,512]{1,0:T(8,128)(2,1)S(1)} %get-tuple-element.19.order_ref, f32[128,128]{1,0:T(8,128)S(1)} %collective-permute-done.hist_ref, f32[128,128]{1,0:T(8,128)S(1)} %get-tuple-element.20.head_ref, ...), custom_call_target="tpu_custom_call" | custom-call | tf_op jit(solution)/shard_map/pallas_call | solution.py:101
  16.2 29.8 %all_to_all.16.slab_ref = bf16[64,40,128]{2,1,0:T(8,128)(2,1)S(1)} all-to-all(bf16[64,40,128]{2,1,0:T(8,128)(2,1)S(1)} %shard_map.74), channel_id=1, replica_groups=mesh['row'=4,'plane'=16,'lag'=4] {'plane','lag'}, dimensions={0} | all-to-all | bytes 1310720 | tf_op jit(solution)/shard_map/all_to_all | solution.py:510
  46.0 1.9 %shard_map.76 = (bf16[16,128,128]{2,1,0:T(8,128)(2,1)S(1)}, bf16[16,128,128]{2,1,0:T(8,128)(2,1)S(1)}, bf16[4,128,128]{2,1,0:T(8,128)(2,1)S(1)}) custom-call(bf16[64,40,128]{2,1,0:T(8,128)(2,1)S(1)} %all_to_all.16.slab_ref), custom_call_target="tpu_custom_call" | custom-call | tf_op jit(solution)/shard_map/pallas_call | solution.py:101
  47.9 0.0 copy-start
  47.9 3.5 %collective-permute-start.1 = (bf16[4,128,128]{2,1,0:T(8,128)(2,1)S(1)}, bf16[4,128,128]{2,1,0:T(8,128)(2,1)S(1)}, u32[]{:S(2)}, u32[]{:S(2)}) collective-permute-start(bf16[4,128,128]{2,1,0:T(8,128)(2,1)S(1)} %get-tuple-element.29), channel_id=1, source_target_pairs={{0,64},{64,128},{128,192},{1,65},{65,129},{129,193},{2,66},{66,130... | collective-permute-start | bytes 393224 | tf_op jit(solution)/shard_map/ppermute | solution.py:453
  51.5 2.9 %shard_map.75 = (bf16[16,5,128,128]{3,2,1,0:T(8,128)(2,1)S(1)}, s32[16,128]{1,0:T(8,128)S(1)}) custom-call(bf16[64,40,128]{2,1,0:T(8,128)(2,1)S(1)} %all_to_all.16.slab_ref), custom_call_target="tpu_custom_call" | custom-call | tf_op jit(solution)/shard_map/pallas_call | solution.py:101
  54.4 0.0 collective-permute-done.1.below_ref
  54.4 4.8 %shard_map.77 = f32[256,128]{1,0:T(8,128)S(1)} custom-call(s32[16,128]{1,0:T(8,128)S(1)} %get-tuple-element.25.owner_ref, bf16[16,5,128,128]{3,2,1,0:T(8,128)(2,1)S(1)} %get-tuple-element.26.chosen_ref, bf16[16,128,128]{2,1,0:T(8,128)(2,1)S(1)} %get-tuple-element.27.group_ref, bf16[16,128,128]{2,1,0:T(8,128)(2,1)S(1)} %get-tuple-element.28.swapped_ref, ...), custom_call_target="tpu_custom_call" | custom-call | tf_op jit(solution)/shard_map/pallas_call | solution.py:101
  59.2 21.2 %all_to_all.17 = f32[256,1,128]{2,1,0:T(1,128)S(1)} all-to-all(f32[256,1,128]{2,1,0:T(1,128)S(1)} %bitcast.8), channel_id=1, replica_groups=mesh['row'=4,'plane'=16,'lag'=4] {'row','plane','lag'}, dimensions={0} | all-to-all | bytes 262144 | tf_op jit(solution)/shard_map/all_to_all | solution.py:512
  80.5 0.0 copy-done
  80.5 1.1 %shard_map.78 = f32[1,8,256]{2,1,0:T(8,128)} custom-call(s32[1]{0:T(128)} %bitcast.lag_ref, f32[256,128]{1,0:T(8,128)S(1)} %bitcast.9, bf16[1024,512]{1,0:T(8,128)(2,1)S(1)} %copy-done), custom_call_target="tpu_custom_call" | custom-call | tf_op jit(solution)/shard_map/pallas_call | solution.py:101
Async XLA Ops:
  0.8 14.1 %collective-permute-start = (f32[128,128]{1,0:T(8,128)S(1)}, f32[128,128]{1,0:T(8,128)S(1)}, u32[]{:S(2)}, u32[]{:S(2)}) collective-permute-start(f32[128,128]{1,0:T(8,128)S(1)} %slice.3), channel_id=1, source_target_pairs={{0,1},{1,2},{2,3},{4,5},{5,6},{6,7},{8,9},{9,10},{10,11},{12,13},{... | collective-permute-start | bytes 196616 | tf_op jit(solution)/shard_map/ppermute | solution.py:487
  47.9 32.5 %copy-start = (bf16[1024,512]{1,0:T(8,128)(2,1)S(1)}, bf16[1024,512]{1,0:T(8,128)(2,1)}, u32[]{:S(2)}) copy-start(bf16[1024,512]{1,0:T(8,128)(2,1)} %constant.23.clone.table_ref) | copy-start | bytes 3145732
  47.9 6.5 %collective-permute-start.1 = (bf16[4,128,128]{2,1,0:T(8,128)(2,1)S(1)}, bf16[4,128,128]{2,1,0:T(8,128)(2,1)S(1)}, u32[]{:S(2)}, u32[]{:S(2)}) collective-permute-start(bf16[4,128,128]{2,1,0:T(8,128)(2,1)S(1)} %get-tuple-element.29), channel_id=1, source_target_pairs={{0,64},{64,128},{128,192},{1,65},{65,129},{129,193},{2,66},{66,130... | collective-permute-start | bytes 393224 | tf_op jit(solution)/shard_map/ppermute | solution.py:453
